TPU v7x, 32 devices: a whole 2x2x4 slice. The times are simulated.
32 devices in a mesh: band: 16 (over z, y, x), head: 2 (over core).
Axes of the slice: x: 2, y: 2, z: 4, core: 2. Of those that a mesh axis runs over, the one named last changes fastest.
Arguments:
- tokens: bfloat16 [2, 4096, 1024], P(None, 'band'), may hold values from -6 to 6
- text_states: bfloat16 [2, 2048, 1024], P(None, 'band'), may hold values from -6 to 6
- cotangent: bfloat16 [2, 4096, 1024], P(None, 'band'), may hold values from -18 to 18
- earlier: int32 [2, 16], P(None, 'band'), may hold values from 0 to 3, as said below
- proj_master: float32 [6, 1024, 1024], P(None, 'band', 'head'), may hold values from -0.1875 to 0.1875
- out_master: float32 [2, 1024, 1024], P(None, 'band', 'head'), may hold values from -0.75 to 0.75
- mlp_master: float32 [2, 1024, 4096], P(None, 'band', 'head'), may hold values from -0.1875 to 0.1875
- gain_master: float32 [3, 1024], P(None, 'band'), may hold values from 0.4 to 2.4
- proj_first: float32 [6, 1024, 1024], P(None, 'band', 'head'), may hold values from -0.00015258789 to 0.00015258789
- proj_second: float32 [6, 1024, 1024], P(None, 'band', 'head'), may hold values from 2.9802323e-09 to 1.1920929e-08
- out_first: float32 [2, 1024, 1024], P(None, 'band', 'head'), may hold values from -0.00015258789 to 0.00015258789
- out_second: float32 [2, 1024, 1024], P(None, 'band', 'head'), may hold values from 2.9802323e-09 to 1.1920929e-08
- mlp_first: float32 [2, 1024, 4096], P(None, 'band', 'head'), may hold values from -0.00015258789 to 0.00015258789
- mlp_second: float32 [2, 1024, 4096], P(None, 'band', 'head'), may hold values from 2.9802323e-09 to 1.1920929e-08
- gain_first: float32 [3, 1024], P(None, 'band'), may hold values from -0.0004272461 to 0.0004272461
- gain_second: float32 [3, 1024], P(None, 'band'), may hold values from 2.3841858e-08 to 9.536743e-08
Outputs:
- block_out: bfloat16 [2, 4096, 1024], P(None, 'band')
- grad_tokens: float32 [2, 4096, 1024], P(None, 'band')
- grad_text: float32 [2, 2048, 1024], P(None, 'band')
- grad_norm: float32 [], replicated
- new_proj: float32 [6, 1024, 1024], P(None, 'band', 'head')
- new_proj_first: float32 [6, 1024, 1024], P(None, 'band', 'head')
- new_proj_second: float32 [6, 1024, 1024], P(None, 'band', 'head')
- new_out: float32 [2, 1024, 1024], P(None, 'band', 'head')
- new_out_first: float32 [2, 1024, 1024], P(None, 'band', 'head')
- new_out_second: float32 [2, 1024, 1024], P(None, 'band', 'head')
- new_mlp: float32 [2, 1024, 4096], P(None, 'band', 'head')
- new_mlp_first: float32 [2, 1024, 4096], P(None, 'band', 'head')
- new_mlp_second: float32 [2, 1024, 4096], P(None, 'band', 'head')
- new_gain: float32 [3, 1024], P(None, 'band')
- new_gain_first: float32 [3, 1024], P(None, 'band')
- new_gain_second: float32 [3, 1024], P(None, 'band')
Inputs may be any that keep to these rules, and one draw needn't show every extreme that they name: `earlier`: in each stream the 16 bands hold 3 grids of 4 consecutive bands and 4 grids of one band; a band's entry is its place inside its grid, so a grid of 4 bands carries 0 to 3 on consecutive bands and a grid of one band carries 0. Each stream begins with a grid of 4 bands; band 16 // 2 lies in a grid of 4 bands, at place 1 in even streams and at place 3 in odd ones; the other grids stand in an order drawn from the seed.
All inputs are finite; a program needn't handle non-finite values.
Results may differ from a plain program's by a relative error of at most 0.02.
The roundings to bfloat16 on the way count: a program that leaves them out, or rounds other values in their place, can miss the bound.
Values may be sent and summed in bfloat16 or wider, within the bound.
A program may use at most 192 MiB of HBM per device.

v0:
```python
from functools import partial

import jax
import jax.numpy as jnp
from jax import lax
from jax.sharding import PartitionSpec as P

D = 1024
HEAD_DIM = 64
SEQ_BANDS = 4
STEP = 10


EPS = 1e-05
NEG = -1e30
CLIP = 1.0
BETA_ONE = 0.9
BETA_TWO = 0.95
ADAM_EPS = 1e-08
DECAY = 0.1
GAIN_RATE = 0.5


def from_behind(x, axis, by):
    size = lax.axis_size(axis)
    pairs = [(i, i + by) for i in range(size) if 0 <= i + by < size]
    return lax.ppermute(x, axis, pairs)


def norm_rows(values, gain_row):
    centre = values - jnp.mean(values, axis=-1, keepdims=True)
    spread = jnp.mean(centre * centre, axis=-1, keepdims=True)
    return centre * lax.rsqrt(spread + EPS) * gain_row


def matmul(former, latter):
    return jnp.dot(former, latter, preferred_element_type=jnp.float32)


def matmul_t(former, latter):
    return lax.dot_general(
        former, latter, (((1,), (1,)), ((), ())), preferred_element_type=jnp.float32
    )


def inner_t(former, latter):
    return lax.dot_general(
        former, latter, (((0,), (0,)), ((), ())), preferred_element_type=jnp.float32
    )


def head_total(partials):
    return lax.psum(partials, "head")


def earlier_bands(key_pair):
    return [from_behind(key_pair, "band", behind) for behind in range(1, SEQ_BANDS)]


def caption_from_first(caption_pair):
    return [from_behind(caption_pair, "band", behind) for behind in range(1, SEQ_BANDS)]


def caption_back(masked_pair, behind):
    return from_behind(masked_pair.astype(jnp.bfloat16), "band", -behind).astype(masked_pair.dtype)


def log_sum(scores):
    row_max = jnp.max(scores, axis=-1, keepdims=True)
    return row_max + jnp.log(jnp.sum(jnp.exp(scores - row_max), axis=-1, keepdims=True))


def pair_scores(queries, key_block):
    return jnp.einsum("qhd,khd->hqk", queries, key_block, preferred_element_type=jnp.float32)


def pair_zero(queries, key_block):
    return jnp.zeros((queries.shape[1], queries.shape[0], key_block.shape[0]), jnp.float32)


def mix_values(weights, values):
    return jnp.einsum("hqk,khd->qhd", weights, values, preferred_element_type=jnp.float32)


def mix_nothing(weights, values):
    return jnp.zeros((weights.shape[1], values.shape[1], values.shape[2]), jnp.float32)


def spread_back(weights, rows_side):
    return jnp.einsum("hqk,qhd->khd", weights, rows_side, preferred_element_type=jnp.float32)


def spread_none(weights, rows_side):
    return jnp.zeros((weights.shape[2], rows_side.shape[1], rows_side.shape[2]), jnp.float32)


def masked_scores(queries, key_list, offset):
    score_scale = HEAD_DIM ** (-0.5)
    band_rows = queries.shape[0]
    row_ids = lax.broadcasted_iota(jnp.int32, (band_rows, band_rows), 0)
    col_ids = lax.broadcasted_iota(jnp.int32, (band_rows, band_rows), 1)
    own_scores = pair_scores(queries, key_list[0]) * score_scale
    blocks = [jnp.where((col_ids <= row_ids)[None], own_scores, NEG)]
    for behind in range(1, SEQ_BANDS):
        valid = behind <= offset
        far_block = lax.cond(valid, pair_scores, pair_zero, queries, key_list[behind]) * score_scale
        blocks.append(jnp.where(valid, far_block, NEG))
    return jnp.concatenate(blocks, axis=2)


def self_forward(queries, key_list, value_list, offset):
    band_rows = queries.shape[0]
    scores = masked_scores(queries, key_list, offset)
    log_total = log_sum(scores)
    weights = jnp.exp(scores - log_total).astype(jnp.bfloat16)
    result = mix_values(weights[:, :, :band_rows], value_list[0])
    for behind in range(1, SEQ_BANDS):
        weight_block = weights[:, :, behind * band_rows : (behind + 1) * band_rows]
        result = result + lax.cond(
            behind <= offset, mix_values, mix_nothing, weight_block, value_list[behind]
        )
    return (result.astype(jnp.bfloat16), log_total)


def self_backward(queries, key_list, value_list, offset, log_total, grad_out):
    score_scale = HEAD_DIM ** (-0.5)
    band_rows = queries.shape[0]
    probs_full = jnp.exp(masked_scores(queries, key_list, offset) - log_total)
    probs_low = probs_full.astype(jnp.bfloat16)
    grad_blocks = [pair_scores(grad_out, value_list[0])]
    for behind in range(1, SEQ_BANDS):
        grad_blocks.append(
            lax.cond(behind <= offset, pair_scores, pair_zero, grad_out, value_list[behind])
        )
    grad_probs = jnp.concatenate(grad_blocks, axis=2)
    centred = grad_probs - jnp.sum(grad_probs * probs_full, axis=-1, keepdims=True)
    grad_scores = (probs_full * centred).astype(jnp.bfloat16)
    grad_query = mix_values(grad_scores[:, :, :band_rows], key_list[0])
    key_grads = [spread_back(grad_scores[:, :, :band_rows], queries) * score_scale]
    value_grads = [spread_back(probs_low[:, :, :band_rows], grad_out)]
    for behind in range(1, SEQ_BANDS):
        valid = behind <= offset
        score_block = grad_scores[:, :, behind * band_rows : (behind + 1) * band_rows]
        prob_block = probs_low[:, :, behind * band_rows : (behind + 1) * band_rows]
        grad_query = grad_query + lax.cond(
            valid, mix_values, mix_nothing, score_block, key_list[behind]
        )
        key_grads.append(
            lax.cond(valid, spread_back, spread_none, score_block, queries) * score_scale
        )
        value_grads.append(lax.cond(valid, spread_back, spread_none, prob_block, grad_out))
    return (grad_query * score_scale, key_grads, value_grads)


def adamw_update(weight, moment_one, moment_two, gradient, step_rate, decay_rate):
    moment_one_new = BETA_ONE * moment_one + (1.0 - BETA_ONE) * gradient
    moment_two_new = BETA_TWO * moment_two + (1.0 - BETA_TWO) * gradient * gradient
    unbiased_one = moment_one_new / (1.0 - BETA_ONE**STEP)
    unbiased_two = moment_two_new / (1.0 - BETA_TWO**STEP)
    weight_new = weight - step_rate * (
        unbiased_one / (jnp.sqrt(unbiased_two) + ADAM_EPS) + decay_rate * weight
    )
    return (weight_new, moment_one_new, moment_two_new)


def local(
    tokens,
    text_states,
    cotangent,
    earlier,
    proj_master,
    out_master,
    mlp_master,
    gain_master,
    proj_first,
    proj_second,
    out_first,
    out_second,
    mlp_first,
    mlp_second,
    gain_first,
    gain_second,
):
    streams, band_rows, model_width = tokens.shape
    row_count = streams * band_rows
    text_rows = text_states.shape[1]
    proj_low = proj_master.astype(jnp.bfloat16)
    out_low = out_master.astype(jnp.bfloat16)
    mlp_low = mlp_master.astype(jnp.bfloat16)
    gain_low = gain_master.astype(jnp.bfloat16)
    proj_w, out_w, mlp_w, gain_w = (
        lax.all_gather(proj_low, "band", axis=1, tiled=True),
        lax.all_gather(out_low, "band", axis=1, tiled=True),
        lax.all_gather(mlp_low, "band", axis=1, tiled=True),
        lax.all_gather(gain_low, "band", axis=1, tiled=True),
    )
    gains = gain_w.astype(jnp.float32)
    local_width = proj_w.shape[2]
    local_heads = local_width // HEAD_DIM
    score_scale = HEAD_DIM ** (-0.5)
    head_shape = (streams, band_rows, local_heads, HEAD_DIM)
    text_shape = (streams, text_rows, local_heads, HEAD_DIM)
    offsets = earlier[:, 0]
    inputs = tokens.astype(jnp.float32).reshape(row_count, model_width)
    normed_one = norm_rows(inputs, gains[0]).astype(jnp.bfloat16)
    queries = matmul(normed_one, proj_w[0]).astype(jnp.bfloat16).reshape(head_shape)
    key_rows = matmul(normed_one, proj_w[1]).astype(jnp.bfloat16)
    value_rows = matmul(normed_one, proj_w[2]).astype(jnp.bfloat16)
    own_pair = jnp.stack([key_rows.reshape(head_shape), value_rows.reshape(head_shape)])
    pair_list = [own_pair] + earlier_bands(own_pair)
    attended_list = []
    total_list = []
    for stream in range(streams):
        offset = earlier[stream, 0]
        result, log_total = self_forward(
            queries[stream],
            [neighbour[0, stream] for neighbour in pair_list],
            [neighbour[1, stream] for neighbour in pair_list],
            offset,
        )
        attended_list.append(result)
        total_list.append(log_total)
    attended = jnp.stack(attended_list).reshape(row_count, local_width)
    hidden_one = inputs + head_total(matmul_t(attended, out_w[0]))
    normed_two = norm_rows(hidden_one, gains[1]).astype(jnp.bfloat16)
    cross_queries = matmul(normed_two, proj_w[3]).astype(jnp.bfloat16).reshape(head_shape)
    text_flat = text_states.reshape(streams * text_rows, model_width)
    slot_keys = matmul(text_flat, proj_w[4]).astype(jnp.bfloat16).reshape(text_shape)
    slot_values = matmul(text_flat, proj_w[5]).astype(jnp.bfloat16).reshape(text_shape)
    caption_pair = jnp.stack([slot_keys, slot_values])
    moved_list = caption_from_first(caption_pair)
    chosen = caption_pair
    for behind in range(1, SEQ_BANDS):
        chosen = jnp.where(
            (offsets == behind)[None, :, None, None, None], moved_list[behind - 1], chosen
        )
    cross_keys = chosen[0]
    cross_values = chosen[1]
    cross_scores = (
        jnp.einsum("sqhd,skhd->shqk", cross_queries, cross_keys, preferred_element_type=jnp.float32)
        * score_scale
    )
    cross_probs = jnp.exp(cross_scores - log_sum(cross_scores))
    cross_low = cross_probs.astype(jnp.bfloat16)
    crossed = (
        jnp.einsum("shqk,skhd->sqhd", cross_low, cross_values, preferred_element_type=jnp.float32)
        .astype(jnp.bfloat16)
        .reshape(row_count, local_width)
    )
    hidden_two = hidden_one + head_total(matmul_t(crossed, out_w[1]))
    normed_three = norm_rows(hidden_two, gains[2]).astype(jnp.bfloat16)
    before = matmul(normed_three, mlp_w[0])
    activated = jax.nn.gelu(before, approximate=False).astype(jnp.bfloat16)
    block_out = (
        (hidden_two + head_total(matmul_t(activated, mlp_w[1])))
        .astype(jnp.bfloat16)
        .reshape(streams, band_rows, model_width)
    )
    incoming = cotangent.astype(jnp.float32).reshape(row_count, model_width)
    incoming_low = cotangent.reshape(row_count, model_width)
    grad_down = inner_t(incoming_low, activated)
    grad_act = matmul(incoming_low, mlp_w[1])
    _, gelu_pull = jax.vjp(partial(jax.nn.gelu, approximate=False), before)
    grad_before = gelu_pull(grad_act)[0].astype(jnp.bfloat16)
    grad_up = inner_t(normed_three, grad_before)
    mlp_grad_local = jnp.stack([grad_up, grad_down])
    grad_normed_three = head_total(matmul_t(grad_before, mlp_w[0]))
    _, pull_three = jax.vjp(norm_rows, hidden_two, gains[2])
    back_two, gain_grad_three = pull_three(grad_normed_three)
    grad_two = incoming + back_two
    grad_two_low = grad_two.astype(jnp.bfloat16)
    grad_cross_out = inner_t(grad_two_low, crossed)
    grad_crossed = matmul(grad_two_low, out_w[1]).astype(jnp.bfloat16).reshape(head_shape)
    cross_dp = jnp.einsum(
        "sqhd,skhd->shqk", grad_crossed, cross_values, preferred_element_type=jnp.float32
    )
    cross_ds = (
        cross_probs * (cross_dp - jnp.sum(cross_dp * cross_probs, axis=-1, keepdims=True))
    ).astype(jnp.bfloat16)
    grad_cq = (
        (
            jnp.einsum("shqk,skhd->sqhd", cross_ds, cross_keys, preferred_element_type=jnp.float32)
            * score_scale
        )
        .astype(jnp.bfloat16)
        .reshape(row_count, local_width)
    )
    key_part = (
        jnp.einsum("shqk,sqhd->skhd", cross_ds, cross_queries, preferred_element_type=jnp.float32)
        * score_scale
    )
    value_part = jnp.einsum(
        "shqk,sqhd->skhd", cross_low, grad_crossed, preferred_element_type=jnp.float32
    )
    grad_caption = jnp.stack([key_part, value_part])
    caption_total = jnp.where((offsets == 0)[None, :, None, None, None], grad_caption, 0.0)
    for behind in range(1, SEQ_BANDS):
        masked_pair = jnp.where((offsets == behind)[None, :, None, None, None], grad_caption, 0.0)
        caption_total = caption_total + caption_back(masked_pair, behind)
    grad_ck = caption_total[0].astype(jnp.bfloat16).reshape(streams * text_rows, local_width)
    grad_cv = caption_total[1].astype(jnp.bfloat16).reshape(streams * text_rows, local_width)
    text_partial = matmul_t(grad_ck, proj_w[4]) + matmul_t(grad_cv, proj_w[5])
    grad_normed_two, grad_text = head_total((matmul_t(grad_cq, proj_w[3]), text_partial))
    _, pull_two = jax.vjp(norm_rows, hidden_one, gains[1])
    back_one, gain_grad_two = pull_two(grad_normed_two)
    grad_one = grad_two + back_one
    grad_one_low = grad_one.astype(jnp.bfloat16)
    grad_self_out = inner_t(grad_one_low, attended)
    grad_attended = matmul(grad_one_low, out_w[0]).astype(jnp.bfloat16).reshape(head_shape)
    query_grads = []
    key_grads = []
    value_grads = []
    for stream in range(streams):
        offset = earlier[stream, 0]
        grad_query, key_blocks, value_blocks = self_backward(
            queries[stream],
            [neighbour[0, stream] for neighbour in pair_list],
            [neighbour[1, stream] for neighbour in pair_list],
            offset,
            total_list[stream],
            grad_attended[stream],
        )
        query_grads.append(grad_query)
        key_grads.append(key_blocks)
        value_grads.append(value_blocks)
    grad_pairs = [
        jnp.stack(
            [
                jnp.stack([key_grads[stream][behind] for stream in range(streams)]),
                jnp.stack([value_grads[stream][behind] for stream in range(streams)]),
            ]
        )
        for behind in range(SEQ_BANDS)
    ]
    pair_total = grad_pairs[0]
    for behind in range(1, SEQ_BANDS):
        pair_total = pair_total + from_behind(
            grad_pairs[behind].astype(jnp.bfloat16), "band", -behind
        ).astype(jnp.float32)
    grad_queries = jnp.stack(query_grads).astype(jnp.bfloat16).reshape(row_count, local_width)
    grad_keys = pair_total[0].astype(jnp.bfloat16).reshape(row_count, local_width)
    grad_values = pair_total[1].astype(jnp.bfloat16).reshape(row_count, local_width)
    proj_grad_local = jnp.stack(
        [
            inner_t(normed_one, grad_queries),
            inner_t(normed_one, grad_keys),
            inner_t(normed_one, grad_values),
            inner_t(normed_two, grad_cq),
            inner_t(text_flat, grad_ck),
            inner_t(text_flat, grad_cv),
        ]
    )
    norm_partial = (
        matmul_t(grad_queries, proj_w[0])
        + matmul_t(grad_keys, proj_w[1])
        + matmul_t(grad_values, proj_w[2])
    )
    grad_normed_one = head_total(norm_partial)
    _, pull_one = jax.vjp(norm_rows, inputs, gains[0])
    back_zero, gain_grad_one = pull_one(grad_normed_one)
    grad_tokens = (grad_one + back_zero).reshape(streams, band_rows, model_width)
    out_grad_local = jnp.stack([grad_self_out, grad_cross_out])
    gain_grad_local = jnp.stack([gain_grad_one, gain_grad_two, gain_grad_three])
    proj_grad, out_grad, mlp_grad, gain_grad = (
        lax.psum_scatter(proj_grad_local, "band", scatter_dimension=1, tiled=True),
        lax.psum_scatter(out_grad_local, "band", scatter_dimension=1, tiled=True),
        lax.psum_scatter(mlp_grad_local, "band", scatter_dimension=1, tiled=True),
        lax.psum_scatter(gain_grad_local, "band", scatter_dimension=1, tiled=True),
    )
    local_squares = (
        jnp.sum(proj_grad * proj_grad)
        + jnp.sum(out_grad * out_grad)
        + jnp.sum(mlp_grad * mlp_grad)
        + 0.5 * jnp.sum(gain_grad * gain_grad)
    )
    grad_norm = jnp.sqrt(lax.psum(local_squares, ("band", "head")))
    factor = jnp.minimum(1.0, CLIP / grad_norm)
    matrix_rate = 2.0 * D ** (-0.5)
    new_proj = adamw_update(
        proj_master, proj_first, proj_second, proj_grad * factor, matrix_rate, DECAY
    )
    new_out = adamw_update(out_master, out_first, out_second, out_grad * factor, matrix_rate, DECAY)
    new_mlp = adamw_update(mlp_master, mlp_first, mlp_second, mlp_grad * factor, matrix_rate, DECAY)
    new_gain = adamw_update(
        gain_master, gain_first, gain_second, gain_grad * factor, GAIN_RATE, 0.0
    )
    grad_text_out = grad_text.reshape(streams, text_rows, model_width)
    return (
        block_out,
        grad_tokens,
        grad_text_out,
        grad_norm,
        new_proj[0],
        new_proj[1],
        new_proj[2],
        new_out[0],
        new_out[1],
        new_out[2],
        new_mlp[0],
        new_mlp[1],
        new_mlp[2],
        new_gain[0],
        new_gain[1],
        new_gain[2],
    )


def solution(mesh):
    return jax.shard_map(
        local,
        mesh=mesh,
        in_specs=(
            P(None, "band", None),
            P(None, "band", None),
            P(None, "band", None),
            P(None, "band"),
            P(None, "band", "head"),
            P(None, "band", "head"),
            P(None, "band", "head"),
            P(None, "band"),
            P(None, "band", "head"),
            P(None, "band", "head"),
            P(None, "band", "head"),
            P(None, "band", "head"),
            P(None, "band", "head"),
            P(None, "band", "head"),
            P(None, "band"),
            P(None, "band"),
        ),
        out_specs=(
            P(None, "band", None),
            P(None, "band", None),
            P(None, "band", None),
            P(),
            P(None, "band", "head"),
            P(None, "band", "head"),
            P(None, "band", "head"),
            P(None, "band", "head"),
            P(None, "band", "head"),
            P(None, "band", "head"),
            P(None, "band", "head"),
            P(None, "band", "head"),
            P(None, "band", "head"),
            P(None, "band"),
            P(None, "band"),
            P(None, "band"),
        ),
        check_vma=False,
    )
```

profile of v0, /device:TPU:0, one launch (start us, length us, event | category | flops | bytes accessed | tf_op | source)
XLA Modules:
  0.0 1690.6 jit_solution(16297848461887249185)
XLA Ops:
  17.5 43.1 %all-gather = bf16[16,64,3]{1,2,0:T(4,128)(2,1)S(1)} all-gather(bf16[1,64,3]{1,2,0:T(4,128)(2,1)S(1)} %convert_bitcast_fusion), channel_id=1, replica_groups=mesh['band'=16,'head'=2] {'band'}, dimensions={0}, use_global_device_ids=true | all-gather | bytes 6528 | tf_op jit(solution)/shard_map/all_gather | solution.py:195
  61.1 46.3 %all-gather.5.cloned.1.call-done = bf16[6,1024,512]{2,1,0:T(8,128)(2,1)} async-done(((bf16[6,64,512]{2,1,0:T(8,128)(2,1)}), bf16[6,1024,512]{2,1,0:T(8,128)(2,1)}) %all-gather.5.cloned.1.call-update) | async-done | bytes 6291472 | tf_op jit(solution)/shard_map/all_gather | solution.py:192
  116.4 3.6 collective-permute-start.2
  119.9 4.2 collective-permute-start.1
  124.1 2.5 collective-permute-start
  134.3 9.4 collective-permute-done.2
  143.7 2.6 fusion.142
  147.1 22.1 %collective-permute-done.1 = bf16[2,2,256,8,64]{2,1,4,3,0:T(2,128)(2,1)S(1)} collective-permute-done((bf16[2,2,256,8,64]{2,1,4,3,0:T(2,128)(2,1)}, bf16[2,2,256,8,64]{2,1,4,3,0:T(2,128)(2,1)S(1)}, u32[]{:S(2)}, u32[]{:S(2)}) %collective-permute-start.1) | collective-permute-done | bytes 1048608 | tf_op jit(solution)/shard_map/ppermute | solution.py:27
  169.2 2.7 fusion.141
  172.6 2.7 fusion.140
  184.3 4.2 fusion.135
  190.0 2.9 fusion.133
  192.9 4.2 fusion.136
  200.9 9.0 fusion.119
  209.9 2.2 copy_bitcast_fusion.6
  221.0 3.0 fusion.131
  230.1 2.6 multiply_select_fusion.3
  232.7 8.0 fusion.117
  251.4 3.5 fusion.71
  259.6 18.2 %collective-permute-start.5 = (bf16[2,2,128,8,64]{2,4,3,1,0:T(8,128)(2,1)S(1)}, bf16[2,2,128,8,64]{2,4,3,1,0:T(8,128)(2,1)S(1)}, u32[]{:S(2)}, u32[]{:S(2)}) collective-permute-start(bf16[2,2,128,8,64]{2,4,3,1,0:T(8,128)(2,1)S(1)} %pad_maximum_fusion.15), channel_id=1, source_target_pairs={{0,2},{2,4},{4,6},{6,8},{8,10},{10,12},{12,14},{14,16},{16,18},{18... | collective-permute-start | bytes 1572872 | tf_op jit(solution)/shard_map/ppermute | solution.py:27
  277.8 75.3 %collective-permute-start.4 = (bf16[2,2,128,8,64]{2,4,3,1,0:T(8,128)(2,1)S(1)}, bf16[2,2,128,8,64]{2,4,3,1,0:T(8,128)(2,1)S(1)}, u32[]{:S(2)}, u32[]{:S(2)}) collective-permute-start(bf16[2,2,128,8,64]{2,4,3,1,0:T(8,128)(2,1)S(1)} %pad_maximum_fusion.15), channel_id=1, source_target_pairs={{0,4},{2,6},{4,8},{6,10},{8,12},{10,14},{12,16},{14,18},{16,20},{1... | collective-permute-start | bytes 1572872 | tf_op jit(solution)/shard_map/ppermute | solution.py:27
  354.5 7.8 collective-permute-done.4
  377.1 2.2 fusion.74
  382.0 40.1 %all-reduce.9.cloned.1.call-done = f32[512,1024]{1,0:T(8,128)} async-done(((f32[512,1024]{1,0:T(8,128)}), f32[512,1024]{1,0:T(8,128)}) %all-reduce.9.cloned.1.call-update) | async-done | bytes 2097168 | tf_op jit(solution)/shard_map/psum | solution.py:53
  425.6 113.0 %all-gather.9.cloned.1.call-done = bf16[2,1024,2048]{2,1,0:T(8,128)(2,1)} async-done(((bf16[2,64,2048]{2,1,0:T(8,128)(2,1)}), bf16[2,1024,2048]{2,1,0:T(8,128)(2,1)}) %all-gather.9.cloned.1.call-update) | async-done | bytes 8388624 | tf_op jit(solution)/shard_map/all_gather | solution.py:194
  538.6 14.5 multiply_convert_fusion.2
  553.1 3.7 add_convert_fusion
  558.1 3.8 fusion.38
  562.1 19.4 %all-reduce.11.cloned.1.call-done = f32[512,1024]{1,0:T(8,128)} async-done(((f32[512,1024]{1,0:T(8,128)}), f32[512,1024]{1,0:T(8,128)}) %all-reduce.11.cloned.1.call-update) | async-done | bytes 2097168 | tf_op jit(solution)/shard_map/psum | solution.py:53
  581.5 3.1 multiply_reduce_fusion.2
  592.1 3.1 convolution_bitcast_fusion.28
  599.1 3.4 fusion.73
  609.1 6.4 fusion.41
  615.4 5.5 collective-permute-done.9
  621.0 14.3 collective-permute-done.10
  638.1 2.8 convolution_add_fusion
  640.9 2.4 multiply_reduce_fusion.3
  648.1 2.5 convolution_bitcast_fusion.29
  650.6 2.5 convolution_bitcast_fusion.30
  661.4 12.2 multiply_convert_fusion.1
  681.8 12.2 multiply_convert_fusion
  739.1 68.3 %collective-permute-done.6 = bf16[2,2,256,8,64]{2,4,3,1,0:T(8,128)(2,1)} collective-permute-done((bf16[2,2,256,8,64]{2,4,3,1,0:T(8,128)(2,1)}, bf16[2,2,256,8,64]{2,4,3,1,0:T(8,128)(2,1)}, u32[]{:S(2)}, u32[]{:S(2)}) %collective-permute-start.6) | collective-permute-done | bytes 1048608 | tf_op jit(solution)/shard_map/ppermute | solution.py:27
  807.4 22.6 %collective-permute-done.8 = bf16[2,2,256,8,64]{2,4,3,1,0:T(8,128)(2,1)} collective-permute-done((bf16[2,2,256,8,64]{2,4,3,1,0:T(8,128)(2,1)}, bf16[2,2,256,8,64]{2,4,3,1,0:T(8,128)(2,1)}, u32[]{:S(2)}, u32[]{:S(2)}) %collective-permute-start.8) | collective-permute-done | bytes 1048608 | tf_op jit(solution)/shard_map/ppermute | solution.py:27
  831.1 2.6 fusion.44
  835.8 2.2 add_add_fusion.4
  838.7 3.6 convolution_bitcast_fusion.26
  844.5 43.4 %all-reduce.15.cloned.1.call-done = (f32[512,1024]{1,0:T(8,128)}, f32[512,1024]{1,0:T(8,128)}, f32[2,128,1024]{2,1,0:T(8,128)}) async-done(((f32[512,1024]{1,0:T(8,128)}, f32[512,1024]{1,0:T(8,128)}, f32[2,128,1024]{2,1,0:T(8,128)}), (f32[512,1024]{1,0:T(8,128)}, f32[512,1024]{1,0:T(8,128)}, f32[2,128,1024]{2,1,0:T(8,128)})) %all-reduce.15.cloned.1.call-update) | async-done | bytes 5242896 | tf_op jit(solution)/shard_map/psum | solution.py:53
  887.8 2.5 fusion.53
  892.8 4.6 pad_maximum_fusion.9
  898.5 3.5 bitcast_dynamic-update-slice_fusion.5
  904.1 2.2 bitcast_dynamic-update-slice_fusion.3
  906.3 2.3 bitcast_dynamic-update-slice_fusion.2
  912.4 4.4 convolution_bitcast_fusion.24
  916.9 2.5 convolution_bitcast_fusion.25
  919.4 6.0 pad_maximum_fusion
  925.5 4.6 add_add_fusion.3
  930.1 41.6 %reduce-scatter.13.cloned.1.call-done = f32[64,3]{1,0:T(8,128)} async-done(((f32[1024,3]{1,0:T(8,128)}), f32[64,3]{1,0:T(8,128)}) %reduce-scatter.13.cloned.1.call-update) | async-done | bytes 784
  973.7 91.6 %reduce-scatter.9.cloned.1.call-done = f32[2,64,512]{2,1,0:T(8,128)} async-done(((f32[2,1024,512]{2,1,0:T(8,128)}), f32[2,64,512]{2,1,0:T(8,128)}) %reduce-scatter.9.cloned.1.call-update) | async-done | bytes 262160 | tf_op jit(solution)/shard_map/reduce_scatter | solution.py:366
  1067.0 207.0 %reduce-scatter.7.cloned.1.call-done = f32[6,64,512]{2,1,0:T(8,128)} async-done(((f32[6,1024,512]{2,1,0:T(8,128)}), f32[6,64,512]{2,1,0:T(8,128)}) %reduce-scatter.7.cloned.1.call-update) | async-done | bytes 786448 | tf_op jit(solution)/shard_map/reduce_scatter | solution.py:365
  1277.2 344.8 %reduce-scatter.11.cloned.1.call-done = f32[2,64,2048]{2,1,0:T(8,128)} async-done(((f32[2,1024,2048]{2,1,0:T(8,128)}), f32[2,64,2048]{2,1,0:T(8,128)}) %reduce-scatter.11.cloned.1.call-update) | async-done | bytes 1048592 | tf_op jit(solution)/shard_map/reduce_scatter | solution.py:367
  1624.9 2.9 add_convert_fusion.1
  1627.8 44.6 %psum.63 = f32[]{:T(128)} all-reduce(f32[]{:T(128)S(6)} %add.271), channel_id=1, replica_groups=mesh['band'=16,'head'=2] {'band','head'}, use_global_device_ids=true, to_apply=%region_129.130 | all-reduce | flops 1 | bytes 8 | tf_op jit(solution)/shard_map/psum | solution.py:376
  1675.8 3.3 multiply_subtract_fusion.1
  1679.2 2.2 multiply_subtract_fusion
  (594 shorter events, 223.2 us)
Async XLA Ops:
  7.2 247.7 %copy-start = (bf16[2,128,1024]{2,1,0:T(8,128)(2,1)S(1)}, bf16[2,128,1024]{2,1,0:T(8,128)(2,1)}, u32[]{:S(2)}) copy-start(bf16[2,128,1024]{2,1,0:T(8,128)(2,1)} %param.101) | copy-start | bytes 1572868
  7.2 8.4 copy-start.146
  7.2 8.4 copy-start.6
  7.2 100.2 %all-gather.5.cloned.1.call-start = ((), (), s32[]{:S(2)}) async-start(), calls=%async_computation.4 | async-start | bytes 6684672 | tf_op jit(solution)/shard_map/all_gather | solution.py:192
  9.3 242.0 %all-gather.7.cloned.1.call-start = ((), (), s32[]{:S(2)}) async-start(), calls=%async_computation.5 | async-start | bytes 2228224 | tf_op jit(solution)/shard_map/all_gather | solution.py:193
  11.0 353.9 %all-reduce.7.cloned.1.call-start = ((), (), s32[]{:S(2)}) async-start(), calls=%async_computation.6 | async-start | bytes 4194304 | tf_op jit(solution)/shard_map/psum | solution.py:53
  60.7 48.7 %copy-start.134 = (f32[1,1024]{1,0:T(1,128)}, f32[1,1024]{1,0:T(1,128)S(1)}, u32[]{:S(2)}) copy-start(f32[1,1024]{1,0:T(1,128)S(1)} %get-tuple-element.752) | copy-start | bytes 12292
  60.7 523.9 %copy-start.136 = (f32[1,1024]{1,0:T(1,128)}, f32[1,1024]{1,0:T(1,128)S(1)}, u32[]{:S(2)}) copy-start(f32[1,1024]{1,0:T(1,128)S(1)} %get-tuple-element.750) | copy-start | bytes 12292
  61.1 65.5 %copy-start.24 = (bf16[2,256,1024]{2,1,0:T(8,128)(2,1)}, bf16[2,256,1024]{2,1,0:T(8,128)(2,1)S(1)}, u32[]{:S(2)}) copy-start(bf16[2,256,1024]{2,1,0:T(8,128)(2,1)S(1)} %fusion.52) | copy-start | bytes 3145732
  112.7 19.8 %copy-start.108 = (bf16[1,1,256,8,64]{2,1,4,3,0:T(2,128)(2,1)}, bf16[1,1,256,8,64]{2,1,4,3,0:T(2,128)(2,1)S(1)}, u32[]{:S(2)}) copy-start(bf16[1,1,256,8,64]{2,1,4,3,0:T(2,128)(2,1)S(1)} %get-tuple-element.747) | copy-start | bytes 786436
  116.4 12.3 copy-start.110
  116.4 27.3 %collective-permute-start.2 = (bf16[2,2,256,8,64]{2,1,4,3,0:T(2,128)(2,1)}, bf16[2,2,256,8,64]{2,1,4,3,0:T(2,128)(2,1)S(1)}, u32[]{:S(2)}, u32[]{:S(2)}) collective-permute-start(bf16[2,2,256,8,64]{2,1,4,3,0:T(2,128)(2,1)} %constant_dynamic-update-slice_fusion), channel_id=1, source_target_pairs={{0,6},{2,8},{4,10},{6,12},{8,14},{10,16},{12,18},{14,20},{16,22},{... | collective-permute-start | bytes 3145736 | tf_op jit(solution)/shard_map/ppermute | solution.py:27
  119.9 49.3 %collective-permute-start.1 = (bf16[2,2,256,8,64]{2,1,4,3,0:T(2,128)(2,1)}, bf16[2,2,256,8,64]{2,1,4,3,0:T(2,128)(2,1)S(1)}, u32[]{:S(2)}, u32[]{:S(2)}) collective-permute-start(bf16[2,2,256,8,64]{2,1,4,3,0:T(2,128)(2,1)} %constant_dynamic-update-slice_fusion), channel_id=1, source_target_pairs={{0,4},{2,6},{4,8},{6,10},{8,12},{10,14},{12,16},{14,18},{16,20},{1... | collective-permute-start | bytes 3145736 | tf_op jit(solution)/shard_map/ppermute | solution.py:27
  124.1 48.5 %collective-permute-start = (bf16[2,2,256,8,64]{2,1,4,3,0:T(2,128)(2,1)}, bf16[2,2,256,8,64]{2,1,4,3,0:T(2,128)(2,1)S(1)}, u32[]{:S(2)}, u32[]{:S(2)}) collective-permute-start(bf16[2,2,256,8,64]{2,1,4,3,0:T(2,128)(2,1)} %constant_dynamic-update-slice_fusion), channel_id=1, source_target_pairs={{0,2},{2,4},{4,6},{6,8},{8,10},{10,12},{12,14},{14,16},{16,18},{18... | collective-permute-start | bytes 3145736 | tf_op jit(solution)/shard_map/ppermute | solution.py:27
  128.6 52.8 %copy-start.8 = (bf16[256,512]{0,1:T(8,128)(2,1)}, bf16[256,512]{0,1:T(8,128)(2,1)S(1)}, u32[]{:S(2)}) copy-start(bf16[256,512]{0,1:T(8,128)(2,1)S(1)} %get-tuple-element.749) | copy-start | bytes 786436
  128.7 89.4 %copy-start.10 = (bf16[256,512]{0,1:T(8,128)(2,1)}, bf16[256,512]{0,1:T(8,128)(2,1)S(1)}, u32[]{:S(2)}) copy-start(bf16[256,512]{0,1:T(8,128)(2,1)S(1)} %get-tuple-element.748) | copy-start | bytes 786436
  146.3 35.1 %copy-start.63 = (bf16[1,1,256,8,64]{2,4,1,3,0:T(8,128)(2,1)}, bf16[1,1,256,8,64]{2,4,1,3,0:T(8,128)(2,1)S(1)}, u32[]{:S(2)}) copy-start(bf16[1,1,256,8,64]{2,4,1,3,0:T(8,128)(2,1)S(1)} %copy.577) | copy-start | bytes 786436
  198.4 11.5 copy-start.138
  232.6 8.0 copy-start.79
  254.9 167.2 %all-reduce.9.cloned.1.call-start = ((), (), s32[]{:S(2)}) async-start(), calls=%async_computation.7 | async-start | bytes 4194304 | tf_op jit(solution)/shard_map/psum | solution.py:53
  259.6 94.9 %collective-permute-start.5 = (bf16[2,2,128,8,64]{2,4,3,1,0:T(8,128)(2,1)S(1)}, bf16[2,2,128,8,64]{2,4,3,1,0:T(8,128)(2,1)S(1)}, u32[]{:S(2)}, u32[]{:S(2)}) collective-permute-start(bf16[2,2,128,8,64]{2,4,3,1,0:T(8,128)(2,1)S(1)} %pad_maximum_fusion.15), channel_id=1, source_target_pairs={{0,2},{2,4},{4,6},{6,8},{8,10},{10,12},{12,14},{14,16},{16,18},{18... | collective-permute-start | bytes 1572872 | tf_op jit(solution)/shard_map/ppermute | solution.py:27
  277.8 84.5 %collective-permute-start.4 = (bf16[2,2,128,8,64]{2,4,3,1,0:T(8,128)(2,1)S(1)}, bf16[2,2,128,8,64]{2,4,3,1,0:T(8,128)(2,1)S(1)}, u32[]{:S(2)}, u32[]{:S(2)}) collective-permute-start(bf16[2,2,128,8,64]{2,4,3,1,0:T(8,128)(2,1)S(1)} %pad_maximum_fusion.15), channel_id=1, source_target_pairs={{0,4},{2,6},{4,8},{6,10},{8,12},{10,14},{12,16},{14,18},{16,20},{1... | collective-permute-start | bytes 1572872 | tf_op jit(solution)/shard_map/ppermute | solution.py:27
  353.1 10.9 collective-permute-start.3
  379.3 159.3 %all-gather.9.cloned.1.call-start = ((), (), s32[]{:S(2)}) async-start(), calls=%async_computation.8 | async-start | bytes 8912896 | tf_op jit(solution)/shard_map/all_gather | solution.py:194
  381.5 200.0 %all-reduce.11.cloned.1.call-start = ((), (), s32[]{:S(2)}) async-start(), calls=%async_computation.9 | async-start | bytes 4194304 | tf_op jit(solution)/shard_map/psum | solution.py:53
  423.9 160.7 %copy-start.140 = (f32[512]{0:T(512)}, f32[512]{0:T(512)S(1)}, u32[]{:S(2)}) copy-start(f32[512]{0:T(512)S(1)} %broadcast_multiply_fusion) | copy-start | bytes 6148
  425.6 159.0 %copy-start.142 = (f32[512]{0:T(512)}, f32[512]{0:T(512)S(1)}, u32[]{:S(2)}) copy-start(f32[512]{0:T(512)S(1)} %fusion.109) | copy-start | bytes 6148
  538.6 14.5 copy-start.69
  538.6 14.5 copy-start.151
  561.9 79.0 %all-reduce.13.cloned.1.call-start = ((), (), s32[]{:S(2)}) async-start(), calls=%async_computation.10 | async-start | bytes 4194304 | tf_op jit(solution)/shard_map/psum | solution.py:53
  602.5 285.3 %all-reduce.15.cloned.1.call-start = ((), (), s32[]{:S(2)}) async-start(), calls=%async_computation.15 | async-start | bytes 10485760 | tf_op jit(solution)/shard_map/psum | solution.py:53
  602.6 6.5 copy-start.154
  605.0 16.0 collective-permute-start.9
  606.3 29.1 %collective-permute-start.10 = (bf16[2,2,128,8,64]{2,4,3,1,0:T(8,128)(2,1)S(1)}, bf16[2,2,128,8,64]{2,4,3,1,0:T(8,128)(2,1)S(1)}, u32[]{:S(2)}, u32[]{:S(2)}) collective-permute-start(bf16[2,2,128,8,64]{2,4,3,1,0:T(8,128)(2,1)S(1)} %get-tuple-element.724), channel_id=1, source_target_pairs={{4,0},{6,2},{8,4},{10,6},{12,8},{14,10},{16,12},{18,14},{20,16},{2... | collective-permute-start | bytes 1572872 | tf_op jit(solution)/shard_map/ppermute | solution.py:27
  607.6 27.8 %collective-permute-start.11 = (bf16[2,2,128,8,64]{2,4,3,1,0:T(8,128)(2,1)S(1)}, bf16[2,2,128,8,64]{2,4,3,1,0:T(8,128)(2,1)S(1)}, u32[]{:S(2)}, u32[]{:S(2)}) collective-permute-start(bf16[2,2,128,8,64]{2,4,3,1,0:T(8,128)(2,1)S(1)} %get-tuple-element.725), channel_id=1, source_target_pairs={{6,0},{8,2},{10,4},{12,6},{14,8},{16,10},{18,12},{20,14},{22,16},{... | collective-permute-start | bytes 1572872 | tf_op jit(solution)/shard_map/ppermute | solution.py:27
  636.0 4.9 copy-start.87
  636.3 4.6 copy-start.85
  648.1 5.0 copy-start.98
  661.4 12.2 copy-start.111
  681.8 12.2 copy-start.109
  715.9 4.7 copy-start.124
  715.9 4.7 copy-start.128
  719.2 88.2 %collective-permute-start.6 = (bf16[2,2,256,8,64]{2,4,3,1,0:T(8,128)(2,1)}, bf16[2,2,256,8,64]{2,4,3,1,0:T(8,128)(2,1)}, u32[]{:S(2)}, u32[]{:S(2)}) collective-permute-start(bf16[2,2,256,8,64]{2,4,3,1,0:T(8,128)(2,1)} %pad_maximum_fusion.10), channel_id=1, source_target_pairs={{2,0},{4,2},{6,4},{8,6},{10,8},{12,10},{14,12},{16,14},{18,16},{20... | collective-permute-start | bytes 3145736 | tf_op jit(solution)/shard_map/ppermute | solution.py:27
  721.9 108.1 %collective-permute-start.8 = (bf16[2,2,256,8,64]{2,4,3,1,0:T(8,128)(2,1)}, bf16[2,2,256,8,64]{2,4,3,1,0:T(8,128)(2,1)}, u32[]{:S(2)}, u32[]{:S(2)}) collective-permute-start(bf16[2,2,256,8,64]{2,4,3,1,0:T(8,128)(2,1)} %pad_maximum_fusion.12), channel_id=1, source_target_pairs={{6,0},{8,2},{10,4},{12,6},{14,8},{16,10},{18,12},{20,14},{22,16},{... | collective-permute-start | bytes 3145736 | tf_op jit(solution)/shard_map/ppermute | solution.py:27
  724.4 106.7 %collective-permute-start.7 = (bf16[2,2,256,8,64]{2,4,3,1,0:T(8,128)(2,1)}, bf16[2,2,256,8,64]{2,4,3,1,0:T(8,128)(2,1)}, u32[]{:S(2)}, u32[]{:S(2)}) collective-permute-start(bf16[2,2,256,8,64]{2,4,3,1,0:T(8,128)(2,1)} %pad_maximum_fusion.11), channel_id=1, source_target_pairs={{4,0},{6,2},{8,4},{10,6},{12,8},{14,10},{16,12},{18,14},{20,16},{2... | collective-permute-start | bytes 3145736 | tf_op jit(solution)/shard_map/ppermute | solution.py:27
  733.1 5.3 slice-start
  838.1 133.6 %reduce-scatter.13.cloned.1.call-start = ((), (), s32[]{:S(2)}) async-start(), calls=%async_computation.14 | async-start | bytes 557056
  842.3 45.5 %copy-start.135 = (f32[1,1024]{1,0:T(1,128)S(1)}, f32[1,1024]{1,0:T(1,128)}, u32[]{:S(2)}) copy-start(f32[1,1024]{1,0:T(1,128)} %copy-done.134) | copy-start | bytes 12292
  892.8 172.6 %reduce-scatter.9.cloned.1.call-start = ((), (), s32[]{:S(2)}) async-start(), calls=%async_computation.12 | async-start | bytes 4456448 | tf_op jit(solution)/shard_map/reduce_scatter | solution.py:366
  897.5 376.5 %reduce-scatter.7.cloned.1.call-start = ((), (), s32[]{:S(2)}) async-start(), calls=%async_computation.11 | async-start | bytes 13369344 | tf_op jit(solution)/shard_map/reduce_scatter | solution.py:365
  912.3 4.5 copy-start.5
  912.3 4.5 copy-start.137
  912.4 4.5 copy-start.141
  912.4 4.5 copy-start.143
  912.4 709.7 %reduce-scatter.11.cloned.1.call-start = ((), (), s32[]{:S(2)}) async-start(), calls=%async_computation.13 | async-start | bytes 17825792 | tf_op jit(solution)/shard_map/reduce_scatter | solution.py:367
  912.4 4.4 copy-start.153
  1624.8 48.4 %copy-start.147 = (f32[3,64]{1,0:T(4,128)S(1)}, f32[3,64]{1,0:T(4,128)}, u32[]{:S(2)}) copy-start(f32[3,64]{1,0:T(4,128)} %param.107) | copy-start | bytes 2308
  1624.8 48.4 %copy-start.149 = (f32[3,64]{1,0:T(4,128)S(1)}, f32[3,64]{1,0:T(4,128)}, u32[]{:S(2)}) copy-start(f32[3,64]{1,0:T(4,128)} %param.114) | copy-start | bytes 2308
  1624.8 48.4 %copy-start.150 = (f32[3,64]{1,0:T(4,128)S(1)}, f32[3,64]{1,0:T(4,128)}, u32[]{:S(2)}) copy-start(f32[3,64]{1,0:T(4,128)} %param.115) | copy-start | bytes 2308
  1624.8 49.0 %copy-start.121 = (f32[2,64,512]{2,1,0:T(8,128)S(1)}, f32[2,64,512]{2,1,0:T(8,128)}, u32[]{:S(2)}) copy-start(f32[2,64,512]{2,1,0:T(8,128)} %param.105) | copy-start | bytes 786436
  1624.8 49.0 %copy-start.122 = (f32[2,64,512]{2,1,0:T(8,128)S(1)}, f32[2,64,512]{2,1,0:T(8,128)}, u32[]{:S(2)}) copy-start(f32[2,64,512]{2,1,0:T(8,128)} %reduce-scatter.9.cloned.1.call-done) | copy-start | bytes 786436
  1624.8 49.0 %copy-start.133 = (f32[2,64,512]{2,1,0:T(8,128)S(1)}, f32[2,64,512]{2,1,0:T(8,128)}, u32[]{:S(2)}) copy-start(f32[2,64,512]{2,1,0:T(8,128)} %param.110) | copy-start | bytes 786436
  1627.8 48.0 %copy-start.75 = (f32[6,64,512]{2,1,0:T(8,128)S(1)}, f32[6,64,512]{2,1,0:T(8,128)}, u32[]{:S(2)}) copy-start(f32[6,64,512]{2,1,0:T(8,128)} %param.104) | copy-start | bytes 2359300
  1627.8 48.0 %copy-start.76 = (f32[6,64,512]{2,1,0:T(8,128)S(1)}, f32[6,64,512]{2,1,0:T(8,128)}, u32[]{:S(2)}) copy-start(f32[6,64,512]{2,1,0:T(8,128)} %reduce-scatter.7.cloned.1.call-done) | copy-start | bytes 2359300
  (117 other events, 255.2 us)
Sparse Core Ops, SparseCore 0:
  11.4 96.0 all-gather.4
  110.2 91.9 all-gather.6
  255.0 106.1 all-reduce.6
  379.5 42.5 all-reduce.8
  425.2 113.3 all-gather.8
  562.0 19.4 all-reduce.10
  602.6 22.4 all-reduce.12
  838.2 49.6 all-reduce.14
  892.9 78.6 reduce-scatter.12
  973.8 91.5 reduce-scatter.8
  1071.0 202.8 reduce-scatter.6
  1276.1 345.8 reduce-scatter.10
where the time goes:
time: 1700 us; the launch traced here: 1690 us
  waiting for transfers between devices  1100 us (65%)
  other arithmetic  143 us (8%)
  matrix products  115 us (7%)
  starting transfers between devices  114 us (7%)
  local copies, waits for them, and re-layouts  104 us (6%)
  blocking collectives  87.8 us (5%)
  between operations  25.2 us (1%)
    reduce_scatter x1, waiting for transfers between devices, local(): lax.psum_scatter(mlp_grad_local, 'band', scatter_dimension=1, tiled=True)  345 us
    reduce_scatter x1, waiting for transfers between devices, local(): lax.psum_scatter(proj_grad_local, 'band', scatter_dimension=1, tiled=True)  207 us
    ppermute x12, waiting for transfers between devices, from_behind(): return lax.ppermute(x, axis, pairs)  153 us
    ppermute x12, starting transfers between devices, from_behind(): return lax.ppermute(x, axis, pairs)  113 us
    all_gather x1, waiting for transfers between devices, local(): lax.all_gather(mlp_low, 'band', axis=1, tiled=True)  113 us
    psum x5, waiting for transfers between devices, head_total(): return lax.psum(partials, 'head')  103 us
    reduce_scatter x1, waiting for transfers between devices, local(): lax.psum_scatter(out_grad_local, 'band', scatter_dimension=1, tiled=True)  91.6 us
    unnamed x335, local copies, waits for them, and re-layouts  57.1 us
  transfers between devices with their start and end apart: 24, of which 18 were waited for; matrix products, arithmetic and copies ran while one was open for 10% of the time, Pallas kernels for 0%

commit v1 on v0

--- a/solution.py
+++ b/solution.py
@@ -3,6 +3,8 @@
 import jax
 import jax.numpy as jnp
 from jax import lax
+from jax.experimental import pallas as pl
+from jax.experimental.pallas import tpu as pltpu
 from jax.sharding import PartitionSpec as P
 
 D = 1024
@@ -19,6 +21,567 @@
 ADAM_EPS = 1e-08
 DECAY = 0.1
 GAIN_RATE = 0.5
+
+
+MESH = pl.DeviceIdType.MESH
+ORDERS = ((2, 0, 1), (1, 0, 2))
+GROUP = 4
+
+
+def band_dims(bands):
+    inner = 4 if bands >= 64 else 2
+    return (bands // (inner * inner), inner, inner)
+
+
+def strides_of(dims):
+    return (dims[1] * dims[2], dims[2], 1)
+
+
+def place_of(dims):
+    band = lax.axis_index("band")
+    return band, (
+        band // (dims[1] * dims[2]),
+        (band // dims[2]) % dims[1],
+        band % dims[2],
+    )
+
+
+def stage_list(dims, order):
+    return [(phase, step) for phase in range(3) for step in range(dims[order[phase]] - 1)]
+
+
+def block_of(ref, lead, place, order, phase, index, columns):
+    at = list(place)
+    for done in range(phase):
+        at[order[done]] = slice(None)
+    at[order[phase]] = index
+    return ref.at[(*lead, *at, slice(None), columns)]
+
+
+def greet(dims, place, band, head, extra):
+    barrier = pltpu.get_barrier_semaphore()
+    strides = strides_of(dims)
+    total = jnp.int32(0)
+    peers = []
+    for axis in range(3):
+        for sign in (1, -1):
+            there = place[axis] + sign
+            peers.append(((there >= 0) & (there < dims[axis]), band + sign * strides[axis], head))
+    peers += extra
+    for present, peer_band, peer_head in peers:
+        @pl.when(present)
+        def _():
+            pl.semaphore_signal(barrier, inc=1, device_id=(peer_band, peer_head), device_id_type=MESH)
+        total = total + present.astype(jnp.int32)
+    pl.semaphore_wait(barrier, total)
+
+
+def gather_kernel(dims, has_context, *refs):
+    if has_context:
+        (w_ref, gain_ref, ctx_ref, out_ref, gains_ref, ctx_out,
+         own_sem, send_sem, recv_sem, gsend, grecv, prev_ref, up_sem, csend, crecv, psend, precv) = refs
+    else:
+        (w_ref, gain_ref, out_ref, gains_ref, own_sem, send_sem, recv_sem, gsend, grecv) = refs
+    band, place = place_of(dims)
+    head = lax.axis_index("head")
+    strides = strides_of(dims)
+    count = w_ref.shape[0]
+    half = w_ref.shape[2] // 2
+    bands = dims[0] * dims[1] * dims[2]
+    true = band >= 0
+    extra = []
+    if has_context:
+        base = (band // GROUP) * GROUP
+        mine = band % GROUP
+        for shift in range(1, GROUP):
+            extra.append((true, base + (mine + shift) % GROUP, head))
+        extra.append((band + GROUP < bands, band + GROUP, head))
+        extra.append((band >= GROUP, band - GROUP, head))
+        extra.append((true, band, 1 - head))
+    greet(dims, place, band, head, extra)
+
+    own = [
+        pltpu.make_async_copy(w_ref, out_ref.at[:, place[0], place[1], place[2]], own_sem.at[0]),
+        pltpu.make_async_copy(gain_ref, gains_ref.at[place[0], place[1], place[2]], own_sem.at[1]),
+    ]
+    for copy in own:
+        copy.start()
+
+    def up_copy():
+        return pltpu.make_async_remote_copy(
+            ctx_ref, prev_ref, up_sem.at[0], up_sem.at[1], device_id=(band + GROUP, head), device_id_type=MESH
+        )
+
+    def peer_copy(back, source):
+        return pltpu.make_async_remote_copy(
+            source, ctx_out.at[head, back - 1], csend.at[back - 1], crecv.at[back - 1],
+            device_id=(base + (mine + back) % GROUP, head), device_id_type=MESH,
+        )
+
+    def pair_copy(back):
+        return pltpu.make_async_remote_copy(
+            ctx_out.at[head, back - 1], ctx_out.at[head, back - 1], psend.at[back - 1], precv.at[back - 1],
+            device_id=(band, 1 - head), device_id_type=MESH,
+        )
+
+    if has_context:
+        @pl.when(band + GROUP < bands)
+        def _():
+            up_copy().start()
+        for back in range(1, GROUP):
+            @pl.when(mine + back < GROUP)
+            def _():
+                peer_copy(back, ctx_ref).start()
+
+    def piece(color, m, phase, step, way, incoming):
+        order = ORDERS[color]
+        axis = order[phase]
+        size, at = dims[axis], place[axis]
+        toward = 1 if way == 0 else -1
+        stage = stage_list(dims, order).index((phase, step))
+        if incoming:
+            index = at - toward * (step + 1)
+            present = (index >= 0) & (index < size)
+        else:
+            index = at - toward * step
+            present = (index >= 0) & (index < size) & (at + toward >= 0) & (at + toward < size)
+        columns = pl.ds(color * half, half)
+        target = (band + toward * strides[axis], head)
+        land = block_of(out_ref, (m,), place, order, phase, index, columns)
+        source = w_ref.at[m, :, columns] if stage == 0 else land
+        copy = pltpu.make_async_remote_copy(
+            source, land, send_sem.at[color, stage, way, m], recv_sem.at[color, stage, way, m],
+            device_id=target, device_id_type=MESH,
+        )
+        return present, copy
+
+    def gain_piece(phase, step, way, incoming):
+        order = ORDERS[0]
+        axis = order[phase]
+        size, at = dims[axis], place[axis]
+        toward = 1 if way == 0 else -1
+        stage = stage_list(dims, order).index((phase, step))
+        if incoming:
+            index = at - toward * (step + 1)
+            present = (index >= 0) & (index < size)
+        else:
+            index = at - toward * step
+            present = (index >= 0) & (index < size) & (at + toward >= 0) & (at + toward < size)
+        land = block_of(gains_ref, (), place, order, phase, index, slice(None))
+        source = gain_ref if stage == 0 else land
+        copy = pltpu.make_async_remote_copy(
+            source, land, gsend.at[stage, way], grecv.at[stage, way],
+            device_id=(band + toward * strides[axis], head), device_id_type=MESH,
+        )
+        return present, copy
+
+    stages = [stage_list(dims, order) for order in ORDERS]
+    depth = len(stages[0])
+
+    def context_step(t):
+        @pl.when(t == 1)
+        def _():
+            @pl.when(band >= GROUP)
+            def _():
+                pltpu.make_async_remote_copy(
+                    ctx_ref, prev_ref, up_sem.at[0], up_sem.at[1], device_id=(band - GROUP, head), device_id_type=MESH
+                ).wait_recv()
+            for back in range(1, GROUP):
+                @pl.when((mine + back >= GROUP) & (band >= GROUP))
+                def _():
+                    peer_copy(back, prev_ref).start()
+        @pl.when(t == 4)
+        def _():
+            for back in range(1, GROUP):
+                @pl.when((mine >= back) | (band >= GROUP))
+                def _():
+                    peer_copy(back, ctx_ref).wait_recv()
+                    pair_copy(back).start()
+
+    def gains_step(t):
+        for stage in range(depth + 1):
+            @pl.when(t == stage)
+            def _():
+                if stage == 1:
+                    for copy in own:
+                        copy.wait()
+                if stage > 0:
+                    for way in range(2):
+                        present, copy = gain_piece(*stages[0][stage - 1], way, True)
+                        @pl.when(present)
+                        def _():
+                            copy.wait_recv()
+                if stage < depth:
+                    for way in range(2):
+                        present, copy = gain_piece(*stages[0][stage], way, False)
+                        @pl.when(present)
+                        def _():
+                            copy.start()
+
+    def body(t, carry):
+        gains_step(t)
+        if has_context:
+            context_step(t)
+        for stage in range(depth, -1, -1):
+            m = t - stage
+            @pl.when((m >= 0) & (m < count))
+            def _():
+                for color in range(2):
+                    if stage > 0:
+                        for way in range(2):
+                            present, copy = piece(color, m, *stages[color][stage - 1], way, True)
+                            @pl.when(present)
+                            def _():
+                                copy.wait_recv()
+                    if stage < depth:
+                        for way in range(2):
+                            present, copy = piece(color, m, *stages[color][stage], way, False)
+                            @pl.when(present)
+                            def _():
+                                copy.start()
+        return carry
+
+    lax.fori_loop(0, count + depth, body, 0)
+
+    if has_context:
+        for back in range(1, GROUP):
+            @pl.when((mine >= back) | (band >= GROUP))
+            def _():
+                pltpu.make_async_remote_copy(
+                    ctx_out.at[1 - head, back - 1], ctx_out.at[1 - head, back - 1], psend.at[back - 1],
+                    precv.at[back - 1], device_id=(band, 1 - head), device_id_type=MESH,
+                ).wait_recv()
+                pair_copy(back).wait_send()
+            @pl.when((mine + back < GROUP) | (band >= GROUP))
+            def _():
+                peer_copy(back, ctx_ref).wait_send()
+        @pl.when(band + GROUP < bands)
+        def _():
+            up_copy().wait_send()
+
+    for stage in range(depth):
+        for way in range(2):
+            present, copy = gain_piece(*stages[0][stage], way, False)
+            @pl.when(present)
+            def _():
+                copy.wait_send()
+
+    def drain(m, carry):
+        for stage in range(depth):
+            for color in range(2):
+                for way in range(2):
+                    present, copy = piece(color, m, *stages[color][stage], way, False)
+                    @pl.when(present)
+                    def _():
+                        copy.wait_send()
+        return carry
+
+    lax.fori_loop(0, count, drain, 0)
+
+
+def gather_weights(bands, shard, gain_tile, context, collective_id):
+    dims = band_dims(bands)
+    count, rows, width = shard.shape
+    depth = len(stage_list(dims, ORDERS[0]))
+    vmem = pl.BlockSpec(memory_space=pltpu.VMEM)
+    anyspace = pl.BlockSpec(memory_space=pl.ANY)
+    has_context = context is not None
+    out_shape = [
+        jax.ShapeDtypeStruct((count, *dims, rows, width), shard.dtype),
+        jax.ShapeDtypeStruct((*dims, *gain_tile.shape), gain_tile.dtype),
+    ]
+    scratch = [
+        pltpu.SemaphoreType.DMA((2,)),
+        pltpu.SemaphoreType.DMA((2, depth, 2, count)),
+        pltpu.SemaphoreType.DMA((2, depth, 2, count)),
+        pltpu.SemaphoreType.DMA((depth, 2)),
+        pltpu.SemaphoreType.DMA((depth, 2)),
+    ]
+    args = [shard, gain_tile]
+    if has_context:
+        args.append(context)
+        out_shape.append(jax.ShapeDtypeStruct((2, GROUP - 1, *context.shape), context.dtype))
+        scratch += [
+            pltpu.VMEM(context.shape, context.dtype),
+            pltpu.SemaphoreType.DMA((2,)),
+            pltpu.SemaphoreType.DMA((GROUP - 1,)),
+            pltpu.SemaphoreType.DMA((GROUP - 1,)),
+            pltpu.SemaphoreType.DMA((GROUP - 1,)),
+            pltpu.SemaphoreType.DMA((GROUP - 1,)),
+        ]
+    return pl.pallas_call(
+        partial(gather_kernel, dims, has_context),
+        out_shape=out_shape,
+        in_specs=[vmem] * len(args),
+        out_specs=[anyspace] * len(out_shape),
+        scratch_shapes=scratch,
+        compiler_params=pltpu.CompilerParams(collective_id=collective_id, has_side_effects=True),
+        name="gather_weights",
+    )(*args)
+
+
+def reduce_kernel(dims, has_context, *refs):
+    if has_context:
+        (g_ref, back_ref, out_ref, back_out, gv, load_sem, last_ref, mid_ref, first_ref, send_sem, recv_sem,
+         landed, relay, from_up, csend, crecv, up_sem) = refs
+    else:
+        (g_ref, out_ref, gv, load_sem, last_ref, mid_ref, first_ref, send_sem, recv_sem) = refs
+    band, place = place_of(dims)
+    head = lax.axis_index("head")
+    strides = strides_of(dims)
+    count = g_ref.shape[0]
+    half = g_ref.shape[-1] // 2
+    bands = dims[0] * dims[1] * dims[2]
+    true = band >= 0
+    orders = tuple(order[::-1] for order in ORDERS)
+    lands = (last_ref, mid_ref, first_ref)
+
+    def load(m):
+        return pltpu.make_async_copy(g_ref.at[m], gv.at[m], load_sem.at[m])
+
+    def load_all(m, carry):
+        load(m).start()
+        return carry
+
+    lax.fori_loop(0, count, load_all, 0)
+
+    extra = []
+    if has_context:
+        base = (band // GROUP) * GROUP
+        mine = band % GROUP
+        for shift in range(1, GROUP):
+            extra.append((true, base + (mine + shift) % GROUP, head))
+        extra.append((band + GROUP < bands, band + GROUP, head))
+        extra.append((band >= GROUP, band - GROUP, head))
+    greet(dims, place, band, head, extra)
+
+    def peer_copy(back):
+        return pltpu.make_async_remote_copy(
+            back_ref.at[back - 1], landed.at[back - 1], csend.at[back - 1], crecv.at[back - 1],
+            device_id=(base + (mine + GROUP - back) % GROUP, head), device_id_type=MESH,
+        )
+
+    def down_copy(target):
+        return pltpu.make_async_remote_copy(
+            relay, from_up, up_sem.at[0], up_sem.at[1], device_id=(target, head), device_id_type=MESH
+        )
+
+    if has_context:
+        for back in range(1, GROUP):
+            @pl.when((mine >= back) | (band >= GROUP))
+            def _():
+                peer_copy(back).start()
+
+    def slot(size, step, way):
+        return 0 if size == 2 else step * 2 + way
+
+    def own_block(m, color, phase, index):
+        order = orders[color]
+        at = list(place)
+        for later in range(phase + 1, 3):
+            at[order[later]] = slice(None)
+        at[order[phase]] = index
+        return gv.at[(m, *at, slice(None), pl.ds(color * half, half))]
+
+    def landing(m, color, phase, step, way):
+        size = dims[orders[color][phase]]
+        return lands[phase].at[m, color, slot(size, step, way)]
+
+    def outgoing(m, color, phase, step, way):
+        axis = orders[color][phase]
+        size, at = dims[axis], place[axis]
+        toward = 1 if way == 0 else -1
+        rank = at if way == 0 else size - 1 - at
+        index = size - 1 - step + at if way == 0 else step + at - (size - 1)
+        present = (rank <= step) & (at + toward >= 0) & (at + toward < size)
+        stage = stage_list(dims, orders[color]).index((phase, step))
+        target = (band + toward * strides[axis], head)
+
+        def copy(source):
+            return pltpu.make_async_remote_copy(
+                source, landing(m, color, phase, step, way),
+                send_sem.at[color, stage, way, m], recv_sem.at[color, stage, way, m],
+                device_id=target, device_id_type=MESH,
+            )
+
+        return present, rank, index, copy
+
+    def arrived(m, color, phase, step, way):
+        axis = orders[color][phase]
+        size, at = dims[axis], place[axis]
+        before = at - 1 if way == 0 else at + 1
+        rank = before if way == 0 else size - 1 - before
+        present = (before >= 0) & (before < size) & (rank <= step)
+        _, _, _, copy = outgoing(m, color, phase, step, way)
+        return present, copy(landing(m, color, phase, step, way))
+
+    def add_into(target, source):
+        lead = target.shape[:-2]
+        if len(lead) == 0:
+            target[...] = target[...] + source[...]
+        elif len(lead) == 1:
+            for i in range(lead[0]):
+                target[i] = target[i] + source[i]
+        else:
+            for i in range(lead[0]):
+                for j in range(lead[1]):
+                    target[i, j] = target[i, j] + source[i, j]
+
+    stages = [stage_list(dims, order) for order in orders]
+    depth = len(stages[0])
+
+    def send(m, color, phase, step):
+        axis = orders[color][phase]
+        size = dims[axis]
+        for way in range(2):
+            present, rank, index, copy = outgoing(m, color, phase, step, way)
+            @pl.when(present & (rank == 0))
+            def _():
+                copy(own_block(m, color, phase, index)).start()
+            if step > 0:
+                @pl.when(present & (rank > 0))
+                def _():
+                    from_before = landing(m, color, phase, step - 1, way)
+                    add_into(from_before, own_block(m, color, phase, index))
+                    copy(from_before).start()
+
+    def settle(m, color, phase, step):
+        axis = orders[color][phase]
+        size = dims[axis]
+        for way in range(2):
+            present, copy = arrived(m, color, phase, step, way)
+            @pl.when(present)
+            def _():
+                copy.wait_recv()
+                if step == size - 2:
+                    landed_here = landing(m, color, phase, step, way)
+                    if phase < 2:
+                        add_into(own_block(m, color, phase, place[axis]), landed_here)
+                    else:
+                        columns = pl.ds(color * half, half)
+                        if size == 2:
+                            own = own_block(m, color, phase, place[axis])
+                            out_ref[m, :, columns] = own[...].astype(jnp.float32) + landed_here[...].astype(jnp.float32)
+                        else:
+                            add_into(own_block(m, color, phase, place[axis]), landed_here)
+        if phase == 2 and step == size - 2 and size > 2:
+            columns = pl.ds(color * half, half)
+            out_ref[m, :, columns] = own_block(m, color, phase, place[axis])[...].astype(jnp.float32)
+
+    def body(t, carry):
+        for stage in range(depth, -1, -1):
+            m = t - stage
+            @pl.when((m >= 0) & (m < count))
+            def _():
+                if stage == 0:
+                    load(m).wait()
+                for color in range(2):
+                    if stage > 0:
+                        settle(m, color, *stages[color][stage - 1])
+                    if stage < depth:
+                        send(m, color, *stages[color][stage])
+        if has_context:
+            @pl.when(t == 1)
+            def _():
+                for back in range(1, GROUP):
+                    @pl.when((mine + back < GROUP) | (band >= GROUP))
+                    def _():
+                        peer_copy(back).wait_recv()
+                @pl.when((mine > 0) & (band >= GROUP))
+                def _():
+                    for cut in range(0, relay.shape[0], 64):
+                        rows = pl.ds(cut, 64)
+                        total = landed[GROUP - 2, rows, :].astype(jnp.float32)
+                        for back in range(1, GROUP - 1):
+                            total = total + jnp.where(mine + back >= GROUP, landed[back - 1, rows, :].astype(jnp.float32), 0.0)
+                        relay[rows, :] = total.astype(relay.dtype)
+                    down_copy(band - GROUP).start()
+            @pl.when(t == 4)
+            def _():
+                @pl.when((mine > 0) & (band + GROUP < bands))
+                def _():
+                    down_copy(band + GROUP).wait_recv()
+                for cut in range(0, relay.shape[0], 64):
+                    rows = pl.ds(cut, 64)
+                    total = jnp.where((mine > 0) & (band + GROUP < bands), from_up[rows, :].astype(jnp.float32), 0.0)
+                    for back in range(1, GROUP):
+                        total = total + jnp.where(mine + back < GROUP, landed[back - 1, rows, :].astype(jnp.float32), 0.0)
+                    back_out[rows, :] = total
+        return carry
+
+    lax.fori_loop(0, count + depth, body, 0)
+
+    if has_context:
+        for back in range(1, GROUP):
+            @pl.when((mine >= back) | (band >= GROUP))
+            def _():
+                peer_copy(back).wait_send()
+        @pl.when((mine > 0) & (band >= GROUP))
+        def _():
+            down_copy(band - GROUP).wait_send()
+
+    def drain(m, carry):
+        for stage in range(depth):
+            for color in range(2):
+                phase, step = stages[color][stage]
+                for way in range(2):
+                    present, rank, index, copy = outgoing(m, color, phase, step, way)
+                    @pl.when(present)
+                    def _():
+                        copy(own_block(m, color, phase, index)).wait_send()
+        return carry
+
+    lax.fori_loop(0, count, drain, 0)
+
+
+def reduce_grads(bands, grads, returned, collective_id):
+    dims = band_dims(bands)
+    count, depth_rows, width = grads.shape
+    rows = depth_rows // bands
+    half = width // 2
+    depth = len(stage_list(dims, ORDERS[0]))
+    vmem = pl.BlockSpec(memory_space=pltpu.VMEM)
+    anyspace = pl.BlockSpec(memory_space=pl.ANY)
+    slots = lambda size: 1 if size == 2 else 2 * (size - 1)
+    inner = dims[1]
+    has_context = returned is not None
+    grads = grads.reshape(count, *dims, rows, width)
+    scratch = [
+        pltpu.VMEM(grads.shape, grads.dtype),
+        pltpu.SemaphoreType.DMA((count,)),
+        pltpu.VMEM((count, 2, slots(inner), dims[0], inner, rows, half), grads.dtype),
+        pltpu.VMEM((count, 2, slots(dims[0]), inner, rows, half), grads.dtype),
+        pltpu.VMEM((count, 2, slots(inner), rows, half), grads.dtype),
+        pltpu.SemaphoreType.DMA((2, depth, 2, count)),
+        pltpu.SemaphoreType.DMA((2, depth, 2, count)),
+    ]
+    args = [grads]
+    in_specs = [anyspace]
+    out_shape = [jax.ShapeDtypeStruct((count, rows, width), jnp.float32)]
+    if has_context:
+        args.append(returned)
+        in_specs.append(vmem)
+        ctx_shape = returned.shape[1:]
+        out_shape.append(jax.ShapeDtypeStruct(ctx_shape, jnp.float32))
+        scratch += [
+            pltpu.VMEM(returned.shape, returned.dtype),
+            pltpu.VMEM(ctx_shape, returned.dtype),
+            pltpu.VMEM(ctx_shape, returned.dtype),
+            pltpu.SemaphoreType.DMA((GROUP - 1,)),
+            pltpu.SemaphoreType.DMA((GROUP - 1,)),
+            pltpu.SemaphoreType.DMA((2,)),
+        ]
+    return pl.pallas_call(
+        partial(reduce_kernel, dims, has_context),
+        out_shape=out_shape,
+        in_specs=in_specs,
+        out_specs=[vmem] * len(out_shape),
+        scratch_shapes=scratch,
+        compiler_params=pltpu.CompilerParams(
+            collective_id=collective_id, has_side_effects=True, vmem_limit_bytes=67043328
+        ),
+        name="reduce_grads",
+    )(*args)
 
 
 def from_behind(x, axis, by):
@@ -188,13 +751,18 @@
     out_low = out_master.astype(jnp.bfloat16)
     mlp_low = mlp_master.astype(jnp.bfloat16)
     gain_low = gain_master.astype(jnp.bfloat16)
-    proj_w, out_w, mlp_w, gain_w = (
-        lax.all_gather(proj_low, "band", axis=1, tiled=True),
-        lax.all_gather(out_low, "band", axis=1, tiled=True),
-        lax.all_gather(mlp_low, "band", axis=1, tiled=True),
-        lax.all_gather(gain_low, "band", axis=1, tiled=True),
-    )
-    gains = gain_w.astype(jnp.float32)
+    bands = lax.axis_size("band")
+    shard_rows, width = proj_low.shape[1:]
+    chunks = mlp_low.shape[2] // width
+    mlp_cut = mlp_low.reshape(2, shard_rows, chunks, width).transpose(0, 2, 1, 3)
+    shard = jnp.concatenate([proj_low, out_low, mlp_cut.reshape(2 * chunks, shard_rows, width)])
+    gain_tile = jnp.pad(gain_low.astype(jnp.float32), ((0, 5), (0, 128 - shard_rows)))
+    gathered, gain_tiles = gather_weights(bands, shard, gain_tile, None, 1)
+    gathered = gathered.reshape(shard.shape[0], model_width, width)
+    proj_w, out_w = gathered[:6], gathered[6:8]
+    mlp_w = gathered[8:].reshape(2, chunks, model_width, width).transpose(0, 2, 1, 3)
+    mlp_w = mlp_w.reshape(2, model_width, chunks * width)
+    gains = gain_tiles.reshape(bands, 8, 128)[:, :3, :shard_rows].transpose(1, 0, 2).reshape(3, model_width)
     local_width = proj_w.shape[2]
     local_heads = local_width // HEAD_DIM
     score_scale = HEAD_DIM ** (-0.5)
@@ -361,12 +929,19 @@
     grad_tokens = (grad_one + back_zero).reshape(streams, band_rows, model_width)
     out_grad_local = jnp.stack([grad_self_out, grad_cross_out])
     gain_grad_local = jnp.stack([gain_grad_one, gain_grad_two, gain_grad_three])
-    proj_grad, out_grad, mlp_grad, gain_grad = (
-        lax.psum_scatter(proj_grad_local, "band", scatter_dimension=1, tiled=True),
-        lax.psum_scatter(out_grad_local, "band", scatter_dimension=1, tiled=True),
-        lax.psum_scatter(mlp_grad_local, "band", scatter_dimension=1, tiled=True),
-        lax.psum_scatter(gain_grad_local, "band", scatter_dimension=1, tiled=True),
-    )
+    mlp_parts = mlp_grad_local.astype(jnp.bfloat16).reshape(2, model_width, chunks, width).transpose(0, 2, 1, 3)
+    grads = jnp.concatenate(
+        [
+            proj_grad_local.astype(jnp.bfloat16),
+            out_grad_local.astype(jnp.bfloat16),
+            mlp_parts.reshape(2 * chunks, model_width, width),
+        ]
+    )
+    (summed,) = reduce_grads(bands, grads, None, 2)
+    proj_grad, out_grad = summed[:6], summed[6:8]
+    mlp_grad = summed[8:].reshape(2, chunks, shard_rows, width).transpose(0, 2, 1, 3)
+    mlp_grad = mlp_grad.reshape(2, shard_rows, chunks * width)
+    gain_grad = lax.psum_scatter(gain_grad_local, "band", scatter_dimension=1, tiled=True)
     local_squares = (
         jnp.sum(proj_grad * proj_grad)
         + jnp.sum(out_grad * out_grad)

time: 1700 us -> 1140 us (0.67)
  waiting for transfers between devices: 1100 us -> 230 us
  Pallas kernels: 0 us -> 342 us
  local copies, waits for them, and re-layouts: 104 us -> 167 us
  blocking collectives: 87.8 us -> 36.8 us
  starting transfers between devices: 114 us -> 93.7 us
    reduce_scatter x3 -> x0, waiting for transfers between devices: 643 us -> none  [the longest x1 345 us: local(): lax.psum_scatter(mlp_grad_local, 'band', scatter_dimension=1, tiled=True)]
    pallas_call x0 -> x2, Pallas kernels: none -> 342 us  [the longest x1 179 us: reduce_grads(): pl.pallas_call(partial(reduce_kernel, dims, has_context), out_shape=out_s...]
    all_gather x3 -> x0, waiting for transfers between devices: 159 us -> none  [the longest x1 113 us: local(): lax.all_gather(mlp_low, 'band', axis=1, tiled=True)]
    psum x5, waiting for transfers between devices: 103 us -> 26.7 us  [head_total(): return lax.psum(partials, 'head')]
    all_gather x1 -> x0, blocking collectives: 43.1 us -> none  [local(): lax.all_gather(gain_low, 'band', axis=1, tiled=True)]
    unnamed x13 -> x7, waiting for transfers between devices: 41.7 us -> 71.3 us
    ppermute x12, waiting for transfers between devices: 153 us -> 132 us  [from_behind(): return lax.ppermute(x, axis, pairs)]
    slice x0 -> x4, local copies, waits for them, and re-layouts: none -> 20.3 us  [the longest x1 7.79 us: local(): gathered[8:].reshape(2, chunks, model_width, width).transpose(0, 2, 1, 3)]
  transfers between devices with their start and end apart: 24 -> 18, of which waited for: 18 -> 12; matrix products, arithmetic and copies ran while one was open for 10% -> 12% of each run, Pallas kernels for 0% -> 16%
where the time goes in v1:
time: 1140 us; the launch traced here: 1130 us
  Pallas kernels  342 us (30%)
  waiting for transfers between devices  230 us (20%)
  local copies, waits for them, and re-layouts  167 us (15%)
  other arithmetic  131 us (11%)
  matrix products  98.7 us (9%)
  starting transfers between devices  93.7 us (8%)
  blocking collectives  36.8 us (3%)
  between operations  25.3 us (2%)
    pallas_call x1, Pallas kernels, reduce_grads(): pl.pallas_call(partial(reduce_kernel, dims, has_context), out_shape=out_s...  179 us
    pallas_call x1, Pallas kernels, gather_weights(): pl.pallas_call(partial(gather_kernel, dims, has_context), out_shape=out_s...  163 us
    ppermute x12, waiting for transfers between devices, from_behind(): return lax.ppermute(x, axis, pairs)  132 us
    ppermute x12, starting transfers between devices, from_behind(): return lax.ppermute(x, axis, pairs)  93.3 us
    unnamed x7, waiting for transfers between devices  71.3 us
    unnamed x414, local copies, waits for them, and re-layouts  67.7 us
    psum x1, blocking collectives, local(): grad_norm = jnp.sqrt(lax.psum(local_squares, ('band', 'head')))  36.8 us
    dot_general x10, matrix products, matmul(): return jnp.dot(former, latter, preferred_element_type=jnp.float32)  27.5 us
  transfers between devices with their start and end apart: 18, of which 12 were waited for; matrix products, arithmetic and copies ran while one was open for 12% of the time, Pallas kernels for 16%

profile of v1, /device:TPU:0, one launch (start us, length us, event | category | flops | bytes accessed | tf_op | source)
XLA Modules:
  0.0 1126.3 jit_solution(11444025592262698137)
XLA Ops:
  14.3 162.7 %gather_weights.1 = (bf16[16,4,2,2,64,512]{5,4,3,2,1,0:T(8,128)(2,1)}, f32[4,2,2,8,128]{4,3,2,1,0:T(8,128)}) custom-call(bf16[16,64,512]{2,1,0:T(8,128)(2,1)} %pad_maximum_fusion.9.refs_0_, f32[8,128]{1,0:T(8,128)} %pad_convert_fusion.refs_1_), custom_call_target="tpu_custom_call" | custom-call | tf_op jit(solution)/shard_map/gather_weights/pallas_call | solution.py:312
  178.0 5.9 fusion.162
  195.0 3.4 collective-permute-start.2
  198.4 2.6 collective-permute-start.1
  201.0 3.9 collective-permute-start
  218.3 3.9 collective-permute-done.2
  222.2 2.6 fusion.169
  224.9 15.4 %collective-permute-done.1 = bf16[2,2,256,8,64]{2,1,4,3,0:T(2,128)(2,1)} collective-permute-done((bf16[2,2,256,8,64]{2,1,4,3,0:T(2,128)(2,1)}, bf16[2,2,256,8,64]{2,1,4,3,0:T(2,128)(2,1)}, u32[]{:S(2)}, u32[]{:S(2)}) %collective-permute-start.1) | collective-permute-done | bytes 1048608 | tf_op jit(solution)/shard_map/ppermute | solution.py:590
  240.3 4.4 fusion.168
  244.8 4.5 fusion.167
  251.0 3.1 multiply_select_fusion.5
  257.2 3.2 multiply_select_fusion.2
  274.3 2.9 fusion.156
  291.2 9.0 fusion.142
  300.2 2.1 copy_bitcast_fusion.6
  302.3 4.7 multiply_select_fusion.3
  307.0 8.0 fusion.140
  328.0 2.2 fusion.86
  333.3 18.6 %collective-permute-start.5 = (bf16[2,2,128,8,64]{2,4,3,1,0:T(8,128)(2,1)S(1)}, bf16[2,2,128,8,64]{2,4,3,1,0:T(8,128)(2,1)S(1)}, u32[]{:S(2)}, u32[]{:S(2)}) collective-permute-start(bf16[2,2,128,8,64]{2,4,3,1,0:T(8,128)(2,1)S(1)} %copy_dynamic-update-slice_fusion), channel_id=1, source_target_pairs={{0,2},{2,4},{4,6},{6,8},{8,10},{10,12},{12,14},{14,16},{16,18},{18... | collective-permute-start | bytes 1572872 | tf_op jit(solution)/shard_map/ppermute | solution.py:590
  351.9 54.2 %collective-permute-start.4 = (bf16[2,2,128,8,64]{2,4,3,1,0:T(8,128)(2,1)S(1)}, bf16[2,2,128,8,64]{2,4,3,1,0:T(8,128)(2,1)}, u32[]{:S(2)}, u32[]{:S(2)}) collective-permute-start(bf16[2,2,128,8,64]{2,4,3,1,0:T(8,128)(2,1)S(1)} %copy_dynamic-update-slice_fusion), channel_id=1, source_target_pairs={{0,4},{2,6},{4,8},{6,10},{8,12},{10,14},{12,16},{14,18},{16,20},{1... | collective-permute-start | bytes 1572872 | tf_op jit(solution)/shard_map/ppermute | solution.py:590
  408.3 3.7 collective-permute-done.4
  412.0 2.1 collective-permute-done.3
  414.1 2.1 select_select_fusion
  429.1 7.8 slice.355
  437.0 11.7 %copy.315 = bf16[2,4,1024,512]{2,3,1,0:T(8,128)(2,1)} copy(bf16[2,4,1024,512]{3,2,1,0:T(8,128)(2,1)} %bitcast.582) | data formatting | bytes 16777216 | tf_op jit(solution)/shard_map/reshape | solution.py:763
  448.7 6.6 fusion.163
  455.3 11.8 %all-reduce.10.cloned.1.call-done = f32[512,1024]{1,0:T(8,128)} async-done(((f32[512,1024]{1,0:T(8,128)}), f32[512,1024]{1,0:T(8,128)}) %all-reduce.10.cloned.1.call-update) | async-done | bytes 2097168 | tf_op jit(solution)/shard_map/psum | solution.py:616
  467.0 2.7 fusion.154
  470.5 12.6 %multiply_convert_fusion.2 = (bf16[512,2048]{1,0:T(8,128)(2,1)}, f32[512,2048]{1,0:T(8,128)S(1)}, f32[512,2048]{1,0:T(8,128)S(1)}) fusion(bf16[1024,2048]{0,1:T(8,128)(2,1)S(1)} %bitcast.647, f32[512,1024]{1,0:T(8,128)S(1)} %get-tuple-element.659, f32[1024]{0:T(1024)S(1)} %mul.565, f32[512]{0:T(512)S(1)} %fusion.132, f32[512]{0:T(512)S(1)} %broadcast_multiply_fusion), kind=kOutput, calls=%fused_computation.87 | convolution fusion | flops 2217738240 | bytes 16785408 | tf_op jit(solution)/shard_map/dot_general | solution.py:600
  483.1 3.6 fusion.39
  488.0 3.7 fusion.204
  493.5 2.7 copy.366
  496.2 6.5 fusion.203
  502.6 14.9 %all-reduce.12.cloned.1.call-done = f32[512,1024]{1,0:T(8,128)} async-done(((f32[512,1024]{1,0:T(8,128)}), f32[512,1024]{1,0:T(8,128)}) %all-reduce.12.cloned.1.call-update) | async-done | bytes 2097168 | tf_op jit(solution)/shard_map/psum | solution.py:616
  517.6 3.7 multiply_reduce_fusion.2
  525.8 2.4 reshape.563
  528.1 2.5 copy.318
  530.7 2.4 convolution_bitcast_fusion.24
  537.0 2.2 fusion.205
  547.1 4.5 convert_bitcast_fusion.1
  551.6 7.3 collective-permute-done.9
  558.9 14.3 %collective-permute-done.10 = bf16[2,2,128,8,64]{2,4,3,1,0:T(8,128)(2,1)S(1)} collective-permute-done((bf16[2,2,128,8,64]{2,4,3,1,0:T(8,128)(2,1)S(1)}, bf16[2,2,128,8,64]{2,4,3,1,0:T(8,128)(2,1)S(1)}, u32[]{:S(2)}, u32[]{:S(2)}) %collective-permute-start.10) | collective-permute-done | bytes 524320 | tf_op jit(solution)/shard_map/ppermute | solution.py:590
  576.7 3.0 multiply_reduce_fusion.3
  584.7 2.5 convolution_bitcast_fusion.25
  587.2 2.5 convolution_bitcast_fusion.26
  599.0 11.0 multiply_convert_fusion.1
  619.0 11.0 multiply_convert_fusion
  667.8 66.5 %collective-permute-done.6 = bf16[2,2,256,8,64]{2,4,3,1,0:T(8,128)(2,1)} collective-permute-done((bf16[2,2,256,8,64]{2,4,3,1,0:T(8,128)(2,1)}, bf16[2,2,256,8,64]{2,4,3,1,0:T(8,128)(2,1)}, u32[]{:S(2)}, u32[]{:S(2)}) %collective-permute-start.6) | collective-permute-done | bytes 1048608 | tf_op jit(solution)/shard_map/ppermute | solution.py:590
  734.3 15.6 %collective-permute-done.8 = bf16[2,2,256,8,64]{2,4,3,1,0:T(8,128)(2,1)} collective-permute-done((bf16[2,2,256,8,64]{2,4,3,1,0:T(8,128)(2,1)}, bf16[2,2,256,8,64]{2,4,3,1,0:T(8,128)(2,1)}, u32[]{:S(2)}, u32[]{:S(2)}) %collective-permute-start.8) | collective-permute-done | bytes 1048608 | tf_op jit(solution)/shard_map/ppermute | solution.py:590
  749.9 3.5 collective-permute-done.7
  753.4 2.6 fusion.51
  758.8 2.2 add_add_fusion.4
  762.9 2.4 convert_bitcast_fusion
  766.0 4.3 fusion.26
  773.6 2.4 copy.374
  777.3 3.2 fusion.66
  791.5 8.0 constant_dynamic-update-slice_fusion.2.refs_0_
  799.5 179.0 %reduce_grads.1 = f32[16,64,512]{2,1,0:T(8,128)} custom-call(bf16[16,4,2,2,64,512]{5,4,3,2,1,0:T(8,128)(2,1)} %constant_dynamic-update-slice_fusion.2.refs_0_), custom_call_target="tpu_custom_call" | custom-call | tf_op jit(solution)/shard_map/reduce_grads/pallas_call | solution.py:574
  986.3 2.2 fusion.60
  990.7 4.4 add_add_fusion.3
  995.1 71.2 %reduce-scatter.4.cloned.1.call-done = f32[64,3]{1,0:T(8,128)} async-done(((f32[1024,3]{1,0:T(8,128)}), f32[64,3]{1,0:T(8,128)}) %reduce-scatter.4.cloned.1.call-update) | async-done | bytes 784
  1068.5 2.9 add_convert_fusion
  1071.3 36.8 %psum.63 = f32[]{:T(128)} all-reduce(f32[]{:T(128)S(6)} %add.267), channel_id=1, replica_groups=mesh['band'=16,'head'=2] {'band','head'}, use_global_device_ids=true, to_apply=%region_126.127 | all-reduce | flops 1 | bytes 8 | tf_op jit(solution)/shard_map/psum | solution.py:951
  1114.9 2.2 multiply_subtract_fusion
  (672 shorter events, 226.3 us)
Async XLA Ops:
  7.2 5.7 copy-start.162
  7.2 5.8 copy-start.96
  7.2 5.8 copy-start.80
  7.2 409.1 %all-reduce.8.cloned.1.call-start = ((), (), s32[]{:S(2)}) async-start(), calls=%async_computation.1 | async-start | bytes 4194304 | tf_op jit(solution)/shard_map/psum | solution.py:616
  178.0 5.9 copy-start.177
  178.0 5.9 copy-start.6
  183.9 6.4 copy-start.58
  192.6 14.3 %copy-start.62 = (bf16[1,4,2,2,64,512]{5,4,3,2,1,0:T(8,128)(2,1)S(1)}, bf16[1,4,2,2,64,512]{5,4,3,2,1,0:T(8,128)(2,1)}, u32[]{:S(2)}) copy-start(bf16[1,4,2,2,64,512]{5,4,3,2,1,0:T(8,128)(2,1)} %get-tuple-element.680) | copy-start | bytes 3145732
  192.6 14.3 %copy-start.86 = (bf16[2,256,1024]{2,1,0:T(8,128)(2,1)S(1)}, bf16[2,256,1024]{2,1,0:T(8,128)(2,1)}, u32[]{:S(2)}) copy-start(bf16[2,256,1024]{2,1,0:T(8,128)(2,1)} %copy-done.85) | copy-start | bytes 3145732
  195.0 27.2 %collective-permute-start.2 = (bf16[2,2,256,8,64]{2,1,4,3,0:T(2,128)(2,1)}, bf16[2,2,256,8,64]{2,1,4,3,0:T(2,128)(2,1)S(1)}, u32[]{:S(2)}, u32[]{:S(2)}) collective-permute-start(bf16[2,2,256,8,64]{2,1,4,3,0:T(2,128)(2,1)} %constant_dynamic-update-slice_fusion), channel_id=1, source_target_pairs={{0,6},{2,8},{4,10},{6,12},{8,14},{10,16},{12,18},{14,20},{16,22},{... | collective-permute-start | bytes 3145736 | tf_op jit(solution)/shard_map/ppermute | solution.py:590
  198.4 41.8 %collective-permute-start.1 = (bf16[2,2,256,8,64]{2,1,4,3,0:T(2,128)(2,1)}, bf16[2,2,256,8,64]{2,1,4,3,0:T(2,128)(2,1)}, u32[]{:S(2)}, u32[]{:S(2)}) collective-permute-start(bf16[2,2,256,8,64]{2,1,4,3,0:T(2,128)(2,1)} %constant_dynamic-update-slice_fusion), channel_id=1, source_target_pairs={{0,4},{2,6},{4,8},{6,10},{8,12},{10,14},{12,16},{14,18},{16,20},{1... | collective-permute-start | bytes 3145736 | tf_op jit(solution)/shard_map/ppermute | solution.py:590
  201.0 43.8 %collective-permute-start = (bf16[2,2,256,8,64]{2,1,4,3,0:T(2,128)(2,1)}, bf16[2,2,256,8,64]{2,1,4,3,0:T(2,128)(2,1)}, u32[]{:S(2)}, u32[]{:S(2)}) collective-permute-start(bf16[2,2,256,8,64]{2,1,4,3,0:T(2,128)(2,1)} %constant_dynamic-update-slice_fusion), channel_id=1, source_target_pairs={{0,2},{2,4},{4,6},{6,8},{8,10},{10,12},{12,14},{14,16},{16,18},{18... | collective-permute-start | bytes 3145736 | tf_op jit(solution)/shard_map/ppermute | solution.py:590
  207.7 60.3 %copy-start.10 = (bf16[256,512]{0,1:T(8,128)(2,1)}, bf16[256,512]{0,1:T(8,128)(2,1)S(1)}, u32[]{:S(2)}) copy-start(bf16[256,512]{0,1:T(8,128)(2,1)S(1)} %get-tuple-element.723) | copy-start | bytes 786436
  207.7 63.8 %copy-start.8 = (bf16[256,512]{0,1:T(8,128)(2,1)}, bf16[256,512]{0,1:T(8,128)(2,1)S(1)}, u32[]{:S(2)}) copy-start(bf16[256,512]{0,1:T(8,128)(2,1)S(1)} %get-tuple-element.724) | copy-start | bytes 786436
  207.7 4.2 copy-start.190
  209.3 7.1 copy-start.142
  224.8 46.7 %copy-start.68 = (bf16[1,1,256,8,64]{2,4,1,3,0:T(8,128)(2,1)}, bf16[1,1,256,8,64]{2,4,1,3,0:T(8,128)(2,1)S(1)}, u32[]{:S(2)}) copy-start(bf16[1,1,256,8,64]{2,4,1,3,0:T(8,128)(2,1)S(1)} %copy.535) | copy-start | bytes 786436
  224.9 43.2 %copy-start.74 = (bf16[1,1,256,8,64]{2,4,1,3,0:T(8,128)(2,1)}, bf16[1,1,256,8,64]{2,4,1,3,0:T(8,128)(2,1)S(1)}, u32[]{:S(2)}) copy-start(bf16[1,1,256,8,64]{2,4,1,3,0:T(8,128)(2,1)S(1)} %copy.538) | copy-start | bytes 786436
  244.7 20.3 %copy-start.72 = (bf16[1,1,256,8,64]{2,4,1,3,0:T(8,128)(2,1)}, bf16[1,1,256,8,64]{2,4,1,3,0:T(8,128)(2,1)S(1)}, u32[]{:S(2)}) copy-start(bf16[1,1,256,8,64]{2,4,1,3,0:T(8,128)(2,1)S(1)} %copy.536) | copy-start | bytes 786436
  244.8 17.3 %copy-start.78 = (bf16[1,1,256,8,64]{2,4,1,3,0:T(8,128)(2,1)}, bf16[1,1,256,8,64]{2,4,1,3,0:T(8,128)(2,1)S(1)}, u32[]{:S(2)}) copy-start(bf16[1,1,256,8,64]{2,4,1,3,0:T(8,128)(2,1)S(1)} %copy.539) | copy-start | bytes 786436
  249.4 11.0 copy-start.70
  249.4 4.7 copy-start.76
  278.5 9.0 copy-start.19
  280.7 26.3 %copy-start.181 = (f32[8,256]{1,0:T(8,128)}, f32[8,256]{1,0:T(8,128)S(1)}, u32[]{:S(2)}) copy-start(f32[8,256]{1,0:T(8,128)S(1)} %log_add_fusion.2) | copy-start | bytes 24580
  288.8 11.4 %copy-start.179 = (f32[8,256]{1,0:T(8,128)}, f32[8,256]{1,0:T(8,128)S(1)}, u32[]{:S(2)}) copy-start(f32[8,256]{1,0:T(8,128)S(1)} %log_add_fusion.1) | copy-start | bytes 24580
  290.3 25.7 %copy-start.100 = (bf16[256,8,64]{0,2,1:T(8,128)(2,1)}, bf16[256,8,64]{0,2,1:T(8,128)(2,1)S(1)}, u32[]{:S(2)}) copy-start(bf16[256,8,64]{0,2,1:T(8,128)(2,1)S(1)} %get-tuple-element.755) | copy-start | bytes 786436
  327.9 139.1 %all-reduce.10.cloned.1.call-start = ((), (), s32[]{:S(2)}) async-start(), calls=%async_computation.2 | async-start | bytes 4194304 | tf_op jit(solution)/shard_map/psum | solution.py:616
  333.3 75.0 %collective-permute-start.5 = (bf16[2,2,128,8,64]{2,4,3,1,0:T(8,128)(2,1)S(1)}, bf16[2,2,128,8,64]{2,4,3,1,0:T(8,128)(2,1)S(1)}, u32[]{:S(2)}, u32[]{:S(2)}) collective-permute-start(bf16[2,2,128,8,64]{2,4,3,1,0:T(8,128)(2,1)S(1)} %copy_dynamic-update-slice_fusion), channel_id=1, source_target_pairs={{0,2},{2,4},{4,6},{6,8},{8,10},{10,12},{12,14},{14,16},{16,18},{18... | collective-permute-start | bytes 1572872 | tf_op jit(solution)/shard_map/ppermute | solution.py:590
  351.9 60.1 %collective-permute-start.4 = (bf16[2,2,128,8,64]{2,4,3,1,0:T(8,128)(2,1)S(1)}, bf16[2,2,128,8,64]{2,4,3,1,0:T(8,128)(2,1)}, u32[]{:S(2)}, u32[]{:S(2)}) collective-permute-start(bf16[2,2,128,8,64]{2,4,3,1,0:T(8,128)(2,1)S(1)} %copy_dynamic-update-slice_fusion), channel_id=1, source_target_pairs={{0,4},{2,6},{4,8},{6,10},{8,12},{10,14},{12,16},{14,18},{16,20},{1... | collective-permute-start | bytes 1572872 | tf_op jit(solution)/shard_map/ppermute | solution.py:590
  406.1 8.0 collective-permute-start.3
  429.0 88.5 %all-reduce.12.cloned.1.call-start = ((), (), s32[]{:S(2)}) async-start(), calls=%async_computation.3 | async-start | bytes 4194304 | tf_op jit(solution)/shard_map/psum | solution.py:616
  469.7 13.4 %copy-start = (f32[512,1024]{1,0:T(8,128)}, f32[512,1024]{1,0:T(8,128)S(1)}, u32[]{:S(2)}) copy-start(f32[512,1024]{1,0:T(8,128)S(1)} %get-tuple-element.659) | copy-start | bytes 6291460
  470.5 12.6 %copy-start.90 = (bf16[1,1024,4,512]{1,3,2,0:T(8,128)(2,1)S(1)}, bf16[1,1024,4,512]{1,3,2,0:T(8,128)(2,1)}, u32[]{:S(2)}) copy-start(bf16[1,1024,4,512]{1,3,2,0:T(8,128)(2,1)} %get-tuple-element.685) | copy-start | bytes 12582916
  470.5 12.6 %copy-start.92 = (bf16[2,256,1024]{2,1,0:T(8,128)(2,1)S(1)}, bf16[2,256,1024]{2,1,0:T(8,128)(2,1)}, u32[]{:S(2)}) copy-start(bf16[2,256,1024]{2,1,0:T(8,128)(2,1)} %param.102) | copy-start | bytes 3145732
  491.7 84.7 %all-reduce.14.cloned.1.call-start = ((), (), s32[]{:S(2)}) async-start(), calls=%async_computation.4 | async-start | bytes 4194304 | tf_op jit(solution)/shard_map/psum | solution.py:616
  517.6 3.7 copy-start.1
  517.6 3.7 copy-start.50
  539.2 7.8 copy-start.2
  539.2 447.1 %all-reduce.16.cloned.1.call-start = ((), (), s32[]{:S(2)}) async-start(), calls=%async_computation.6 | async-start | bytes 10485760 | tf_op jit(solution)/shard_map/psum | solution.py:616
  539.3 7.8 copy-start.195
  542.9 16.0 %collective-permute-start.9 = (bf16[2,2,128,8,64]{2,4,3,1,0:T(8,128)(2,1)S(1)}, bf16[2,2,128,8,64]{2,4,3,1,0:T(8,128)(2,1)S(1)}, u32[]{:S(2)}, u32[]{:S(2)}) collective-permute-start(bf16[2,2,128,8,64]{2,4,3,1,0:T(8,128)(2,1)S(1)} %get-tuple-element.698), channel_id=1, source_target_pairs={{2,0},{4,2},{6,4},{8,6},{10,8},{12,10},{14,12},{16,14},{18,16},{20... | collective-permute-start | bytes 1572872 | tf_op jit(solution)/shard_map/ppermute | solution.py:590
  544.2 29.0 %collective-permute-start.10 = (bf16[2,2,128,8,64]{2,4,3,1,0:T(8,128)(2,1)S(1)}, bf16[2,2,128,8,64]{2,4,3,1,0:T(8,128)(2,1)S(1)}, u32[]{:S(2)}, u32[]{:S(2)}) collective-permute-start(bf16[2,2,128,8,64]{2,4,3,1,0:T(8,128)(2,1)S(1)} %get-tuple-element.699), channel_id=1, source_target_pairs={{4,0},{6,2},{8,4},{10,6},{12,8},{14,10},{16,12},{18,14},{20,16},{2... | collective-permute-start | bytes 1572872 | tf_op jit(solution)/shard_map/ppermute | solution.py:590
  545.5 27.8 %copy-start.57 = (f32[1,2,128,8,64]{2,4,3,1,0:T(8,128)S(1)}, f32[1,2,128,8,64]{2,4,3,1,0:T(8,128)}, u32[]{:S(2)}) copy-start(f32[1,2,128,8,64]{2,4,3,1,0:T(8,128)} %convolution_bitcast_fusion.24) | copy-start | bytes 1572868
  545.5 27.7 %collective-permute-start.11 = (bf16[2,2,128,8,64]{2,4,3,1,0:T(8,128)(2,1)S(1)}, bf16[2,2,128,8,64]{2,4,3,1,0:T(8,128)(2,1)S(1)}, u32[]{:S(2)}, u32[]{:S(2)}) collective-permute-start(bf16[2,2,128,8,64]{2,4,3,1,0:T(8,128)(2,1)S(1)} %get-tuple-element.700), channel_id=1, source_target_pairs={{6,0},{8,2},{10,4},{12,6},{14,8},{16,10},{18,12},{20,14},{22,16},{... | collective-permute-start | bytes 1572872 | tf_op jit(solution)/shard_map/ppermute | solution.py:590
  584.7 5.1 copy-start.132
  587.2 4.3 copy-start.110
  587.2 4.3 copy-start.130
  599.0 11.0 copy-start.145
  619.0 11.0 copy-start.143
  643.7 4.7 copy-start.165
  643.7 4.7 copy-start.170
  647.0 4.1 copy-start.167
  647.0 4.1 copy-start.172
  647.0 87.4 %collective-permute-start.6 = (bf16[2,2,256,8,64]{2,4,3,1,0:T(8,128)(2,1)}, bf16[2,2,256,8,64]{2,4,3,1,0:T(8,128)(2,1)}, u32[]{:S(2)}, u32[]{:S(2)}) collective-permute-start(bf16[2,2,256,8,64]{2,4,3,1,0:T(8,128)(2,1)} %pad_maximum_fusion.10), channel_id=1, source_target_pairs={{2,0},{4,2},{6,4},{8,6},{10,8},{12,10},{14,12},{16,14},{18,16},{20... | collective-permute-start | bytes 3145736 | tf_op jit(solution)/shard_map/ppermute | solution.py:590
  649.6 100.3 %collective-permute-start.8 = (bf16[2,2,256,8,64]{2,4,3,1,0:T(8,128)(2,1)}, bf16[2,2,256,8,64]{2,4,3,1,0:T(8,128)(2,1)}, u32[]{:S(2)}, u32[]{:S(2)}) collective-permute-start(bf16[2,2,256,8,64]{2,4,3,1,0:T(8,128)(2,1)} %pad_maximum_fusion.12), channel_id=1, source_target_pairs={{6,0},{8,2},{10,4},{12,6},{14,8},{16,10},{18,12},{20,14},{22,16},{... | collective-permute-start | bytes 3145736 | tf_op jit(solution)/shard_map/ppermute | solution.py:590
  652.3 101.1 %collective-permute-start.7 = (bf16[2,2,256,8,64]{2,4,3,1,0:T(8,128)(2,1)}, bf16[2,2,256,8,64]{2,4,3,1,0:T(8,128)(2,1)}, u32[]{:S(2)}, u32[]{:S(2)}) collective-permute-start(bf16[2,2,256,8,64]{2,4,3,1,0:T(8,128)(2,1)} %pad_maximum_fusion.11), channel_id=1, source_target_pairs={{4,0},{6,2},{8,4},{10,6},{12,8},{14,10},{16,12},{18,14},{20,16},{2... | collective-permute-start | bytes 3145736 | tf_op jit(solution)/shard_map/ppermute | solution.py:590
  663.3 3.7 copy-start.120
  761.0 305.3 %reduce-scatter.4.cloned.1.call-start = ((), (), s32[]{:S(2)}) async-start(), calls=%async_computation.5 | async-start | bytes 557056
  766.0 4.3 copy-start.88
  978.5 7.8 copy-start.7
  978.5 7.8 copy-start.178
  978.6 7.8 copy-start.183
  983.5 5.1 copy-start.188
  990.7 77.7 %copy-start.3 = (f32[512,1024]{1,0:T(8,128)S(1)}, f32[512,1024]{1,0:T(8,128)}, u32[]{:S(2)}) copy-start(f32[512,1024]{1,0:T(8,128)} %copy-done) | copy-start | bytes 6291460
  (149 other events, 266.2 us)
Sparse Core Ops, SparseCore 0:
  328.0 84.5 all-reduce.7
  429.2 37.8 all-reduce.9
  491.8 25.6 all-reduce.11
  539.4 22.4 all-reduce.13
  761.1 49.3 all-reduce.15
  990.9 75.4 reduce-scatter.3

commit v2 on v1

--- a/solution.py
+++ b/solution.py
@@ -21,6 +21,7 @@
 ADAM_EPS = 1e-08
 DECAY = 0.1
 GAIN_RATE = 0.5
+LANES = 128
 
 
 MESH = pl.DeviceIdType.MESH
@@ -584,12 +585,6 @@
     )(*args)
 
 
-def from_behind(x, axis, by):
-    size = lax.axis_size(axis)
-    pairs = [(i, i + by) for i in range(size) if 0 <= i + by < size]
-    return lax.ppermute(x, axis, pairs)
-
-
 def norm_rows(values, gain_row):
     centre = values - jnp.mean(values, axis=-1, keepdims=True)
     spread = jnp.mean(centre * centre, axis=-1, keepdims=True)
@@ -612,107 +607,237 @@
     )
 
 
-def head_total(partials):
-    return lax.psum(partials, "head")
-
-
-def earlier_bands(key_pair):
-    return [from_behind(key_pair, "band", behind) for behind in range(1, SEQ_BANDS)]
-
-
-def caption_from_first(caption_pair):
-    return [from_behind(caption_pair, "band", behind) for behind in range(1, SEQ_BANDS)]
-
-
-def caption_back(masked_pair, behind):
-    return from_behind(masked_pair.astype(jnp.bfloat16), "band", -behind).astype(masked_pair.dtype)
-
-
-def log_sum(scores):
-    row_max = jnp.max(scores, axis=-1, keepdims=True)
-    return row_max + jnp.log(jnp.sum(jnp.exp(scores - row_max), axis=-1, keepdims=True))
-
-
-def pair_scores(queries, key_block):
-    return jnp.einsum("qhd,khd->hqk", queries, key_block, preferred_element_type=jnp.float32)
-
-
-def pair_zero(queries, key_block):
-    return jnp.zeros((queries.shape[1], queries.shape[0], key_block.shape[0]), jnp.float32)
-
-
-def mix_values(weights, values):
-    return jnp.einsum("hqk,khd->qhd", weights, values, preferred_element_type=jnp.float32)
-
-
-def mix_nothing(weights, values):
-    return jnp.zeros((weights.shape[1], values.shape[1], values.shape[2]), jnp.float32)
-
-
-def spread_back(weights, rows_side):
-    return jnp.einsum("hqk,qhd->khd", weights, rows_side, preferred_element_type=jnp.float32)
-
-
-def spread_none(weights, rows_side):
-    return jnp.zeros((weights.shape[2], rows_side.shape[1], rows_side.shape[2]), jnp.float32)
-
-
-def masked_scores(queries, key_list, offset):
-    score_scale = HEAD_DIM ** (-0.5)
-    band_rows = queries.shape[0]
-    row_ids = lax.broadcasted_iota(jnp.int32, (band_rows, band_rows), 0)
-    col_ids = lax.broadcasted_iota(jnp.int32, (band_rows, band_rows), 1)
-    own_scores = pair_scores(queries, key_list[0]) * score_scale
-    blocks = [jnp.where((col_ids <= row_ids)[None], own_scores, NEG)]
-    for behind in range(1, SEQ_BANDS):
-        valid = behind <= offset
-        far_block = lax.cond(valid, pair_scores, pair_zero, queries, key_list[behind]) * score_scale
-        blocks.append(jnp.where(valid, far_block, NEG))
-    return jnp.concatenate(blocks, axis=2)
-
-
-def self_forward(queries, key_list, value_list, offset):
-    band_rows = queries.shape[0]
-    scores = masked_scores(queries, key_list, offset)
-    log_total = log_sum(scores)
-    weights = jnp.exp(scores - log_total).astype(jnp.bfloat16)
-    result = mix_values(weights[:, :, :band_rows], value_list[0])
-    for behind in range(1, SEQ_BANDS):
-        weight_block = weights[:, :, behind * band_rows : (behind + 1) * band_rows]
-        result = result + lax.cond(
-            behind <= offset, mix_values, mix_nothing, weight_block, value_list[behind]
+def heads_of(block):
+    lane = lax.broadcasted_iota(jnp.int32, block.shape, 1) // HEAD_DIM
+    return [
+        block * (lane == one).astype(jnp.float32).astype(block.dtype) for one in range(LANES // HEAD_DIM)
+    ]
+
+
+def shifted(scores, causal, behind):
+    if not causal or behind > 0:
+        return scores
+    key_ids = lax.broadcasted_iota(jnp.int32, scores.shape, 0)
+    query_ids = lax.broadcasted_iota(jnp.int32, scores.shape, 1)
+    return jnp.where(key_ids <= query_ids, scores, NEG)
+
+
+def attend_body(reach, causal, q_ref, k_ref, v_ref, out_ref, total_ref):
+    scale = HEAD_DIM**-0.5
+    values_t = [v_ref[behind].T for behind in range(reach)]
+    outs = []
+    for one, q_one in enumerate(heads_of(q_ref[...])):
+        scores = [shifted(matmul_t(k_ref[behind], q_one) * scale, causal, behind) for behind in range(reach)]
+        top = jnp.max(scores[0], axis=0, keepdims=True)
+        for block in scores[1:]:
+            top = jnp.maximum(top, jnp.max(block, axis=0, keepdims=True))
+        raised = [jnp.exp(block - top) for block in scores]
+        total = jnp.sum(raised[0], axis=0, keepdims=True)
+        for block in raised[1:]:
+            total = total + jnp.sum(block, axis=0, keepdims=True)
+        share = 1.0 / total
+        mixed = None
+        for behind in range(reach):
+            part = matmul(values_t[behind], (raised[behind] * share).astype(jnp.bfloat16))
+            mixed = part if mixed is None else mixed + part
+        outs.append(mixed[one * HEAD_DIM : (one + 1) * HEAD_DIM])
+        total_ref[one : one + 1, :] = top + jnp.log(total)
+    out_ref[...] = jnp.concatenate(outs, axis=0).T.astype(jnp.bfloat16)
+
+
+def attend_back_body(reach, causal, q_ref, k_ref, v_ref, total_ref, g_ref, dq_ref, dk_ref, dv_ref):
+    scale = HEAD_DIM**-0.5
+    keys_t = [k_ref[behind].T for behind in range(reach)]
+    q_heads, g_heads = heads_of(q_ref[...]), heads_of(g_ref[...])
+    query_grads = []
+    key_grads, value_grads = [None] * reach, [None] * reach
+    for one in range(len(q_heads)):
+        q_one, g_one = q_heads[one], g_heads[one]
+        log_total = total_ref[one : one + 1, :]
+        probs, grads, centre = [], [], None
+        for behind in range(reach):
+            scores = shifted(matmul_t(k_ref[behind], q_one) * scale, causal, behind)
+            probs.append(jnp.exp(scores - log_total))
+            grads.append(matmul_t(v_ref[behind], g_one))
+            part = jnp.sum(grads[-1] * probs[-1], axis=0, keepdims=True)
+            centre = part if centre is None else centre + part
+        query_grad = None
+        for behind in range(reach):
+            grad_scores = (probs[behind] * (grads[behind] - centre)).astype(jnp.bfloat16)
+            part = matmul(keys_t[behind], grad_scores)
+            query_grad = part if query_grad is None else query_grad + part
+            key_part = matmul(grad_scores, q_one)
+            value_part = matmul(probs[behind].astype(jnp.bfloat16), g_one)
+            key_grads[behind] = key_part if one == 0 else key_grads[behind] + key_part
+            value_grads[behind] = value_part if one == 0 else value_grads[behind] + value_part
+        query_grads.append(query_grad[one * HEAD_DIM : (one + 1) * HEAD_DIM])
+    dq_ref[...] = (jnp.concatenate(query_grads, axis=0).T * scale).astype(jnp.bfloat16)
+    for behind in range(dk_ref.shape[0]):
+        if behind < reach:
+            dk_ref[behind] = (key_grads[behind] * scale).astype(jnp.bfloat16)
+            dv_ref[behind] = value_grads[behind].astype(jnp.bfloat16)
+        else:
+            dk_ref[behind] = jnp.zeros(dk_ref.shape[1:], dk_ref.dtype)
+            dv_ref[behind] = jnp.zeros(dv_ref.shape[1:], dv_ref.dtype)
+
+
+def by_offset(body, causal, offset_ref, *refs):
+    reaches = refs[1].shape[0]
+    if reaches == 1:
+        body(1, causal, *refs)
+        return
+    offset = offset_ref[pl.program_id(0)]
+    for earlier_bands in range(reaches):
+        @pl.when(offset == earlier_bands)
+        def _():
+            body(earlier_bands + 1, causal, *refs)
+
+
+def attention_specs(queries, keys):
+    rows, reaches, key_rows = queries.shape[1], keys.shape[1], keys.shape[2]
+    row_spec = pl.BlockSpec((None, rows, LANES), lambda stream, pair: (stream, 0, pair))
+    key_spec = pl.BlockSpec((None, reaches, key_rows, LANES), lambda stream, pair: (stream, 0, 0, pair))
+    total_spec = pl.BlockSpec((None, None, 8, rows), lambda stream, pair: (stream, pair, 0, 0))
+    return row_spec, key_spec, total_spec
+
+
+def attention(queries, keys, values, offsets, causal):
+    streams, rows, width = queries.shape
+    row_spec, key_spec, total_spec = attention_specs(queries, keys)
+    return pl.pallas_call(
+        partial(by_offset, attend_body, causal),
+        grid=(streams, width // LANES),
+        in_specs=[pl.BlockSpec(memory_space=pltpu.SMEM), row_spec, key_spec, key_spec],
+        out_specs=[row_spec, total_spec],
+        out_shape=[
+            jax.ShapeDtypeStruct(queries.shape, jnp.bfloat16),
+            jax.ShapeDtypeStruct((streams, width // LANES, 8, rows), jnp.float32),
+        ],
+        name="attend",
+    )(offsets, queries, keys, values)
+
+
+def attention_back(queries, keys, values, offsets, totals, grad_out, causal):
+    streams, rows, width = queries.shape
+    row_spec, key_spec, total_spec = attention_specs(queries, keys)
+    return pl.pallas_call(
+        partial(by_offset, attend_back_body, causal),
+        grid=(streams, width // LANES),
+        in_specs=[pl.BlockSpec(memory_space=pltpu.SMEM), row_spec, key_spec, key_spec, total_spec, row_spec],
+        out_specs=[row_spec, key_spec, key_spec],
+        out_shape=[
+            jax.ShapeDtypeStruct(queries.shape, jnp.bfloat16),
+            jax.ShapeDtypeStruct(keys.shape, jnp.bfloat16),
+            jax.ShapeDtypeStruct(keys.shape, jnp.bfloat16),
+        ],
+        name="attend_back",
+    )(offsets, queries, keys, values, totals, grad_out)
+
+
+def swap_kernel(count, *refs):
+    sources, targets = refs[:count], refs[count : 2 * count]
+    send_sem, recv_sem = refs[2 * count :]
+    band, head = lax.axis_index("band"), lax.axis_index("head")
+    barrier = pltpu.get_barrier_semaphore()
+    pl.semaphore_signal(barrier, inc=1, device_id=(band, 1 - head), device_id_type=MESH)
+    pl.semaphore_wait(barrier, 1)
+    copies = [
+        pltpu.make_async_remote_copy(
+            sources[one], targets[one], send_sem.at[one], recv_sem.at[one],
+            device_id=(band, 1 - head), device_id_type=MESH,
         )
-    return (result.astype(jnp.bfloat16), log_total)
-
-
-def self_backward(queries, key_list, value_list, offset, log_total, grad_out):
-    score_scale = HEAD_DIM ** (-0.5)
-    band_rows = queries.shape[0]
-    probs_full = jnp.exp(masked_scores(queries, key_list, offset) - log_total)
-    probs_low = probs_full.astype(jnp.bfloat16)
-    grad_blocks = [pair_scores(grad_out, value_list[0])]
-    for behind in range(1, SEQ_BANDS):
-        grad_blocks.append(
-            lax.cond(behind <= offset, pair_scores, pair_zero, grad_out, value_list[behind])
-        )
-    grad_probs = jnp.concatenate(grad_blocks, axis=2)
-    centred = grad_probs - jnp.sum(grad_probs * probs_full, axis=-1, keepdims=True)
-    grad_scores = (probs_full * centred).astype(jnp.bfloat16)
-    grad_query = mix_values(grad_scores[:, :, :band_rows], key_list[0])
-    key_grads = [spread_back(grad_scores[:, :, :band_rows], queries) * score_scale]
-    value_grads = [spread_back(probs_low[:, :, :band_rows], grad_out)]
-    for behind in range(1, SEQ_BANDS):
-        valid = behind <= offset
-        score_block = grad_scores[:, :, behind * band_rows : (behind + 1) * band_rows]
-        prob_block = probs_low[:, :, behind * band_rows : (behind + 1) * band_rows]
-        grad_query = grad_query + lax.cond(
-            valid, mix_values, mix_nothing, score_block, key_list[behind]
-        )
-        key_grads.append(
-            lax.cond(valid, spread_back, spread_none, score_block, queries) * score_scale
-        )
-        value_grads.append(lax.cond(valid, spread_back, spread_none, prob_block, grad_out))
-    return (grad_query * score_scale, key_grads, value_grads)
+        for one in range(count)
+    ]
+    for copy in copies:
+        copy.start()
+    for copy in copies:
+        copy.wait()
+
+
+def swapped(collective_id, *arrays):
+    vmem = pl.BlockSpec(memory_space=pltpu.VMEM)
+    return pl.pallas_call(
+        partial(swap_kernel, len(arrays)),
+        out_shape=[jax.ShapeDtypeStruct(array.shape, array.dtype) for array in arrays],
+        in_specs=[vmem] * len(arrays),
+        out_specs=[vmem] * len(arrays),
+        scratch_shapes=[pltpu.SemaphoreType.DMA((len(arrays),)), pltpu.SemaphoreType.DMA((len(arrays),))],
+        compiler_params=pltpu.CompilerParams(collective_id=collective_id, has_side_effects=True),
+        name="swap_heads",
+    )(*arrays)
+
+
+def total_kernel(dims, in_ref, out_ref, *scratch):
+    slots, (send_sem, recv_sem) = scratch[:4], scratch[4:]
+    band, place = place_of(dims)
+    head = lax.axis_index("head")
+    strides = strides_of(dims)
+    lines = [
+        (dims[axis], place[axis], lambda at, axis=axis: (band + (at - place[axis]) * strides[axis], head))
+        for axis in (2, 1, 0)
+    ]
+    lines.append((2, head, lambda at: (band, at)))
+    barrier = pltpu.get_barrier_semaphore()
+    for size, mine, device in lines:
+        for shift in range(1, size):
+            pl.semaphore_signal(barrier, inc=1, device_id=device((mine + shift) % size), device_id_type=MESH)
+    pl.semaphore_wait(barrier, sum(size - 1 for size, _, _ in lines))
+    out_ref[...] = in_ref[...]
+    rows = in_ref.shape[0]
+    for line, (size, mine, device) in enumerate(lines):
+        part = pl.ds(0, rows) if line < 3 else pl.ds(rows - 8, 8)
+        slots[line][mine] = out_ref[part, :]
+
+        def copy(shift):
+            return pltpu.make_async_remote_copy(
+                slots[line].at[mine], slots[line].at[mine], send_sem.at[line, shift - 1], recv_sem.at[line, shift - 1],
+                device_id=device((mine + shift) % size), device_id_type=MESH,
+            )
+
+        def incoming(shift):
+            there = (mine + size - shift) % size
+            return pltpu.make_async_remote_copy(
+                slots[line].at[there], slots[line].at[there], send_sem.at[line, shift - 1], recv_sem.at[line, shift - 1],
+                device_id=device(there), device_id_type=MESH,
+            )
+
+        for shift in range(1, size):
+            copy(shift).start()
+        for shift in range(1, size):
+            incoming(shift).wait_recv()
+        total = slots[line][0]
+        for at in range(1, size):
+            total = total + slots[line][at]
+        out_ref[part, :] = total
+        for shift in range(1, size):
+            copy(shift).wait_send()
+
+
+def mesh_total(bands, tile, collective_id):
+    dims = band_dims(bands)
+    longest = max(*dims, 2)
+    vmem = pl.BlockSpec(memory_space=pltpu.VMEM)
+    rows = tile.shape[0]
+    return pl.pallas_call(
+        partial(total_kernel, dims),
+        out_shape=jax.ShapeDtypeStruct(tile.shape, tile.dtype),
+        in_specs=[vmem],
+        out_specs=vmem,
+        scratch_shapes=[
+            *(pltpu.VMEM((dims[axis], rows, LANES), tile.dtype) for axis in (2, 1, 0)),
+            pltpu.VMEM((2, 8, LANES), tile.dtype),
+            pltpu.SemaphoreType.DMA((4, longest - 1)),
+            pltpu.SemaphoreType.DMA((4, longest - 1)),
+        ],
+        compiler_params=pltpu.CompilerParams(collective_id=collective_id, has_side_effects=True),
+        name="mesh_total",
+    )(tile)
+
+
+def head_total(partials, collective_id):
+    low = partials.astype(jnp.bfloat16)
+    (there,) = swapped(collective_id, low)
+    return low.astype(jnp.float32) + there.astype(jnp.float32)
 
 
 def adamw_update(weight, moment_one, moment_two, gradient, step_rate, decay_rate):
@@ -747,208 +872,150 @@
     streams, band_rows, model_width = tokens.shape
     row_count = streams * band_rows
     text_rows = text_states.shape[1]
-    proj_low = proj_master.astype(jnp.bfloat16)
-    out_low = out_master.astype(jnp.bfloat16)
-    mlp_low = mlp_master.astype(jnp.bfloat16)
-    gain_low = gain_master.astype(jnp.bfloat16)
-    bands = lax.axis_size("band")
-    shard_rows, width = proj_low.shape[1:]
-    chunks = mlp_low.shape[2] // width
-    mlp_cut = mlp_low.reshape(2, shard_rows, chunks, width).transpose(0, 2, 1, 3)
-    shard = jnp.concatenate([proj_low, out_low, mlp_cut.reshape(2 * chunks, shard_rows, width)])
-    gain_tile = jnp.pad(gain_low.astype(jnp.float32), ((0, 5), (0, 128 - shard_rows)))
-    gathered, gain_tiles = gather_weights(bands, shard, gain_tile, None, 1)
-    gathered = gathered.reshape(shard.shape[0], model_width, width)
-    proj_w, out_w = gathered[:6], gathered[6:8]
-    mlp_w = gathered[8:].reshape(2, chunks, model_width, width).transpose(0, 2, 1, 3)
-    mlp_w = mlp_w.reshape(2, model_width, chunks * width)
-    gains = gain_tiles.reshape(bands, 8, 128)[:, :3, :shard_rows].transpose(1, 0, 2).reshape(3, model_width)
-    local_width = proj_w.shape[2]
-    local_heads = local_width // HEAD_DIM
-    score_scale = HEAD_DIM ** (-0.5)
-    head_shape = (streams, band_rows, local_heads, HEAD_DIM)
-    text_shape = (streams, text_rows, local_heads, HEAD_DIM)
+    bands, head = lax.axis_size("band"), lax.axis_index("head")
+    shard_rows, width = proj_master.shape[1:]
+    chunks = mlp_master.shape[2] // width
+    mlp_cut = mlp_master.reshape(2, shard_rows, chunks, width).transpose(0, 2, 1, 3)
+    shard = jnp.concatenate(
+        [proj_master, out_master, mlp_cut.reshape(2 * chunks, shard_rows, width)]
+    ).astype(jnp.bfloat16)
+    gain_low = gain_master.astype(jnp.bfloat16).astype(jnp.float32)
+    gain_tile = jnp.pad(gain_low, ((0, 5), (0, LANES - shard_rows)))
+    both = jnp.concatenate([tokens, text_states], axis=1)
+    context = lax.dynamic_index_in_dim(both, head, 0, keepdims=False)
+    gathered, gain_tiles, passed = gather_weights(bands, shard, gain_tile, context, 1)
+    weights = gathered.reshape(shard.shape[0], model_width, width)
+    w_query, w_key, w_value, w_cross, w_text_key, w_text_value, w_self_out, w_cross_out = (
+        weights[at] for at in range(8)
+    )
+    w_up = [weights[8 + at] for at in range(chunks)]
+    w_down = [weights[8 + chunks + at] for at in range(chunks)]
+    gains = gain_tiles.reshape(bands, 8, LANES)[:, :3, :shard_rows].transpose(1, 0, 2).reshape(3, model_width)
+
     offsets = earlier[:, 0]
+    reach_ids = jnp.arange(SEQ_BANDS)
+    within = reach_ids[None, :] <= offsets[:, None]
     inputs = tokens.astype(jnp.float32).reshape(row_count, model_width)
-    normed_one = norm_rows(inputs, gains[0]).astype(jnp.bfloat16)
-    queries = matmul(normed_one, proj_w[0]).astype(jnp.bfloat16).reshape(head_shape)
-    key_rows = matmul(normed_one, proj_w[1]).astype(jnp.bfloat16)
-    value_rows = matmul(normed_one, proj_w[2]).astype(jnp.bfloat16)
-    own_pair = jnp.stack([key_rows.reshape(head_shape), value_rows.reshape(head_shape)])
-    pair_list = [own_pair] + earlier_bands(own_pair)
-    attended_list = []
-    total_list = []
-    for stream in range(streams):
-        offset = earlier[stream, 0]
-        result, log_total = self_forward(
-            queries[stream],
-            [neighbour[0, stream] for neighbour in pair_list],
-            [neighbour[1, stream] for neighbour in pair_list],
-            offset,
-        )
-        attended_list.append(result)
-        total_list.append(log_total)
-    attended = jnp.stack(attended_list).reshape(row_count, local_width)
-    hidden_one = inputs + head_total(matmul_t(attended, out_w[0]))
+    reached = jnp.concatenate([tokens[:, None], passed[:, :, :band_rows]], axis=1)
+    normed_all = jnp.where(
+        within[:, :, None, None], norm_rows(reached.astype(jnp.float32), gains[0]), 0.0
+    ).astype(jnp.bfloat16)
+    normed_one = normed_all[:, 0].reshape(row_count, model_width)
+    normed_all = normed_all.reshape(SEQ_BANDS * row_count, model_width)
+    row_shape = (streams, band_rows, width)
+    reach_shape = (streams, SEQ_BANDS, band_rows, width)
+    text_shape = (streams, 1, text_rows, width)
+    queries = matmul(normed_one, w_query).astype(jnp.bfloat16).reshape(row_shape)
+    keys = matmul(normed_all, w_key).astype(jnp.bfloat16).reshape(reach_shape)
+    values = matmul(normed_all, w_value).astype(jnp.bfloat16).reshape(reach_shape)
+    attended, self_totals = attention(queries, keys, values, offsets, True)
+    attended = attended.reshape(row_count, width)
+    hidden_one = inputs + head_total(matmul_t(attended, w_self_out), 3)
     normed_two = norm_rows(hidden_one, gains[1]).astype(jnp.bfloat16)
-    cross_queries = matmul(normed_two, proj_w[3]).astype(jnp.bfloat16).reshape(head_shape)
-    text_flat = text_states.reshape(streams * text_rows, model_width)
-    slot_keys = matmul(text_flat, proj_w[4]).astype(jnp.bfloat16).reshape(text_shape)
-    slot_values = matmul(text_flat, proj_w[5]).astype(jnp.bfloat16).reshape(text_shape)
-    caption_pair = jnp.stack([slot_keys, slot_values])
-    moved_list = caption_from_first(caption_pair)
-    chosen = caption_pair
+    cross_queries = matmul(normed_two, w_cross).astype(jnp.bfloat16).reshape(row_shape)
+    caption = text_states
     for behind in range(1, SEQ_BANDS):
-        chosen = jnp.where(
-            (offsets == behind)[None, :, None, None, None], moved_list[behind - 1], chosen
-        )
-    cross_keys = chosen[0]
-    cross_values = chosen[1]
-    cross_scores = (
-        jnp.einsum("sqhd,skhd->shqk", cross_queries, cross_keys, preferred_element_type=jnp.float32)
-        * score_scale
-    )
-    cross_probs = jnp.exp(cross_scores - log_sum(cross_scores))
-    cross_low = cross_probs.astype(jnp.bfloat16)
-    crossed = (
-        jnp.einsum("shqk,skhd->sqhd", cross_low, cross_values, preferred_element_type=jnp.float32)
-        .astype(jnp.bfloat16)
-        .reshape(row_count, local_width)
-    )
-    hidden_two = hidden_one + head_total(matmul_t(crossed, out_w[1]))
+        caption = jnp.where((offsets == behind)[:, None, None], passed[:, behind - 1, band_rows:], caption)
+    caption = caption.reshape(streams * text_rows, model_width)
+    cross_keys = matmul(caption, w_text_key).astype(jnp.bfloat16).reshape(text_shape)
+    cross_values = matmul(caption, w_text_value).astype(jnp.bfloat16).reshape(text_shape)
+    crossed, cross_totals = attention(cross_queries, cross_keys, cross_values, offsets, False)
+    crossed = crossed.reshape(row_count, width)
+    hidden_two = hidden_one + head_total(matmul_t(crossed, w_cross_out), 4)
     normed_three = norm_rows(hidden_two, gains[2]).astype(jnp.bfloat16)
-    before = matmul(normed_three, mlp_w[0])
-    activated = jax.nn.gelu(before, approximate=False).astype(jnp.bfloat16)
-    block_out = (
-        (hidden_two + head_total(matmul_t(activated, mlp_w[1])))
-        .astype(jnp.bfloat16)
-        .reshape(streams, band_rows, model_width)
-    )
-    incoming = cotangent.astype(jnp.float32).reshape(row_count, model_width)
+    before = [matmul(normed_three, part) for part in w_up]
+    gelu = partial(jax.nn.gelu, approximate=False)
+    activated = [gelu(part).astype(jnp.bfloat16) for part in before]
+    mlp_out = sum(matmul_t(part, weight) for part, weight in zip(activated, w_down))
+    block_out = (hidden_two + head_total(mlp_out, 5)).astype(jnp.bfloat16).reshape(tokens.shape)
+
     incoming_low = cotangent.reshape(row_count, model_width)
-    grad_down = inner_t(incoming_low, activated)
-    grad_act = matmul(incoming_low, mlp_w[1])
-    _, gelu_pull = jax.vjp(partial(jax.nn.gelu, approximate=False), before)
-    grad_before = gelu_pull(grad_act)[0].astype(jnp.bfloat16)
-    grad_up = inner_t(normed_three, grad_before)
-    mlp_grad_local = jnp.stack([grad_up, grad_down])
-    grad_normed_three = head_total(matmul_t(grad_before, mlp_w[0]))
+    incoming = incoming_low.astype(jnp.float32)
+    grad_down = [inner_t(incoming_low, part) for part in activated]
+    grad_before = []
+    for part, weight in zip(before, w_down):
+        _, gelu_pull = jax.vjp(gelu, part)
+        grad_before.append(gelu_pull(matmul(incoming_low, weight))[0].astype(jnp.bfloat16))
+    grad_up = [inner_t(normed_three, part) for part in grad_before]
+    grad_normed_three = head_total(sum(matmul_t(part, weight) for part, weight in zip(grad_before, w_up)), 6)
     _, pull_three = jax.vjp(norm_rows, hidden_two, gains[2])
     back_two, gain_grad_three = pull_three(grad_normed_three)
     grad_two = incoming + back_two
     grad_two_low = grad_two.astype(jnp.bfloat16)
     grad_cross_out = inner_t(grad_two_low, crossed)
-    grad_crossed = matmul(grad_two_low, out_w[1]).astype(jnp.bfloat16).reshape(head_shape)
-    cross_dp = jnp.einsum(
-        "sqhd,skhd->shqk", grad_crossed, cross_values, preferred_element_type=jnp.float32
-    )
-    cross_ds = (
-        cross_probs * (cross_dp - jnp.sum(cross_dp * cross_probs, axis=-1, keepdims=True))
-    ).astype(jnp.bfloat16)
-    grad_cq = (
-        (
-            jnp.einsum("shqk,skhd->sqhd", cross_ds, cross_keys, preferred_element_type=jnp.float32)
-            * score_scale
-        )
-        .astype(jnp.bfloat16)
-        .reshape(row_count, local_width)
-    )
-    key_part = (
-        jnp.einsum("shqk,sqhd->skhd", cross_ds, cross_queries, preferred_element_type=jnp.float32)
-        * score_scale
-    )
-    value_part = jnp.einsum(
-        "shqk,sqhd->skhd", cross_low, grad_crossed, preferred_element_type=jnp.float32
-    )
-    grad_caption = jnp.stack([key_part, value_part])
-    caption_total = jnp.where((offsets == 0)[None, :, None, None, None], grad_caption, 0.0)
-    for behind in range(1, SEQ_BANDS):
-        masked_pair = jnp.where((offsets == behind)[None, :, None, None, None], grad_caption, 0.0)
-        caption_total = caption_total + caption_back(masked_pair, behind)
-    grad_ck = caption_total[0].astype(jnp.bfloat16).reshape(streams * text_rows, local_width)
-    grad_cv = caption_total[1].astype(jnp.bfloat16).reshape(streams * text_rows, local_width)
-    text_partial = matmul_t(grad_ck, proj_w[4]) + matmul_t(grad_cv, proj_w[5])
-    grad_normed_two, grad_text = head_total((matmul_t(grad_cq, proj_w[3]), text_partial))
+    grad_crossed = matmul(grad_two_low, w_cross_out).astype(jnp.bfloat16).reshape(row_shape)
+    grad_cq, grad_ck, grad_cv = attention_back(
+        cross_queries, cross_keys, cross_values, offsets, cross_totals, grad_crossed, False
+    )
+    grad_cq = grad_cq.reshape(row_count, width)
+    grad_ck = grad_ck.reshape(streams * text_rows, width)
+    grad_cv = grad_cv.reshape(streams * text_rows, width)
+    text_part = (matmul_t(grad_ck, w_text_key) + matmul_t(grad_cv, w_text_value)).astype(jnp.bfloat16)
+    text_part = text_part.reshape(text_states.shape)
+    grad_normed_two = head_total(matmul_t(grad_cq, w_cross), 7)
     _, pull_two = jax.vjp(norm_rows, hidden_one, gains[1])
     back_one, gain_grad_two = pull_two(grad_normed_two)
     grad_one = grad_two + back_one
     grad_one_low = grad_one.astype(jnp.bfloat16)
     grad_self_out = inner_t(grad_one_low, attended)
-    grad_attended = matmul(grad_one_low, out_w[0]).astype(jnp.bfloat16).reshape(head_shape)
-    query_grads = []
-    key_grads = []
-    value_grads = []
-    for stream in range(streams):
-        offset = earlier[stream, 0]
-        grad_query, key_blocks, value_blocks = self_backward(
-            queries[stream],
-            [neighbour[0, stream] for neighbour in pair_list],
-            [neighbour[1, stream] for neighbour in pair_list],
-            offset,
-            total_list[stream],
-            grad_attended[stream],
-        )
-        query_grads.append(grad_query)
-        key_grads.append(key_blocks)
-        value_grads.append(value_blocks)
-    grad_pairs = [
-        jnp.stack(
-            [
-                jnp.stack([key_grads[stream][behind] for stream in range(streams)]),
-                jnp.stack([value_grads[stream][behind] for stream in range(streams)]),
-            ]
-        )
-        for behind in range(SEQ_BANDS)
-    ]
-    pair_total = grad_pairs[0]
-    for behind in range(1, SEQ_BANDS):
-        pair_total = pair_total + from_behind(
-            grad_pairs[behind].astype(jnp.bfloat16), "band", -behind
-        ).astype(jnp.float32)
-    grad_queries = jnp.stack(query_grads).astype(jnp.bfloat16).reshape(row_count, local_width)
-    grad_keys = pair_total[0].astype(jnp.bfloat16).reshape(row_count, local_width)
-    grad_values = pair_total[1].astype(jnp.bfloat16).reshape(row_count, local_width)
-    proj_grad_local = jnp.stack(
+    grad_attended = matmul(grad_one_low, w_self_out).astype(jnp.bfloat16).reshape(row_shape)
+    grad_queries, grad_keys, grad_values = attention_back(
+        queries, keys, values, offsets, self_totals, grad_attended, True
+    )
+    grad_queries = grad_queries.reshape(row_count, width)
+    reach_part = matmul_t(grad_keys.reshape(-1, width), w_key) + matmul_t(grad_values.reshape(-1, width), w_value)
+    reach_part = reach_part.reshape(streams, SEQ_BANDS, band_rows, model_width)
+    own_part = matmul_t(grad_queries, w_query).reshape(tokens.shape) + reach_part[:, 0]
+    own_text = jnp.where((offsets == 0)[:, None, None], text_part, 0).astype(jnp.bfloat16)
+    sent_text = jnp.where(
+        (offsets[:, None] == reach_ids[None, 1:])[:, :, None, None], text_part[:, None], 0
+    ).astype(jnp.bfloat16)
+    own_back = jnp.concatenate([own_part.astype(jnp.bfloat16), own_text], axis=1)
+    sent_back = jnp.concatenate([reach_part[:, 1:].astype(jnp.bfloat16), sent_text], axis=2)
+    mine = lax.dynamic_index_in_dim(sent_back, head, 0, keepdims=False)
+    other = lax.dynamic_index_in_dim(sent_back, 1 - head, 0, keepdims=False)
+    own_there, mine_there = swapped(8, own_back, other)
+    own_back = own_back.astype(jnp.float32) + own_there.astype(jnp.float32)
+    returned = (mine.astype(jnp.float32) + mine_there.astype(jnp.float32)).astype(jnp.bfloat16)
+
+    flat = lambda part: part.reshape(-1, width)
+    grads = jnp.stack(
         [
-            inner_t(normed_one, grad_queries),
-            inner_t(normed_one, grad_keys),
-            inner_t(normed_one, grad_values),
-            inner_t(normed_two, grad_cq),
-            inner_t(text_flat, grad_ck),
-            inner_t(text_flat, grad_cv),
+            part.astype(jnp.bfloat16)
+            for part in (
+                inner_t(normed_one, grad_queries),
+                inner_t(normed_all, flat(grad_keys)),
+                inner_t(normed_all, flat(grad_values)),
+                inner_t(normed_two, grad_cq),
+                inner_t(caption, grad_ck),
+                inner_t(caption, grad_cv),
+                grad_self_out,
+                grad_cross_out,
+                *grad_up,
+                *grad_down,
+            )
         ]
     )
-    norm_partial = (
-        matmul_t(grad_queries, proj_w[0])
-        + matmul_t(grad_keys, proj_w[1])
-        + matmul_t(grad_values, proj_w[2])
-    )
-    grad_normed_one = head_total(norm_partial)
+    summed, came_back = reduce_grads(bands, grads, returned, 2)
+    came_low = came_back.astype(jnp.bfloat16)
+    (came_there,) = swapped(9, came_low)
+    came_both = jnp.stack([jnp.where(head == 0, came_low, came_there), jnp.where(head == 0, came_there, came_low)])
+    back_all = own_back + came_both.astype(jnp.float32)
+    grad_normed_one = back_all[:, :band_rows].reshape(row_count, model_width)
+    grad_text = back_all[:, band_rows:]
     _, pull_one = jax.vjp(norm_rows, inputs, gains[0])
     back_zero, gain_grad_one = pull_one(grad_normed_one)
-    grad_tokens = (grad_one + back_zero).reshape(streams, band_rows, model_width)
-    out_grad_local = jnp.stack([grad_self_out, grad_cross_out])
-    gain_grad_local = jnp.stack([gain_grad_one, gain_grad_two, gain_grad_three])
-    mlp_parts = mlp_grad_local.astype(jnp.bfloat16).reshape(2, model_width, chunks, width).transpose(0, 2, 1, 3)
-    grads = jnp.concatenate(
-        [
-            proj_grad_local.astype(jnp.bfloat16),
-            out_grad_local.astype(jnp.bfloat16),
-            mlp_parts.reshape(2 * chunks, model_width, width),
-        ]
-    )
-    (summed,) = reduce_grads(bands, grads, None, 2)
+    grad_tokens = (grad_one + back_zero).reshape(tokens.shape)
+
+    squares = jnp.sum(summed * summed)
+    gain_rows = jnp.stack([gain_grad_one, gain_grad_two, gain_grad_three]).reshape(-1, LANES)
+    tile = jnp.concatenate([gain_rows, jnp.full((8, LANES), squares)])
+    tile = mesh_total(bands, tile, 10)
+    gain_total = tile[:-8].reshape(3, model_width)
+    grad_norm = jnp.sqrt(tile[-1, 0] + jnp.sum(gain_total * gain_total))
+    gain_grad = lax.dynamic_slice_in_dim(gain_total, lax.axis_index("band") * shard_rows, shard_rows, 1)
     proj_grad, out_grad = summed[:6], summed[6:8]
-    mlp_grad = summed[8:].reshape(2, chunks, shard_rows, width).transpose(0, 2, 1, 3)
-    mlp_grad = mlp_grad.reshape(2, shard_rows, chunks * width)
-    gain_grad = lax.psum_scatter(gain_grad_local, "band", scatter_dimension=1, tiled=True)
-    local_squares = (
-        jnp.sum(proj_grad * proj_grad)
-        + jnp.sum(out_grad * out_grad)
-        + jnp.sum(mlp_grad * mlp_grad)
-        + 0.5 * jnp.sum(gain_grad * gain_grad)
-    )
-    grad_norm = jnp.sqrt(lax.psum(local_squares, ("band", "head")))
+    mlp_grad = summed[8:].reshape(2, chunks, shard_rows, width).transpose(0, 2, 1, 3).reshape(mlp_master.shape)
     factor = jnp.minimum(1.0, CLIP / grad_norm)
     matrix_rate = 2.0 * D ** (-0.5)
     new_proj = adamw_update(
@@ -959,11 +1026,10 @@
     new_gain = adamw_update(
         gain_master, gain_first, gain_second, gain_grad * factor, GAIN_RATE, 0.0
     )
-    grad_text_out = grad_text.reshape(streams, text_rows, model_width)
     return (
         block_out,
         grad_tokens,
-        grad_text_out,
+        grad_text,
         grad_norm,
         new_proj[0],
         new_proj[1],

time: 1140 us -> 762 us (0.67)
  waiting for transfers between devices: 230 us -> 0 us
  Pallas kernels: 342 us -> 520 us
  local copies, waits for them, and re-layouts: 167 us -> 59.6 us
  starting transfers between devices: 93.7 us -> 0 us
  other arithmetic: 131 us -> 59.7 us
  blocking collectives: 36.8 us -> 0 us
  between operations: 25.3 us -> 4.68 us
    ppermute x12 -> x0, waiting for transfers between devices: 132 us -> none  [from_behind(): return lax.ppermute(x, axis, pairs)]
    ppermute x12 -> x0, starting transfers between devices: 93.3 us -> none  [from_behind(): return lax.ppermute(x, axis, pairs)]
    pallas_call x0 -> x12, Pallas kernels: none -> 92.2 us  [the longest x7 39.9 us: swapped(): pl.pallas_call(partial(swap_kernel, len(arrays)), out_shape=[jax.ShapeDty...]
    unnamed x7 -> x0, waiting for transfers between devices: 71.3 us -> none
    pallas_call x1, Pallas kernels: 163 us -> 207 us  [gather_weights(): pl.pallas_call(partial(gather_kernel, dims, has_context), out_shape=out_s...]
    pallas_call x1, Pallas kernels: 179 us -> 221 us  [reduce_grads(): pl.pallas_call(partial(reduce_kernel, dims, has_context), out_shape=out_s...]
    psum x1 -> x0, blocking collectives: 36.8 us -> none  [local(): grad_norm = jnp.sqrt(lax.psum(local_squares, ('band', 'head')))]
    unnamed x414 -> x253, local copies, waits for them, and re-layouts: 67.7 us -> 35.6 us
  transfers between devices with their start and end apart: 18 -> 0, of which waited for: 12 -> 0; matrix products, arithmetic and copies ran while one was open for 12% -> 0% of each run, Pallas kernels for 16% -> 0%
where the time goes in v2:
time: 762 us; the launch traced here: 751 us
  Pallas kernels  520 us (68%)
  matrix products  108 us (14%)
  other arithmetic  59.7 us (8%)
  local copies, waits for them, and re-layouts  59.6 us (8%)
    pallas_call x1, Pallas kernels, reduce_grads(): pl.pallas_call(partial(reduce_kernel, dims, has_context), out_shape=out_s...  221 us
    pallas_call x1, Pallas kernels, gather_weights(): pl.pallas_call(partial(gather_kernel, dims, has_context), out_shape=out_s...  207 us
    dot_general x16, matrix products, matmul(): return jnp.dot(former, latter, preferred_element_type=jnp.float32)  46 us
    pallas_call x7, Pallas kernels, swapped(): pl.pallas_call(partial(swap_kernel, len(arrays)), out_shape=[jax.ShapeDty...  39.9 us
    unnamed x253, local copies, waits for them, and re-layouts  35.6 us
    dot_general x16, matrix products, inner_t(): lax.dot_general(former, latter, (((0,), (0,)), ((), ())), preferred_eleme...  34.7 us
    dot_general x16, matrix products, matmul_t(): lax.dot_general(former, latter, (((1,), (1,)), ((), ())), preferred_eleme...  27.2 us
    pallas_call x2, Pallas kernels, attention_back(): pl.pallas_call(partial(by_offset, attend_back_body, causal), grid=(stream...  19.3 us

profile of v2, /device:TPU:0, one launch (start us, length us, event | category | flops | bytes accessed | tf_op | source)
XLA Modules:
  0.0 751.5 jit_solution(17337330137820575238)
XLA Ops:
  11.7 206.5 %gather_weights.1 = (bf16[16,4,2,2,64,512]{5,4,3,2,1,0:T(8,128)(2,1)}, f32[4,2,2,8,128]{4,3,2,1,0:T(8,128)}, bf16[2,3,384,1024]{3,2,1,0:T(8,128)(2,1)}) custom-call(bf16[16,64,512]{2,1,0:T(8,128)(2,1)} %pad_maximum_fusion.2.refs_0_, f32[8,128]{1,0:T(8,128)} %pad_convert_fusion.refs_1_, bf16[384,1024]{1,0:T(8,128)(2,1)} %fusion.61.refs_2_), custom_call_target="tpu_custom_call" | custom-call | tf_op jit(solution)/shard_map/gather_weights/pallas_call | solution.py:313
  219.4 1.9 fusion.63
  221.3 2.4 slice.148
  225.9 1.7 fusion.5
  231.4 4.9 fusion.85
  240.7 3.7 convolution_convert_fusion
  244.4 3.7 convolution_convert_fusion.1
  248.2 9.8 %attend.2 = (bf16[2,256,512]{2,1,0:T(8,128)(2,1)}, f32[2,4,8,256]{3,2,1,0:T(8,128)}) custom-call(s32[2]{0:T(128)} %bitcast.368, bf16[2,256,512]{2,1,0:T(8,128)(2,1)} %bitcast.332, bf16[2,4,256,512]{3,2,1,0:T(8,128)(2,1)} %bitcast.278, bf16[2,4,256,512]{3,2,1,0:T(8,128)(2,1)} %bitcast.276), custom_call_target="tpu_custom_call" | custom-call | tf_op jit(solution)/shard_map/attend/pallas_call | solution.py:707
  258.0 2.8 convolution_convert_fusion.18.refs_0_
  260.7 4.9 swap_heads.7
  265.7 2.0 fusion.84
  270.5 8.0 %attend.3 = (bf16[2,256,512]{2,1,0:T(8,128)(2,1)}, f32[2,4,8,256]{3,2,1,0:T(8,128)}) custom-call(s32[2]{0:T(128)} %bitcast.369, bf16[2,256,512]{2,1,0:T(8,128)(2,1)} %bitcast.328, bf16[2,1,128,512]{3,2,1,0:T(8,128)(2,1)} %bitcast.326, bf16[2,1,128,512]{3,2,1,0:T(8,128)(2,1)} %bitcast.324), custom_call_target="tpu_custom_call" | custom-call | tf_op jit(solution)/shard_map/attend/pallas_call | solution.py:707
  278.5 2.8 convolution_convert_fusion.17.refs_0_
  281.3 5.0 swap_heads.8
  290.0 5.5 multiply_convert_fusion.2
  296.5 1.8 convolution_convert_fusion.8
  298.3 1.7 fusion.31
  300.1 2.3 copy.57
  302.4 7.2 multiply_convert_fusion.4
  309.6 1.8 add_convert_fusion.5
  311.4 2.1 fusion.90
  313.5 1.7 fusion.29
  315.2 2.3 copy.55
  317.5 3.2 convolution_convert_fusion.10
  320.8 2.1 fusion.93
  322.8 5.5 multiply_convert_fusion.5
  328.3 1.8 add_convert_fusion.6
  330.1 2.1 fusion.89
  332.2 1.7 fusion.28
  333.9 2.3 copy.54
  336.2 3.2 convolution_convert_fusion.11
  340.9 6.6 multiply_convert_fusion.3
  348.4 1.7 convolution_convert_fusion.9
  351.8 1.8 add_convert_fusion.refs_0_
  353.6 5.0 swap_heads.10
  358.6 3.5 multiply_reduce_fusion.1
  364.1 1.7 add_convert_fusion.2.refs_0_
  365.8 1.7 fusion.30
  367.5 2.3 copy.56
  369.8 4.9 swap_heads.9
  374.7 4.6 fusion.78
  382.8 1.7 convolution_convert_fusion.12
  384.6 8.3 %attend_back.2 = (bf16[2,256,512]{2,1,0:T(8,128)(2,1)}, bf16[2,1,128,512]{3,2,1,0:T(8,128)(2,1)}, bf16[2,1,128,512]{3,2,1,0:T(8,128)(2,1)}) custom-call(s32[2]{0:T(128)} %bitcast.370, bf16[2,256,512]{2,1,0:T(8,128)(2,1)} %bitcast.329, bf16[2,1,128,512]{3,2,1,0:T(8,128)(2,1)} %bitcast.327, bf16[2,1,128,512]{3,2,1,0:T(8,128)(2,1)} %bitcast.325, ...), custom_call_target="tpu_custom_call" | custom-call | tf_op jit(solution)/shard_map/attend_back/pallas_call | solution.py:723
  392.9 3.2 convolution_convert_fusion.16.refs_0_
  398.0 1.9 convolution_convert_fusion.14
  404.2 4.9 swap_heads.11
  409.1 2.7 multiply_reduce_fusion.2
  416.5 11.0 %attend_back.3 = (bf16[2,256,512]{2,1,0:T(8,128)(2,1)}, bf16[2,4,256,512]{3,2,1,0:T(8,128)(2,1)}, bf16[2,4,256,512]{3,2,1,0:T(8,128)(2,1)}) custom-call(s32[2]{0:T(128)} %bitcast.371, bf16[2,256,512]{2,1,0:T(8,128)(2,1)} %bitcast.333, bf16[2,4,256,512]{3,2,1,0:T(8,128)(2,1)} %bitcast.279, bf16[2,4,256,512]{3,2,1,0:T(8,128)(2,1)} %bitcast.277, ...), custom_call_target="tpu_custom_call" | custom-call | tf_op jit(solution)/shard_map/attend_back/pallas_call | solution.py:723
  427.5 2.9 convolution_convert_fusion.15
  430.4 1.8 convolution_convert_fusion.13
  432.2 3.3 bitcast_convert_fusion.1
  435.5 3.3 bitcast_convert_fusion
  438.9 2.4 fusion.95
  441.3 2.4 convolution_add_fusion
  447.8 1.6 fusion.10.refs_1_
  449.5 10.9 %swap_heads.12 = (bf16[2,384,1024]{2,1,0:T(8,128)(2,1)}, bf16[3,384,1024]{2,1,0:T(8,128)(2,1)}) custom-call(bf16[2,384,1024]{2,1,0:T(8,128)(2,1)} %pad_maximum_fusion.1.refs_0_, bf16[3,384,1024]{2,1,0:T(8,128)(2,1)} %fusion.10.refs_1_), custom_call_target="tpu_custom_call" | custom-call | tf_op jit(solution)/shard_map/swap_heads/pallas_call | solution.py:759
  460.4 4.5 fusion.6.refs_1_
  483.2 220.9 %reduce_grads.1 = (f32[16,64,512]{2,1,0:T(8,128)}, f32[384,1024]{1,0:T(8,128)}) custom-call(bf16[16,4,2,2,64,512]{5,4,3,2,1,0:T(8,128)(2,1)} %constant_dynamic-update-slice_fusion.refs_0_, bf16[3,384,1024]{2,1,0:T(8,128)(2,1)} %fusion.6.refs_1_), custom_call_target="tpu_custom_call" | custom-call | tf_op jit(solution)/shard_map/reduce_grads/pallas_call | solution.py:575
  704.1 2.9 multiply_reduce_fusion
  707.9 4.3 swap_heads.13
  719.1 2.0 fusion.12
  722.4 15.3 %mesh_total.1 = f32[32,128]{1,0:T(8,128)} custom-call(f32[32,128]{1,0:T(8,128)} %concatenate.30.in_ref), custom_call_target="tpu_custom_call" | custom-call | tf_op jit(solution)/shard_map/mesh_total/pallas_call | solution.py:821
  745.0 1.8 multiply_subtract_fusion.1
  747.7 2.2 multiply_subtract_fusion
  (334 shorter events, 88.3 us)
Async XLA Ops:
  0.6 8.3 %copy-start.46 = (f32[2,64,2048]{2,1,0:T(8,128)S(1)}, f32[2,64,2048]{2,1,0:T(8,128)}, u32[]{:S(2)}) copy-start(f32[2,64,2048]{2,1,0:T(8,128)} %param.22) | copy-start | bytes 3145732
  219.4 6.5 copy-start.105
  221.3 16.2 %copy-start.10 = (bf16[2,128,1024]{2,1,0:T(8,128)(2,1)}, bf16[2,128,1024]{2,1,0:T(8,128)(2,1)S(1)}, u32[]{:S(2)}) copy-start(bf16[2,128,1024]{2,1,0:T(8,128)(2,1)S(1)} %fusion.63) | copy-start | bytes 1572868
  223.8 7.6 %copy-start.8 = (bf16[16,4,2,2,64,512]{5,4,3,2,1,0:T(8,128)(2,1)S(1)}, bf16[16,4,2,2,64,512]{5,4,3,2,1,0:T(8,128)(2,1)}, u32[]{:S(2)}) copy-start(bf16[16,4,2,2,64,512]{5,4,3,2,1,0:T(8,128)(2,1)} %get-tuple-element.35) | copy-start | bytes 50331652
  227.5 2.6 copy-start.24
  236.3 4.4 copy-start.12
  236.3 4.4 copy-start.14
  236.3 4.4 copy-start.31
  236.3 2.3 copy-start.59
  236.3 2.8 copy-start.79
  237.5 3.2 copy-start.25
  240.7 3.7 copy-start.70
  248.2 9.8 %copy-start.33 = (bf16[1,4,2,2,64,512]{5,4,3,2,1,0:T(8,128)(2,1)S(1)}, bf16[1,4,2,2,64,512]{5,4,3,2,1,0:T(8,128)(2,1)}, u32[]{:S(2)}) copy-start(bf16[1,4,2,2,64,512]{5,4,3,2,1,0:T(8,128)(2,1)} %get-tuple-element.101) | copy-start | bytes 3145732
  268.9 9.6 %copy-start.73 = (bf16[1,4,2,2,64,512]{5,4,3,2,1,0:T(8,128)(2,1)S(1)}, bf16[1,4,2,2,64,512]{5,4,3,2,1,0:T(8,128)(2,1)}, u32[]{:S(2)}) copy-start(bf16[1,4,2,2,64,512]{5,4,3,2,1,0:T(8,128)(2,1)} %get-tuple-element.97) | copy-start | bytes 3145732
  281.3 5.0 copy-start.64
  290.0 6.5 copy-start.75
  290.0 5.5 copy-start.35
  290.0 5.5 copy-start.51
  295.5 2.9 copy-start.95
  302.4 7.2 copy-start.45
  302.4 7.2 copy-start.52
  317.5 3.2 copy-start.44
  317.5 3.3 copy-start.101
  322.8 5.5 copy-start.43
  322.8 5.5 copy-start.53
  336.2 3.2 copy-start.42
  336.2 3.2 copy-start.102
  340.9 6.6 copy-start.37
  340.9 6.6 copy-start.54
  353.6 5.0 copy-start.7
  358.6 3.5 copy-start.38
  358.6 3.5 copy-start.99
  358.6 4.3 copy-start.21
  374.7 4.6 copy-start.56
  384.6 11.5 %copy-start.15 = (bf16[1,4,2,2,64,512]{5,4,3,2,1,0:T(8,128)(2,1)S(1)}, bf16[1,4,2,2,64,512]{5,4,3,2,1,0:T(8,128)(2,1)}, u32[]{:S(2)}) copy-start(bf16[1,4,2,2,64,512]{5,4,3,2,1,0:T(8,128)(2,1)} %copy-done.14) | copy-start | bytes 3145732
  392.9 3.2 copy-start.78
  392.9 3.7 copy-start.13
  392.9 3.7 copy-start.91
  402.8 6.3 copy-start.18
  409.1 2.8 copy-start.19
  414.9 15.5 %copy-start.3 = (f32[512,1024]{1,0:T(8,128)}, f32[512,1024]{1,0:T(8,128)S(1)}, u32[]{:S(2)}) copy-start(f32[512,1024]{1,0:T(8,128)S(1)} %add_add_fusion.4) | copy-start | bytes 6291460
  416.5 11.0 %copy-start.80 = (bf16[2,1,256,1024]{3,2,1,0:T(8,128)(2,1)S(1)}, bf16[2,1,256,1024]{3,2,1,0:T(8,128)(2,1)}, u32[]{:S(2)}) copy-start(bf16[2,1,256,1024]{3,2,1,0:T(8,128)(2,1)} %slice.189) | copy-start | bytes 3145732
  427.4 2.9 copy-start.94
  427.5 4.7 copy-start.26
  432.2 3.3 copy-start.27
  435.5 3.3 copy-start.71
  438.9 2.4 copy-start.32
  441.3 2.4 copy-start.60
  441.3 2.4 copy-start.100
  460.4 4.5 copy-start.87
  464.9 2.7 copy-start.88
  470.8 2.5 copy-start.85
  471.9 2.6 copy-start.83
  473.3 2.2 copy-start.82
  704.1 2.9 copy-start.28
  719.0 22.6 %copy-start.110 = (f32[3,64]{1,0:T(4,128)S(1)}, f32[3,64]{1,0:T(4,128)}, u32[]{:S(2)}) copy-start(f32[3,64]{1,0:T(4,128)} %param.23) | copy-start | bytes 2308
  719.0 22.6 %copy-start.112 = (f32[3,64]{1,0:T(4,128)S(1)}, f32[3,64]{1,0:T(4,128)}, u32[]{:S(2)}) copy-start(f32[3,64]{1,0:T(4,128)} %param.30) | copy-start | bytes 2308
  719.0 22.6 %copy-start.113 = (f32[3,64]{1,0:T(4,128)S(1)}, f32[3,64]{1,0:T(4,128)}, u32[]{:S(2)}) copy-start(f32[3,64]{1,0:T(4,128)} %param.31) | copy-start | bytes 2308
  719.0 23.3 %copy-start.23 = (f32[16,64,512]{2,1,0:T(8,128)S(1)}, f32[16,64,512]{2,1,0:T(8,128)}, u32[]{:S(2)}) copy-start(f32[16,64,512]{2,1,0:T(8,128)} %get-tuple-element.49) | copy-start | bytes 6291460
  719.0 23.3 %copy-start.90 = (f32[2,64,512]{2,1,0:T(8,128)S(1)}, f32[2,64,512]{2,1,0:T(8,128)}, u32[]{:S(2)}) copy-start(f32[2,64,512]{2,1,0:T(8,128)} %param.21) | copy-start | bytes 786436
  719.1 23.3 %copy-start.103 = (f32[2,64,512]{2,1,0:T(8,128)S(1)}, f32[2,64,512]{2,1,0:T(8,128)}, u32[]{:S(2)}) copy-start(f32[2,64,512]{2,1,0:T(8,128)} %param.26) | copy-start | bytes 786436
  719.1 23.3 %copy-start.104 = (f32[2,64,512]{2,1,0:T(8,128)S(1)}, f32[2,64,512]{2,1,0:T(8,128)}, u32[]{:S(2)}) copy-start(f32[2,64,512]{2,1,0:T(8,128)} %param.27) | copy-start | bytes 786436
  745.0 2.3 copy-start.68
  745.0 2.7 copy-start.69
  (53 other events, 91.1 us)

commit v3 on v2

--- a/solution.py
+++ b/solution.py
@@ -27,6 +27,7 @@
 MESH = pl.DeviceIdType.MESH
 ORDERS = ((2, 0, 1), (1, 0, 2))
 GROUP = 4
+GAP = 2
 
 
 def band_dims(bands):
@@ -129,10 +130,6 @@
         @pl.when(band + GROUP < bands)
         def _():
             up_copy().start()
-        for back in range(1, GROUP):
-            @pl.when(mine + back < GROUP)
-            def _():
-                peer_copy(back, ctx_ref).start()
 
     def piece(color, m, phase, step, way, incoming):
         order = ORDERS[color]
@@ -180,24 +177,24 @@
     depth = len(stages[0])
 
     def context_step(t):
-        @pl.when(t == 1)
+        for back in range(1, GROUP):
+            @pl.when((t == back - 1) & (mine + back < GROUP))
+            def _():
+                peer_copy(back, ctx_ref).start()
+        @pl.when((t == 2) & (band >= GROUP))
         def _():
-            @pl.when(band >= GROUP)
-            def _():
-                pltpu.make_async_remote_copy(
-                    ctx_ref, prev_ref, up_sem.at[0], up_sem.at[1], device_id=(band - GROUP, head), device_id_type=MESH
-                ).wait_recv()
-            for back in range(1, GROUP):
-                @pl.when((mine + back >= GROUP) & (band >= GROUP))
-                def _():
-                    peer_copy(back, prev_ref).start()
-        @pl.when(t == 4)
-        def _():
-            for back in range(1, GROUP):
-                @pl.when((mine >= back) | (band >= GROUP))
-                def _():
-                    peer_copy(back, ctx_ref).wait_recv()
-                    pair_copy(back).start()
+            pltpu.make_async_remote_copy(
+                ctx_ref, prev_ref, up_sem.at[0], up_sem.at[1], device_id=(band - GROUP, head), device_id_type=MESH
+            ).wait_recv()
+        for back in range(1, GROUP):
+            @pl.when((t == GROUP - back + 1) & (mine + back >= GROUP) & (band >= GROUP))
+            def _():
+                peer_copy(back, prev_ref).start()
+        for back in range(1, GROUP):
+            @pl.when((t == 7) & ((mine >= back) | (band >= GROUP)))
+            def _():
+                peer_copy(back, ctx_ref).wait_recv()
+                pair_copy(back).start()
 
     def gains_step(t):
         for stage in range(depth + 1):
@@ -224,7 +221,7 @@
         if has_context:
             context_step(t)
         for stage in range(depth, -1, -1):
-            m = t - stage
+            m = t - GAP * stage
             @pl.when((m >= 0) & (m < count))
             def _():
                 for color in range(2):
@@ -242,7 +239,7 @@
                                 copy.start()
         return carry
 
-    lax.fori_loop(0, count + depth, body, 0)
+    lax.fori_loop(0, count + GAP * depth, body, 0)
 
     if has_context:
         for back in range(1, GROUP):
@@ -321,30 +318,27 @@
     )(*args)
 
 
-def reduce_kernel(dims, has_context, *refs):
+def reduce_kernel(dims, count, has_context, *refs):
+    g_refs, refs = refs[:count], refs[count:]
     if has_context:
-        (g_ref, back_ref, out_ref, back_out, gv, load_sem, last_ref, mid_ref, first_ref, send_sem, recv_sem,
+        (back_ref, out_ref, back_out, gv, load_sem, last_ref, mid_ref, first_ref, send_sem, recv_sem,
          landed, relay, from_up, csend, crecv, up_sem) = refs
     else:
-        (g_ref, out_ref, gv, load_sem, last_ref, mid_ref, first_ref, send_sem, recv_sem) = refs
+        (out_ref, gv, load_sem, last_ref, mid_ref, first_ref, send_sem, recv_sem) = refs
     band, place = place_of(dims)
     head = lax.axis_index("head")
     strides = strides_of(dims)
-    count = g_ref.shape[0]
-    half = g_ref.shape[-1] // 2
+    half = g_refs[0].shape[-1] // 2
     bands = dims[0] * dims[1] * dims[2]
     true = band >= 0
     orders = tuple(order[::-1] for order in ORDERS)
     lands = (last_ref, mid_ref, first_ref)
 
-    def load(m):
-        return pltpu.make_async_copy(g_ref.at[m], gv.at[m], load_sem.at[m])
-
-    def load_all(m, carry):
-        load(m).start()
-        return carry
-
-    lax.fori_loop(0, count, load_all, 0)
+    def load(m, source):
+        return pltpu.make_async_copy(source, gv.at[m], load_sem.at[m])
+
+    for m in range(count):
+        load(m, g_refs[m]).start()
 
     extra = []
     if has_context:
@@ -366,12 +360,6 @@
         return pltpu.make_async_remote_copy(
             relay, from_up, up_sem.at[0], up_sem.at[1], device_id=(target, head), device_id_type=MESH
         )
-
-    if has_context:
-        for back in range(1, GROUP):
-            @pl.when((mine >= back) | (band >= GROUP))
-            def _():
-                peer_copy(back).start()
 
     def slot(size, step, way):
         return 0 if size == 2 else step * 2 + way
@@ -475,14 +463,18 @@
             @pl.when((m >= 0) & (m < count))
             def _():
                 if stage == 0:
-                    load(m).wait()
+                    load(m, g_refs[0]).wait()
                 for color in range(2):
                     if stage > 0:
                         settle(m, color, *stages[color][stage - 1])
                     if stage < depth:
                         send(m, color, *stages[color][stage])
         if has_context:
-            @pl.when(t == 1)
+            for back in range(1, GROUP):
+                @pl.when((t == back - 1) & ((mine >= back) | (band >= GROUP)))
+                def _():
+                    peer_copy(back).start()
+            @pl.when(t == 4)
             def _():
                 for back in range(1, GROUP):
                     @pl.when((mine + back < GROUP) | (band >= GROUP))
@@ -497,7 +489,7 @@
                             total = total + jnp.where(mine + back >= GROUP, landed[back - 1, rows, :].astype(jnp.float32), 0.0)
                         relay[rows, :] = total.astype(relay.dtype)
                     down_copy(band - GROUP).start()
-            @pl.when(t == 4)
+            @pl.when(t == 8)
             def _():
                 @pl.when((mine > 0) & (band + GROUP < bands))
                 def _():
@@ -537,7 +529,8 @@
 
 def reduce_grads(bands, grads, returned, collective_id):
     dims = band_dims(bands)
-    count, depth_rows, width = grads.shape
+    count = len(grads)
+    depth_rows, width = grads[0].shape
     rows = depth_rows // bands
     half = width // 2
     depth = len(stage_list(dims, ORDERS[0]))
@@ -546,18 +539,18 @@
     slots = lambda size: 1 if size == 2 else 2 * (size - 1)
     inner = dims[1]
     has_context = returned is not None
-    grads = grads.reshape(count, *dims, rows, width)
+    grads = [part.reshape(*dims, rows, width) for part in grads]
     scratch = [
-        pltpu.VMEM(grads.shape, grads.dtype),
+        pltpu.VMEM((count, *grads[0].shape), jnp.bfloat16),
         pltpu.SemaphoreType.DMA((count,)),
-        pltpu.VMEM((count, 2, slots(inner), dims[0], inner, rows, half), grads.dtype),
-        pltpu.VMEM((count, 2, slots(dims[0]), inner, rows, half), grads.dtype),
-        pltpu.VMEM((count, 2, slots(inner), rows, half), grads.dtype),
+        pltpu.VMEM((count, 2, slots(inner), dims[0], inner, rows, half), jnp.bfloat16),
+        pltpu.VMEM((count, 2, slots(dims[0]), inner, rows, half), jnp.bfloat16),
+        pltpu.VMEM((count, 2, slots(inner), rows, half), jnp.bfloat16),
         pltpu.SemaphoreType.DMA((2, depth, 2, count)),
         pltpu.SemaphoreType.DMA((2, depth, 2, count)),
     ]
-    args = [grads]
-    in_specs = [anyspace]
+    args = list(grads)
+    in_specs = [anyspace] * count
     out_shape = [jax.ShapeDtypeStruct((count, rows, width), jnp.float32)]
     if has_context:
         args.append(returned)
@@ -573,7 +566,7 @@
             pltpu.SemaphoreType.DMA((2,)),
         ]
     return pl.pallas_call(
-        partial(reduce_kernel, dims, has_context),
+        partial(reduce_kernel, dims, count, has_context),
         out_shape=out_shape,
         in_specs=in_specs,
         out_specs=[vmem] * len(out_shape),
@@ -874,22 +867,19 @@
     text_rows = text_states.shape[1]
     bands, head = lax.axis_size("band"), lax.axis_index("head")
     shard_rows, width = proj_master.shape[1:]
-    chunks = mlp_master.shape[2] // width
-    mlp_cut = mlp_master.reshape(2, shard_rows, chunks, width).transpose(0, 2, 1, 3)
-    shard = jnp.concatenate(
-        [proj_master, out_master, mlp_cut.reshape(2 * chunks, shard_rows, width)]
-    ).astype(jnp.bfloat16)
+    shard = jnp.concatenate([proj_master, out_master]).astype(jnp.bfloat16)
     gain_low = gain_master.astype(jnp.bfloat16).astype(jnp.float32)
     gain_tile = jnp.pad(gain_low, ((0, 5), (0, LANES - shard_rows)))
     both = jnp.concatenate([tokens, text_states], axis=1)
     context = lax.dynamic_index_in_dim(both, head, 0, keepdims=False)
     gathered, gain_tiles, passed = gather_weights(bands, shard, gain_tile, context, 1)
+    w_up = lax.all_gather(mlp_master[0].astype(jnp.bfloat16), "band", axis=0, tiled=True)
+    down_low, gain_tiles = lax.optimization_barrier((mlp_master[1].astype(jnp.bfloat16), gain_tiles))
+    w_down = lax.all_gather(down_low, "band", axis=0, tiled=True)
     weights = gathered.reshape(shard.shape[0], model_width, width)
     w_query, w_key, w_value, w_cross, w_text_key, w_text_value, w_self_out, w_cross_out = (
         weights[at] for at in range(8)
     )
-    w_up = [weights[8 + at] for at in range(chunks)]
-    w_down = [weights[8 + chunks + at] for at in range(chunks)]
     gains = gain_tiles.reshape(bands, 8, LANES)[:, :3, :shard_rows].transpose(1, 0, 2).reshape(3, model_width)
 
     offsets = earlier[:, 0]
@@ -923,21 +913,23 @@
     crossed = crossed.reshape(row_count, width)
     hidden_two = hidden_one + head_total(matmul_t(crossed, w_cross_out), 4)
     normed_three = norm_rows(hidden_two, gains[2]).astype(jnp.bfloat16)
-    before = [matmul(normed_three, part) for part in w_up]
+    before = matmul(normed_three, w_up)
     gelu = partial(jax.nn.gelu, approximate=False)
-    activated = [gelu(part).astype(jnp.bfloat16) for part in before]
-    mlp_out = sum(matmul_t(part, weight) for part, weight in zip(activated, w_down))
+    activated = gelu(before).astype(jnp.bfloat16)
+    mlp_out = matmul_t(activated, w_down)
     block_out = (hidden_two + head_total(mlp_out, 5)).astype(jnp.bfloat16).reshape(tokens.shape)
 
     incoming_low = cotangent.reshape(row_count, model_width)
     incoming = incoming_low.astype(jnp.float32)
-    grad_down = [inner_t(incoming_low, part) for part in activated]
-    grad_before = []
-    for part, weight in zip(before, w_down):
-        _, gelu_pull = jax.vjp(gelu, part)
-        grad_before.append(gelu_pull(matmul(incoming_low, weight))[0].astype(jnp.bfloat16))
-    grad_up = [inner_t(normed_three, part) for part in grad_before]
-    grad_normed_three = head_total(sum(matmul_t(part, weight) for part, weight in zip(grad_before, w_up)), 6)
+    grad_down = inner_t(incoming_low, activated).astype(jnp.bfloat16)
+    _, gelu_pull = jax.vjp(gelu, before)
+    grad_before = gelu_pull(matmul(incoming_low, w_down))[0].astype(jnp.bfloat16)
+    grad_up = inner_t(normed_three, grad_before).astype(jnp.bfloat16)
+    grad_before, grad_up, grad_down = lax.optimization_barrier((grad_before, grad_up, grad_down))
+    mlp_grad = jnp.stack(
+        [lax.psum_scatter(part, "band", scatter_dimension=0, tiled=True) for part in (grad_up, grad_down)]
+    ).astype(jnp.float32)
+    grad_normed_three = head_total(matmul_t(grad_before, w_up), 6)
     _, pull_three = jax.vjp(norm_rows, hidden_two, gains[2])
     back_two, gain_grad_three = pull_three(grad_normed_three)
     grad_two = incoming + back_two
@@ -979,23 +971,19 @@
     returned = (mine.astype(jnp.float32) + mine_there.astype(jnp.float32)).astype(jnp.bfloat16)
 
     flat = lambda part: part.reshape(-1, width)
-    grads = jnp.stack(
-        [
-            part.astype(jnp.bfloat16)
-            for part in (
-                inner_t(normed_one, grad_queries),
-                inner_t(normed_all, flat(grad_keys)),
-                inner_t(normed_all, flat(grad_values)),
-                inner_t(normed_two, grad_cq),
-                inner_t(caption, grad_ck),
-                inner_t(caption, grad_cv),
-                grad_self_out,
-                grad_cross_out,
-                *grad_up,
-                *grad_down,
-            )
-        ]
-    )
+    grads = [
+        part.astype(jnp.bfloat16)
+        for part in (
+            inner_t(normed_one, grad_queries),
+            inner_t(normed_all, flat(grad_keys)),
+            inner_t(normed_all, flat(grad_values)),
+            inner_t(normed_two, grad_cq),
+            inner_t(caption, grad_ck),
+            inner_t(caption, grad_cv),
+            grad_self_out,
+            grad_cross_out,
+        )
+    ]
     summed, came_back = reduce_grads(bands, grads, returned, 2)
     came_low = came_back.astype(jnp.bfloat16)
     (came_there,) = swapped(9, came_low)
@@ -1007,7 +995,7 @@
     back_zero, gain_grad_one = pull_one(grad_normed_one)
     grad_tokens = (grad_one + back_zero).reshape(tokens.shape)
 
-    squares = jnp.sum(summed * summed)
+    squares = jnp.sum(summed * summed) + jnp.sum(mlp_grad * mlp_grad)
     gain_rows = jnp.stack([gain_grad_one, gain_grad_two, gain_grad_three]).reshape(-1, LANES)
     tile = jnp.concatenate([gain_rows, jnp.full((8, LANES), squares)])
     tile = mesh_total(bands, tile, 10)
@@ -1015,7 +1003,6 @@
     grad_norm = jnp.sqrt(tile[-1, 0] + jnp.sum(gain_total * gain_total))
     gain_grad = lax.dynamic_slice_in_dim(gain_total, lax.axis_index("band") * shard_rows, shard_rows, 1)
     proj_grad, out_grad = summed[:6], summed[6:8]
-    mlp_grad = summed[8:].reshape(2, chunks, shard_rows, width).transpose(0, 2, 1, 3).reshape(mlp_master.shape)
     factor = jnp.minimum(1.0, CLIP / grad_norm)
     matrix_rate = 2.0 * D ** (-0.5)
     new_proj = adamw_update(

time: 762 us -> 668 us (0.88)
  Pallas kernels: 520 us -> 446 us
  local copies, waits for them, and re-layouts: 59.6 us -> 29.5 us
  between operations: 4.68 us -> 18.8 us
    pallas_call x1, Pallas kernels: 207 us -> 162 us  [gather_weights(): pl.pallas_call(partial(gather_kernel, dims, has_context), out_shape=out_s...]
    pallas_call x1, Pallas kernels: 221 us -> 190 us  [reduce_grads(): pl.pallas_call(partial(reduce_kernel, dims, count, has_context), out_shap...]
    unnamed x253 -> x180, local copies, waits for them, and re-layouts: 35.6 us -> 18.6 us
    dot_general x16 -> x10, matrix products: 27.2 us -> 36.5 us  [matmul_t(): lax.dot_general(former, latter, (((1,), (1,)), ((), ())), preferred_eleme...]
    convert_element_type x4 -> x0, local copies, waits for them, and re-layouts: 9.15 us -> none  [local(): part.astype(jnp.bfloat16)]
    dot_general x16 -> x10, matrix products: 34.7 us -> 26 us  [inner_t(): lax.dot_general(former, latter, (((0,), (0,)), ((), ())), preferred_eleme...]
    dot_general x16 -> x10, matrix products: 46 us -> 41.7 us  [matmul(): return jnp.dot(former, latter, preferred_element_type=jnp.float32)]
  transfers between devices with their start and end apart: 0 -> 4, of which waited for: 0 -> 0; matrix products, arithmetic and copies ran while one was open for 0% -> 22% of each run, Pallas kernels for 0% -> 65%
where the time goes in v3:
time: 668 us; the launch traced here: 657 us
  Pallas kernels  446 us (67%)
  matrix products  104 us (16%)
  other arithmetic  57.9 us (9%)
  local copies, waits for them, and re-layouts  29.5 us (4%)
  between operations  18.8 us (3%)
    pallas_call x1, Pallas kernels, reduce_grads(): pl.pallas_call(partial(reduce_kernel, dims, count, has_context), out_shap...  190 us
    pallas_call x1, Pallas kernels, gather_weights(): pl.pallas_call(partial(gather_kernel, dims, has_context), out_shape=out_s...  162 us
    dot_general x10, matrix products, matmul(): return jnp.dot(former, latter, preferred_element_type=jnp.float32)  41.7 us
    pallas_call x7, Pallas kernels, swapped(): pl.pallas_call(partial(swap_kernel, len(arrays)), out_shape=[jax.ShapeDty...  39.9 us
    dot_general x10, matrix products, matmul_t(): lax.dot_general(former, latter, (((1,), (1,)), ((), ())), preferred_eleme...  36.5 us
    dot_general x10, matrix products, inner_t(): lax.dot_general(former, latter, (((0,), (0,)), ((), ())), preferred_eleme...  26 us
    pallas_call x2, Pallas kernels, attention_back(): pl.pallas_call(partial(by_offset, attend_back_body, causal), grid=(stream...  19.6 us
    unnamed x180, local copies, waits for them, and re-layouts  18.6 us
  transfers between devices with their start and end apart: 4, of which 0 were waited for; matrix products, arithmetic and copies ran while one was open for 22% of the time, Pallas kernels for 65%

profile of v3, /device:TPU:0, one launch (start us, length us, event | category | flops | bytes accessed | tf_op | source)
XLA Modules:
  0.0 656.6 jit_solution(4436526868844356531)
XLA Ops:
  7.3 1.4 convert.18
  12.1 161.8 %gather_weights.1 = (bf16[8,4,2,2,64,512]{5,4,3,2,1,0:T(8,128)(2,1)}, f32[4,2,2,8,128]{4,3,2,1,0:T(8,128)}, bf16[2,3,384,1024]{3,2,1,0:T(8,128)(2,1)}) custom-call(bf16[8,64,512]{2,1,0:T(8,128)(2,1)} %pad_maximum_fusion.2.refs_0_, f32[8,128]{1,0:T(8,128)} %pad_convert_fusion.refs_1_, bf16[384,1024]{1,0:T(8,128)(2,1)} %fusion.56.refs_2_), custom_call_target="tpu_custom_call" | custom-call | tf_op jit(solution)/shard_map/gather_weights/pallas_call | solution.py:310
  175.0 2.3 slice.101
  177.9 1.4 fusion.2
  179.4 1.4 copy-done.26
  180.8 2.1 fusion.78
  182.9 1.7 fusion.5
  184.6 3.8 convolution_convert_fusion.1
  188.4 3.7 convolution_convert_fusion.2
  193.3 2.7 convolution_convert_fusion.16
  196.0 10.1 %attend.2 = (bf16[2,256,512]{2,1,0:T(8,128)(2,1)}, f32[2,4,8,256]{3,2,1,0:T(8,128)}) custom-call(s32[2]{0:T(128)} %bitcast.285, bf16[2,256,512]{2,1,0:T(8,128)(2,1)} %bitcast.251, bf16[2,4,256,512]{3,2,1,0:T(8,128)(2,1)} %bitcast.226, bf16[2,4,256,512]{3,2,1,0:T(8,128)(2,1)} %bitcast.224), custom_call_target="tpu_custom_call" | custom-call | tf_op jit(solution)/shard_map/attend/pallas_call | solution.py:700
  206.2 2.8 convolution_convert_fusion.11.refs_0_
  208.9 4.9 swap_heads.7
  213.8 2.0 fusion.77
  216.9 2.0 fusion.58
  221.3 1.6 convolution_convert_fusion.15
  222.9 8.0 %attend.3 = (bf16[2,256,512]{2,1,0:T(8,128)(2,1)}, f32[2,4,8,256]{3,2,1,0:T(8,128)}) custom-call(s32[2]{0:T(128)} %bitcast.286, bf16[2,256,512]{2,1,0:T(8,128)(2,1)} %bitcast.248, bf16[2,1,128,512]{3,2,1,0:T(8,128)(2,1)} %bitcast.246, bf16[2,1,128,512]{3,2,1,0:T(8,128)(2,1)} %bitcast.244), custom_call_target="tpu_custom_call" | custom-call | tf_op jit(solution)/shard_map/attend/pallas_call | solution.py:700
  230.9 3.1 convolution_convert_fusion.10.refs_0_
  234.0 4.9 swap_heads.8
  238.9 2.0 fusion.76
  240.8 1.4 copy-done.5
  242.6 16.1 %multiply_convert_fusion = (bf16[512,2048]{1,0:T(8,128)(2,1)S(1)}, f32[512,2048]{1,0:T(8,128)}, f32[512,2048]{1,0:T(8,128)}) fusion(bf16[1,1024,2048]{2,1,0:T(8,128)(2,1)} %all-gather.6.cloned.1.call-done, f32[512,1024]{1,0:T(8,128)} %copy-done.5, f32[1024]{0:T(1024)S(1)} %mul.458, f32[512]{0:T(512)S(1)} %fusion.64, f32[512]{0:T(512)S(1)} %broadcast_multiply_fusion.2), kind=kOutput, calls=%fused_computation.32 | convolution fusion | flops 2217738240 | bytes 16785408 | tf_op jit(solution)/shard_map/dot_general | solution.py:588
  260.1 4.4 convert_bitcast_fusion
  264.5 8.5 %fusion.13 = bf16[512,2048]{1,0:T(8,128)(2,1)S(1)} fusion(f32[512,2048]{1,0:T(8,128)} %get-tuple-element.88, f32[512,2048]{1,0:T(8,128)} %get-tuple-element.120, bf16[512,1024]{1,0:T(8,128)(2,1)} %bitcast.237, bf16[1024,2048]{1,0:T(8,128)(2,1)} %all-gather.4.cloned.1.call-done), kind=kOutput, calls=%fused_computation.25 | convolution fusion | flops 2162163712 | bytes 15728640 | tf_op jit(solution)/shard_map/dot_general | solution.py:588
  274.4 4.6 convolution_convert_fusion
  280.8 6.2 convolution_convert_fusion.12.refs_0_
  287.0 4.9 swap_heads.9
  291.9 6.2 fusion.45.refs_0_
  298.1 5.0 swap_heads.10
  303.1 3.5 multiply_reduce_fusion
  306.7 3.4 fusion.74
  312.1 1.5 convolution_convert_fusion.14
  313.6 8.3 %attend_back.2 = (bf16[2,256,512]{2,1,0:T(8,128)(2,1)}, bf16[2,1,128,512]{3,2,1,0:T(8,128)(2,1)}, bf16[2,1,128,512]{3,2,1,0:T(8,128)(2,1)}) custom-call(s32[2]{0:T(128)} %bitcast.287, bf16[2,256,512]{2,1,0:T(8,128)(2,1)} %bitcast.249, bf16[2,1,128,512]{3,2,1,0:T(8,128)(2,1)} %bitcast.247, bf16[2,1,128,512]{3,2,1,0:T(8,128)(2,1)} %bitcast.245, ...), custom_call_target="tpu_custom_call" | custom-call | tf_op jit(solution)/shard_map/attend_back/pallas_call | solution.py:716
  321.9 2.8 convolution_convert_fusion.9.refs_0_
  324.7 5.0 swap_heads.11
  329.7 2.8 multiply_reduce_fusion.1
  334.8 1.3 copy-done.2
  336.2 1.5 convolution_convert_fusion.13
  337.7 11.2 %attend_back.3 = (bf16[2,256,512]{2,1,0:T(8,128)(2,1)}, bf16[2,4,256,512]{3,2,1,0:T(8,128)(2,1)}, bf16[2,4,256,512]{3,2,1,0:T(8,128)(2,1)}) custom-call(s32[2]{0:T(128)} %bitcast.288, bf16[2,256,512]{2,1,0:T(8,128)(2,1)} %bitcast.252, bf16[2,4,256,512]{3,2,1,0:T(8,128)(2,1)} %bitcast.227, bf16[2,4,256,512]{3,2,1,0:T(8,128)(2,1)} %bitcast.225, ...), custom_call_target="tpu_custom_call" | custom-call | tf_op jit(solution)/shard_map/attend_back/pallas_call | solution.py:716
  348.9 7.3 %fusion.82 = f32[2048,1024]{1,0:T(8,128)} fusion(bf16[2048,512]{1,0:T(8,128)(2,1)} %bitcast.295, bf16[1024,512]{1,0:T(8,128)(2,1)S(1)} %bitcast.256), kind=kOutput, calls=%fused_computation.202 | convolution fusion | flops 2147483648 | bytes 11534336 | tf_op jit(solution)/shard_map/dot_general | solution.py:592
  357.4 6.6 %convolution_add_fusion = f32[2048,1024]{1,0:T(8,128)S(1)} fusion(f32[2048,1024]{1,0:T(8,128)} %fusion.82, bf16[2048,512]{1,0:T(8,128)(2,1)} %bitcast.230, bf16[1024,512]{1,0:T(8,128)(2,1)S(1)} %bitcast.234), kind=kOutput, calls=%fused_computation.46 | convolution fusion | flops 2149580800 | bytes 19922944 | tf_op jit(solution)/shard_map/dot_general | solution.py:592
  371.9 1.7 fusion.27.refs_1_
  373.6 10.9 %swap_heads.12 = (bf16[2,384,1024]{2,1,0:T(8,128)(2,1)}, bf16[3,384,1024]{2,1,0:T(8,128)(2,1)}) custom-call(bf16[2,384,1024]{2,1,0:T(8,128)(2,1)} %pad_maximum_fusion.1.refs_0_, bf16[3,384,1024]{2,1,0:T(8,128)(2,1)} %fusion.27.refs_1_), custom_call_target="tpu_custom_call" | custom-call | tf_op jit(solution)/shard_map/swap_heads/pallas_call | solution.py:752
  384.5 1.5 convolution_convert_fusion.3
  386.0 1.4 convolution_convert_fusion.4
  387.5 1.8 convolution_convert_fusion.5
  389.2 1.7 convolution_convert_fusion.8
  391.0 1.7 convolution_convert_fusion.6
  392.7 1.9 convolution_convert_fusion.7
  394.9 2.6 fusion.6.refs_8_
  398.6 3.5 bitcast_convert_fusion.1
  402.2 3.4 bitcast_convert_fusion
  405.5 190.1 %reduce_grads.1 = (f32[8,64,512]{2,1,0:T(8,128)}, f32[384,1024]{1,0:T(8,128)}) custom-call(bf16[4,2,2,64,512]{4,3,2,1,0:T(8,128)(2,1)} %bitcast.272, bf16[4,2,2,64,512]{4,3,2,1,0:T(8,128)(2,1)} %bitcast.274, bf16[4,2,2,64,512]{4,3,2,1,0:T(8,128)(2,1)} %bitcast.275, bf16[4,2,2,64,512]{4,3,2,1,0:T(8,128)(2,1)} %bitcast.273, ...), custom_call_target="tpu_custom_call" | custom-call | tf_op jit(solution)/shard_map/reduce_grads/pallas_call | solution.py:568
  595.7 2.5 convert_element_type.271.refs_0_
  598.2 4.3 swap_heads.13
  602.6 1.4 select_bitcast_fusion.1
  608.0 2.3 fusion.41
  610.4 2.1 multiply_reduce_fusion.6
  612.5 3.6 fusion.29
  616.2 2.0 fusion.52
  620.1 16.3 %mesh_total.1 = f32[32,128]{1,0:T(8,128)} custom-call(f32[32,128]{1,0:T(8,128)} %concatenate.24.in_ref), custom_call_target="tpu_custom_call" | custom-call | tf_op jit(solution)/shard_map/mesh_total/pallas_call | solution.py:814
  640.3 2.1 multiply_subtract_fusion.2
  642.4 3.3 multiply_subtract_fusion.1
  645.9 2.2 multiply_subtract_fusion
  (247 shorter events, 37.2 us)
Async XLA Ops:
  7.2 2.4 copy-start.78
  7.2 2.4 copy-start.60
  7.2 2.4 copy-start.45
  7.2 235.4 %all-gather.6.cloned.1.call-start = ((), (), s32[]{:S(2)}) async-start(), calls=%async_computation.5 | async-start | bytes 4456448 | tf_op jit(solution)/shard_map/all_gather | solution.py:876
  8.6 2.5 copy-start
  8.6 2.5 copy-start.48
  9.5 255.0 %all-gather.4.cloned.1.call-start = ((), (), s32[]{:S(2)}) async-start(), calls=%async_computation.2 | async-start | bytes 4456448 | tf_op jit(solution)/shard_map/all_gather | solution.py:878
  11.1 162.8 %copy-start.75 = (s32[2,1]{0,1:T(1,128)S(1)}, s32[2,1]{0,1:T(1,128)}, u32[]{:S(2)}) copy-start(s32[2,1]{0,1:T(1,128)} %param.19) | copy-start | bytes 28
  173.9 442.2 %reduce-scatter.3.cloned.1.call-start = ((), (), s32[]{:S(2)}) async-start(), calls=%async_computation.3 | async-start | bytes 4456448 | tf_op jit(solution)/shard_map/reduce_scatter | solution.py:930
  175.0 7.9 %copy-start.70 = (f32[1024]{0:T(1024)}, f32[1024]{0:T(1024)S(1)}, u32[]{:S(2)}) copy-start(f32[1024]{0:T(1024)S(1)} %mul.446) | copy-start | bytes 12292
  177.3 3.5 copy-start.26
  182.9 5.5 copy-start.51
  182.9 10.4 %copy-start.41 = (bf16[1,4,2,2,64,512]{5,4,3,2,1,0:T(8,128)(2,1)}, bf16[1,4,2,2,64,512]{5,4,3,2,1,0:T(8,128)(2,1)S(1)}, u32[]{:S(2)}) copy-start(bf16[1,4,2,2,64,512]{5,4,3,2,1,0:T(8,128)(2,1)S(1)} %get-tuple-element.100) | copy-start | bytes 3145732
  182.9 23.2 %copy-start.35 = (bf16[1,4,2,2,64,512]{5,4,3,2,1,0:T(8,128)(2,1)}, bf16[1,4,2,2,64,512]{5,4,3,2,1,0:T(8,128)(2,1)S(1)}, u32[]{:S(2)}) copy-start(bf16[1,4,2,2,64,512]{5,4,3,2,1,0:T(8,128)(2,1)S(1)} %get-tuple-element.97) | copy-start | bytes 3145732
  184.6 7.5 %copy-start.27 = (bf16[2,4,256,1024]{3,2,1,0:T(8,128)(2,1)}, bf16[2,4,256,1024]{3,2,1,0:T(8,128)(2,1)S(1)}, u32[]{:S(2)}) copy-start(bf16[2,4,256,1024]{3,2,1,0:T(8,128)(2,1)S(1)} %fusion.5) | copy-start | bytes 12582916
  215.9 3.1 copy-start.18
  216.9 3.2 copy-start.20
  219.0 2.3 copy-start.53
  242.6 17.5 %copy-start.38 = (bf16[2,256,1024]{2,1,0:T(8,128)(2,1)S(1)}, bf16[2,256,1024]{2,1,0:T(8,128)(2,1)}, u32[]{:S(2)}) copy-start(bf16[2,256,1024]{2,1,0:T(8,128)(2,1)} %param.18) | copy-start | bytes 3145732
  264.5 9.8 %copy-start.6 = (f32[512,1024]{1,0:T(8,128)S(1)}, f32[512,1024]{1,0:T(8,128)}, u32[]{:S(2)}) copy-start(f32[512,1024]{1,0:T(8,128)} %copy-done.5) | copy-start | bytes 6291460
  279.0 337.1 %reduce-scatter.5.cloned.1.call-start = ((), (), s32[]{:S(2)}) async-start(), calls=%async_computation.4 | async-start | bytes 4456448 | tf_op jit(solution)/shard_map/reduce_scatter | solution.py:930
  298.1 5.0 copy-start.16
  303.1 3.5 copy-start.7
  303.1 3.5 copy-start.17
  303.1 3.5 copy-start.37
  306.7 3.4 copy-start.39
  310.1 2.0 copy-start.55
  312.1 9.8 %copy-start.54 = (bf16[1,4,2,2,64,512]{5,4,3,2,1,0:T(8,128)(2,1)S(1)}, bf16[1,4,2,2,64,512]{5,4,3,2,1,0:T(8,128)(2,1)}, u32[]{:S(2)}) copy-start(bf16[1,4,2,2,64,512]{5,4,3,2,1,0:T(8,128)(2,1)} %get-tuple-element.96) | copy-start | bytes 3145732
  324.7 5.0 copy-start.24
  329.7 2.8 copy-start.25
  332.5 1.9 copy-start.40
  337.7 11.2 %copy-start.52 = (bf16[1,4,2,2,64,512]{5,4,3,2,1,0:T(8,128)(2,1)S(1)}, bf16[1,4,2,2,64,512]{5,4,3,2,1,0:T(8,128)(2,1)}, u32[]{:S(2)}) copy-start(bf16[1,4,2,2,64,512]{5,4,3,2,1,0:T(8,128)(2,1)} %copy-done.51) | copy-start | bytes 3145732
  364.6 6.2 copy-start.8
  364.6 2.1 copy-start.19
  364.6 2.3 copy-start.66
  373.6 10.9 %copy-start.15 = (bf16[2,128,1024]{2,1,0:T(8,128)(2,1)S(1)}, bf16[2,128,1024]{2,1,0:T(8,128)(2,1)}, u32[]{:S(2)}) copy-start(bf16[2,128,1024]{2,1,0:T(8,128)(2,1)} %copy-done.14) | copy-start | bytes 1572868
  384.5 2.9 copy-start.65
  384.5 2.9 copy-start.84
  386.0 3.2 copy-start.59
  386.0 3.2 copy-start.69
  389.2 3.5 copy-start.85
  391.0 3.6 copy-start.13
  391.0 3.6 copy-start.47
  392.7 2.2 copy-start.9
  394.9 2.6 copy-start.28
  394.9 3.7 copy-start.83
  398.6 3.5 copy-start.29
  595.7 6.9 %copy-start.30 = (f32[384,1024]{1,0:T(8,128)S(1)}, f32[384,1024]{1,0:T(8,128)}, u32[]{:S(2)}) copy-start(f32[384,1024]{1,0:T(8,128)} %get-tuple-element.56) | copy-start | bytes 4718596
  602.5 2.1 copy-start.50
  608.0 2.3 copy-start.73
  608.0 2.3 copy-start.74
  608.0 4.5 copy-start.4
  608.0 4.5 copy-start.80
  612.5 27.8 %copy-start.61 = (f32[2,64,512]{2,1,0:T(8,128)S(1)}, f32[2,64,512]{2,1,0:T(8,128)}, u32[]{:S(2)}) copy-start(f32[2,64,512]{2,1,0:T(8,128)} %param.21) | copy-start | bytes 786436
  616.1 26.3 %copy-start.44 = (f32[8,64,512]{2,1,0:T(8,128)S(1)}, f32[8,64,512]{2,1,0:T(8,128)}, u32[]{:S(2)}) copy-start(f32[8,64,512]{2,1,0:T(8,128)} %get-tuple-element.57) | copy-start | bytes 3145732
  616.1 26.3 %copy-start.46 = (f32[6,64,512]{2,1,0:T(8,128)S(1)}, f32[6,64,512]{2,1,0:T(8,128)}, u32[]{:S(2)}) copy-start(f32[6,64,512]{2,1,0:T(8,128)} %param.20) | copy-start | bytes 2359300
  642.4 3.4 copy-start.43
  642.4 3.4 copy-start.57
  642.4 3.4 copy-start.58
  642.4 3.4 copy-start.62
  642.4 3.4 copy-start.63
  645.8 2.3 copy-start.79
  645.8 2.3 copy-start.81
  645.8 2.2 copy-start.82
  (28 other events, 39.6 us)
Sparse Core Ops, SparseCore 0:
  11.4 117.8 all-gather.5
  174.0 74.0 all-gather.3
  279.2 95.3 reduce-scatter.2
  376.7 134.8 reduce-scatter.4

commit v4 on v3

--- a/solution.py
+++ b/solution.py
@@ -1,3 +1,4 @@
+import math
 from functools import partial
 
 import jax
@@ -314,12 +315,14 @@
         out_specs=[anyspace] * len(out_shape),
         scratch_shapes=scratch,
         compiler_params=pltpu.CompilerParams(collective_id=collective_id, has_side_effects=True),
+        cost_estimate=worth(200),
         name="gather_weights",
     )(*args)
 
 
-def reduce_kernel(dims, count, has_context, *refs):
-    g_refs, refs = refs[:count], refs[count:]
+def reduce_kernel(dims, arrays, has_context, *refs):
+    sources = [ref.at[one] for ref in refs[:arrays] for one in range(ref.shape[0])]
+    count, refs = len(sources), refs[arrays:]
     if has_context:
         (back_ref, out_ref, back_out, gv, load_sem, last_ref, mid_ref, first_ref, send_sem, recv_sem,
          landed, relay, from_up, csend, crecv, up_sem) = refs
@@ -328,7 +331,7 @@
     band, place = place_of(dims)
     head = lax.axis_index("head")
     strides = strides_of(dims)
-    half = g_refs[0].shape[-1] // 2
+    half = sources[0].shape[-1] // 2
     bands = dims[0] * dims[1] * dims[2]
     true = band >= 0
     orders = tuple(order[::-1] for order in ORDERS)
@@ -338,7 +341,7 @@
         return pltpu.make_async_copy(source, gv.at[m], load_sem.at[m])
 
     for m in range(count):
-        load(m, g_refs[m]).start()
+        load(m, sources[m]).start()
 
     extra = []
     if has_context:
@@ -463,7 +466,7 @@
             @pl.when((m >= 0) & (m < count))
             def _():
                 if stage == 0:
-                    load(m, g_refs[0]).wait()
+                    load(m, sources[0]).wait()
                 for color in range(2):
                     if stage > 0:
                         settle(m, color, *stages[color][stage - 1])
@@ -529,8 +532,8 @@
 
 def reduce_grads(bands, grads, returned, collective_id):
     dims = band_dims(bands)
-    count = len(grads)
-    depth_rows, width = grads[0].shape
+    count = sum(part.shape[0] for part in grads)
+    depth_rows, width = grads[0].shape[1:]
     rows = depth_rows // bands
     half = width // 2
     depth = len(stage_list(dims, ORDERS[0]))
@@ -539,9 +542,9 @@
     slots = lambda size: 1 if size == 2 else 2 * (size - 1)
     inner = dims[1]
     has_context = returned is not None
-    grads = [part.reshape(*dims, rows, width) for part in grads]
+    grads = [part.reshape(-1, *dims, rows, width) for part in grads]
     scratch = [
-        pltpu.VMEM((count, *grads[0].shape), jnp.bfloat16),
+        pltpu.VMEM((count, *grads[0].shape[1:]), jnp.bfloat16),
         pltpu.SemaphoreType.DMA((count,)),
         pltpu.VMEM((count, 2, slots(inner), dims[0], inner, rows, half), jnp.bfloat16),
         pltpu.VMEM((count, 2, slots(dims[0]), inner, rows, half), jnp.bfloat16),
@@ -550,7 +553,7 @@
         pltpu.SemaphoreType.DMA((2, depth, 2, count)),
     ]
     args = list(grads)
-    in_specs = [anyspace] * count
+    in_specs = [anyspace] * len(grads)
     out_shape = [jax.ShapeDtypeStruct((count, rows, width), jnp.float32)]
     if has_context:
         args.append(returned)
@@ -566,7 +569,7 @@
             pltpu.SemaphoreType.DMA((2,)),
         ]
     return pl.pallas_call(
-        partial(reduce_kernel, dims, count, has_context),
+        partial(reduce_kernel, dims, len(grads), has_context),
         out_shape=out_shape,
         in_specs=in_specs,
         out_specs=[vmem] * len(out_shape),
@@ -574,6 +577,7 @@
         compiler_params=pltpu.CompilerParams(
             collective_id=collective_id, has_side_effects=True, vmem_limit_bytes=67043328
         ),
+        cost_estimate=worth(1),
         name="reduce_grads",
     )(*args)
 
@@ -598,6 +602,240 @@
     return lax.dot_general(
         former, latter, (((0,), (0,)), ((), ())), preferred_element_type=jnp.float32
     )
+
+
+def worth(microseconds):
+    return pl.CostEstimate(flops=microseconds * 10**9, bytes_accessed=0, transcendentals=0)
+
+
+def norm_stats(rows):
+    centre = rows - jnp.mean(rows, axis=-1, keepdims=True)
+    inverse = lax.rsqrt(jnp.mean(centre * centre, axis=-1, keepdims=True) + EPS)
+    return centre * inverse, inverse
+
+
+def norm_pull(rows, gain_row, grad):
+    unit, inverse = norm_stats(rows)
+    scaled = grad * gain_row
+    inner = jnp.mean(scaled * unit, axis=-1, keepdims=True)
+    pulled = inverse * (scaled - jnp.mean(scaled, axis=-1, keepdims=True) - unit * inner)
+    return pulled, jnp.sum(grad * unit, axis=0, keepdims=True)
+
+
+def greet_pair():
+    pl.semaphore_signal(
+        pltpu.get_barrier_semaphore(), inc=1,
+        device_id=(lax.axis_index("band"), 1 - lax.axis_index("head")), device_id_type=MESH,
+    )
+
+
+def pair_send(source, target, send_sem, recv_sem):
+    return pltpu.make_async_remote_copy(
+        source, target, send_sem, recv_sem,
+        device_id=(lax.axis_index("band"), 1 - lax.axis_index("head")), device_id_type=MESH,
+    )
+
+
+def mlp_kernel(
+    hidden_ref, incoming_ref, gain_ref, up_ref, down_ref,
+    block_ref, grad_ref, gain_grad_ref, grad_up_ref, grad_down_ref,
+    normed, normed_t, incoming_t, out_sum, back_sum, low, there, send_sem, recv_sem,
+):
+    step, last = pl.program_id(0), pl.num_programs(0) - 1
+    rows = hidden_ref.shape[0]
+    tile = 64
+
+    @pl.when(step == 0)
+    def _():
+        greet_pair()
+
+        def one(at, carry):
+            part = pl.ds(pl.multiple_of(at * tile, tile), tile)
+            unit, _ = norm_stats(hidden_ref[part, :])
+            normed[part, :] = (unit * gain_ref[...]).astype(jnp.bfloat16)
+            return carry
+
+        lax.fori_loop(0, rows // tile, one, 0)
+        normed_t[...] = normed[...].T
+        incoming_t[...] = incoming_ref[...].T
+        out_sum[...] = jnp.zeros_like(out_sum)
+        back_sum[...] = jnp.zeros_like(back_sum)
+
+    copies = [pair_send(low.at[one], there.at[one], send_sem.at[one], recv_sem.at[one]) for one in range(2)]
+    before = matmul(normed[...], up_ref[...])
+    share = 0.5 * (1.0 + lax.erf(before * 2.0**-0.5))
+    activated = (before * share).astype(jnp.bfloat16)
+    out_sum[...] += matmul_t(activated, down_ref[...])
+
+    @pl.when(step == last)
+    def _():
+        pl.semaphore_wait(pltpu.get_barrier_semaphore(), 1)
+        low[0] = out_sum[...].astype(jnp.bfloat16)
+        copies[0].start()
+
+    slope = share + before * jnp.exp(before * before * -0.5) * (2.0 * math.pi) ** -0.5
+    grad_before = (matmul(incoming_ref[...], down_ref[...]) * slope).astype(jnp.bfloat16)
+    back_sum[...] += matmul_t(grad_before, up_ref[...])
+
+    @pl.when(step == last)
+    def _():
+        low[1] = back_sum[...].astype(jnp.bfloat16)
+        copies[1].start()
+
+    grad_down_ref[...] = matmul(incoming_t[...], activated).astype(jnp.bfloat16)
+    grad_up_ref[...] = matmul(normed_t[...], grad_before).astype(jnp.bfloat16)
+
+    @pl.when(step == last)
+    def _():
+        for copy in copies:
+            copy.wait()
+        gain_grad_ref[...] = jnp.zeros_like(gain_grad_ref)
+
+        def one(at, carry):
+            part = pl.ds(pl.multiple_of(at * tile, tile), tile)
+            total = lambda which: low[which, part, :].astype(jnp.float32) + there[which, part, :].astype(jnp.float32)
+            hidden = hidden_ref[part, :]
+            block_ref[part, :] = (hidden + total(0)).astype(jnp.bfloat16)
+            pulled, gain_part = norm_pull(hidden, gain_ref[...], total(1))
+            grad_ref[part, :] = incoming_ref[part, :].astype(jnp.float32) + pulled
+            gain_grad_ref[...] += gain_part
+            return carry
+
+        lax.fori_loop(0, rows // tile, one, 0)
+
+
+def mlp_both_ways(hidden, incoming, gain_row, weights, first, w_down, collective_id):
+    rows, width = hidden.shape
+    units, cut = w_down.shape[1], weights.shape[2]
+    whole = pl.BlockSpec((rows, width), lambda step: (0, 0))
+    line = pl.BlockSpec((1, width), lambda step: (0, 0))
+    columns = pl.BlockSpec((width, cut), lambda step: (0, step))
+    up_matrix = pl.BlockSpec((None, width, cut), lambda step: (first + step, 0, 0))
+    grad_matrix = pl.BlockSpec((None, width, cut), lambda step: (step, 0, 0))
+    return pl.pallas_call(
+        mlp_kernel,
+        grid=(units // cut,),
+        in_specs=[whole, whole, line, up_matrix, columns],
+        out_specs=[whole, whole, line, grad_matrix, columns],
+        out_shape=[
+            jax.ShapeDtypeStruct((rows, width), jnp.bfloat16),
+            jax.ShapeDtypeStruct((rows, width), jnp.float32),
+            jax.ShapeDtypeStruct((1, width), jnp.float32),
+            jax.ShapeDtypeStruct((units // cut, width, cut), jnp.bfloat16),
+            jax.ShapeDtypeStruct((width, units), jnp.bfloat16),
+        ],
+        scratch_shapes=[
+            pltpu.VMEM((rows, width), jnp.bfloat16),
+            pltpu.VMEM((width, rows), jnp.bfloat16),
+            pltpu.VMEM((width, rows), jnp.bfloat16),
+            pltpu.VMEM((rows, width), jnp.float32),
+            pltpu.VMEM((rows, width), jnp.float32),
+            pltpu.VMEM((2, rows, width), jnp.bfloat16),
+            pltpu.VMEM((2, rows, width), jnp.bfloat16),
+            pltpu.SemaphoreType.DMA((2,)),
+            pltpu.SemaphoreType.DMA((2,)),
+        ],
+        compiler_params=pltpu.CompilerParams(
+            collective_id=collective_id, has_side_effects=True, vmem_limit_bytes=63 * 1024 * 1024
+        ),
+        cost_estimate=worth(1),
+        name="mlp_both_ways",
+    )(hidden, incoming, gain_row, weights, w_down)
+
+
+def row_kernel(backward, follows, *refs):
+    refs = list(refs)
+    x_ref, w_ref, base_ref, gain_ref = refs[:4]
+    rest = refs[4:]
+    hidden_ref = rest.pop(0) if backward else None
+    next_ref = rest.pop(0) if follows else None
+    sum_ref = rest.pop(0)
+    low_ref, next_out_ref = (rest.pop(0), rest.pop(0)) if follows else (None, None)
+    gain_grad_ref = rest.pop(0) if backward else None
+    low, there, send_sem, recv_sem = rest
+    rows = x_ref.shape[0]
+    cut = rows // send_sem.shape[0]
+    greet_pair()
+
+    def part_of(at):
+        return pl.ds(pl.multiple_of(at * cut, cut), cut)
+
+    def copy_of(at):
+        return pair_send(low.at[part_of(at)], there.at[part_of(at)], send_sem.at[at], recv_sem.at[at])
+
+    for at in range(rows // cut):
+        low[part_of(at), :] = matmul_t(x_ref[part_of(at), :], w_ref[...]).astype(jnp.bfloat16)
+        if at == 0:
+            pl.semaphore_wait(pltpu.get_barrier_semaphore(), 1)
+        copy_of(at).start()
+    if backward:
+        gain_grad_ref[...] = jnp.zeros_like(gain_grad_ref)
+
+    def finish(at, carry):
+        part = part_of(at)
+        copy_of(at).wait()
+        total = low[part, :].astype(jnp.float32) + there[part, :].astype(jnp.float32)
+        base = base_ref[part, :].astype(jnp.float32)
+        if backward:
+            pulled, gain_part = norm_pull(hidden_ref[part, :], gain_ref[...], total)
+            gain_grad_ref[...] += gain_part
+            result = base + pulled
+            passed_on = result.astype(jnp.bfloat16)
+        else:
+            result = base + total
+            if follows:
+                passed_on = (norm_stats(result)[0] * gain_ref[...]).astype(jnp.bfloat16)
+        sum_ref[part, :] = result
+        if follows:
+            low_ref[part, :] = passed_on
+            next_out_ref[part, :] = matmul(passed_on, next_ref[...]).astype(jnp.bfloat16)
+        return carry
+
+    lax.fori_loop(0, rows // cut, finish, 0)
+
+
+def row_step(x, weights, at, base, gain_row, collective_id, hidden=None, follow=None):
+    rows, width = base.shape
+    units = x.shape[1]
+    backward, follows = hidden is not None, follow is not None
+    whole = pl.BlockSpec((rows, width), lambda step: (0, 0))
+    narrow = pl.BlockSpec((rows, units), lambda step: (0, 0))
+    line = pl.BlockSpec((1, width), lambda step: (0, 0))
+    matrix = lambda which: pl.BlockSpec((None, width, units), lambda step: (which, 0, 0))
+    args, in_specs = [x, weights, base, gain_row], [narrow, matrix(at), whole, line]
+    out_specs, out_shape = [whole], [jax.ShapeDtypeStruct((rows, width), jnp.float32)]
+    if backward:
+        args.append(hidden)
+        in_specs.append(whole)
+    if follows:
+        args.append(weights)
+        in_specs.append(matrix(follow))
+        out_specs += [whole, narrow]
+        out_shape += [
+            jax.ShapeDtypeStruct((rows, width), jnp.bfloat16), jax.ShapeDtypeStruct((rows, units), jnp.bfloat16)
+        ]
+    if backward:
+        out_specs.append(line)
+        out_shape.append(jax.ShapeDtypeStruct((1, width), jnp.float32))
+    cuts = 4
+    return pl.pallas_call(
+        partial(row_kernel, backward, follows),
+        grid=(1,),
+        in_specs=in_specs,
+        out_specs=out_specs,
+        out_shape=out_shape,
+        scratch_shapes=[
+            pltpu.VMEM((rows, width), jnp.bfloat16),
+            pltpu.VMEM((rows, width), jnp.bfloat16),
+            pltpu.SemaphoreType.DMA((cuts,)),
+            pltpu.SemaphoreType.DMA((cuts,)),
+        ],
+        compiler_params=pltpu.CompilerParams(
+            collective_id=collective_id, has_side_effects=True, vmem_limit_bytes=63 * 1024 * 1024
+        ),
+        cost_estimate=worth(1),
+        name="row_step",
+    )(*args)
 
 
 def heads_of(block):
@@ -706,6 +944,7 @@
             jax.ShapeDtypeStruct(queries.shape, jnp.bfloat16),
             jax.ShapeDtypeStruct((streams, width // LANES, 8, rows), jnp.float32),
         ],
+        cost_estimate=worth(1),
         name="attend",
     )(offsets, queries, keys, values)
 
@@ -723,6 +962,7 @@
             jax.ShapeDtypeStruct(keys.shape, jnp.bfloat16),
             jax.ShapeDtypeStruct(keys.shape, jnp.bfloat16),
         ],
+        cost_estimate=worth(1),
         name="attend_back",
     )(offsets, queries, keys, values, totals, grad_out)
 
@@ -756,6 +996,7 @@
         out_specs=[vmem] * len(arrays),
         scratch_shapes=[pltpu.SemaphoreType.DMA((len(arrays),)), pltpu.SemaphoreType.DMA((len(arrays),))],
         compiler_params=pltpu.CompilerParams(collective_id=collective_id, has_side_effects=True),
+        cost_estimate=worth(1),
         name="swap_heads",
     )(*arrays)
 
@@ -823,14 +1064,9 @@
             pltpu.SemaphoreType.DMA((4, longest - 1)),
         ],
         compiler_params=pltpu.CompilerParams(collective_id=collective_id, has_side_effects=True),
+        cost_estimate=worth(1),
         name="mesh_total",
     )(tile)
-
-
-def head_total(partials, collective_id):
-    low = partials.astype(jnp.bfloat16)
-    (there,) = swapped(collective_id, low)
-    return low.astype(jnp.float32) + there.astype(jnp.float32)
 
 
 def adamw_update(weight, moment_one, moment_two, gradient, step_rate, decay_rate):
@@ -867,19 +1103,18 @@
     text_rows = text_states.shape[1]
     bands, head = lax.axis_size("band"), lax.axis_index("head")
     shard_rows, width = proj_master.shape[1:]
-    shard = jnp.concatenate([proj_master, out_master]).astype(jnp.bfloat16)
+    chunks = mlp_master.shape[2] // width
+    up_cut = mlp_master[0].reshape(shard_rows, chunks, width).transpose(1, 0, 2)
+    shard = jnp.concatenate([proj_master, out_master, up_cut]).astype(jnp.bfloat16)
     gain_low = gain_master.astype(jnp.bfloat16).astype(jnp.float32)
     gain_tile = jnp.pad(gain_low, ((0, 5), (0, LANES - shard_rows)))
     both = jnp.concatenate([tokens, text_states], axis=1)
     context = lax.dynamic_index_in_dim(both, head, 0, keepdims=False)
     gathered, gain_tiles, passed = gather_weights(bands, shard, gain_tile, context, 1)
-    w_up = lax.all_gather(mlp_master[0].astype(jnp.bfloat16), "band", axis=0, tiled=True)
     down_low, gain_tiles = lax.optimization_barrier((mlp_master[1].astype(jnp.bfloat16), gain_tiles))
     w_down = lax.all_gather(down_low, "band", axis=0, tiled=True)
     weights = gathered.reshape(shard.shape[0], model_width, width)
-    w_query, w_key, w_value, w_cross, w_text_key, w_text_value, w_self_out, w_cross_out = (
-        weights[at] for at in range(8)
-    )
+    w_query, w_key, w_value, _, w_text_key, w_text_value, _, w_cross_out = (weights[at] for at in range(8))
     gains = gain_tiles.reshape(bands, 8, LANES)[:, :3, :shard_rows].transpose(1, 0, 2).reshape(3, model_width)
 
     offsets = earlier[:, 0]
@@ -900,9 +1135,10 @@
     values = matmul(normed_all, w_value).astype(jnp.bfloat16).reshape(reach_shape)
     attended, self_totals = attention(queries, keys, values, offsets, True)
     attended = attended.reshape(row_count, width)
-    hidden_one = inputs + head_total(matmul_t(attended, w_self_out), 3)
-    normed_two = norm_rows(hidden_one, gains[1]).astype(jnp.bfloat16)
-    cross_queries = matmul(normed_two, w_cross).astype(jnp.bfloat16).reshape(row_shape)
+    hidden_one, normed_two, cross_queries = row_step(
+        attended, weights, 6, tokens.reshape(row_count, model_width), gains[1:2], 3, follow=3
+    )
+    cross_queries = cross_queries.reshape(row_shape)
     caption = text_states
     for behind in range(1, SEQ_BANDS):
         caption = jnp.where((offsets == behind)[:, None, None], passed[:, behind - 1, band_rows:], caption)
@@ -911,28 +1147,14 @@
     cross_values = matmul(caption, w_text_value).astype(jnp.bfloat16).reshape(text_shape)
     crossed, cross_totals = attention(cross_queries, cross_keys, cross_values, offsets, False)
     crossed = crossed.reshape(row_count, width)
-    hidden_two = hidden_one + head_total(matmul_t(crossed, w_cross_out), 4)
-    normed_three = norm_rows(hidden_two, gains[2]).astype(jnp.bfloat16)
-    before = matmul(normed_three, w_up)
-    gelu = partial(jax.nn.gelu, approximate=False)
-    activated = gelu(before).astype(jnp.bfloat16)
-    mlp_out = matmul_t(activated, w_down)
-    block_out = (hidden_two + head_total(mlp_out, 5)).astype(jnp.bfloat16).reshape(tokens.shape)
-
-    incoming_low = cotangent.reshape(row_count, model_width)
-    incoming = incoming_low.astype(jnp.float32)
-    grad_down = inner_t(incoming_low, activated).astype(jnp.bfloat16)
-    _, gelu_pull = jax.vjp(gelu, before)
-    grad_before = gelu_pull(matmul(incoming_low, w_down))[0].astype(jnp.bfloat16)
-    grad_up = inner_t(normed_three, grad_before).astype(jnp.bfloat16)
-    grad_before, grad_up, grad_down = lax.optimization_barrier((grad_before, grad_up, grad_down))
-    mlp_grad = jnp.stack(
-        [lax.psum_scatter(part, "band", scatter_dimension=0, tiled=True) for part in (grad_up, grad_down)]
-    ).astype(jnp.float32)
-    grad_normed_three = head_total(matmul_t(grad_before, w_up), 6)
-    _, pull_three = jax.vjp(norm_rows, hidden_two, gains[2])
-    back_two, gain_grad_three = pull_three(grad_normed_three)
-    grad_two = incoming + back_two
+    (hidden_two,) = row_step(crossed, weights, 7, hidden_one, gains[2:3], 4)
+    incoming = cotangent.reshape(row_count, model_width)
+    block_out, grad_two, gain_grad_three, grad_up, grad_down = mlp_both_ways(
+        hidden_two, incoming, gains[2:3], weights, 8, w_down, 5
+    )
+    block_out = block_out.reshape(tokens.shape)
+    gain_grad_three = gain_grad_three[0]
+    down_sum = lax.psum_scatter(grad_down, "band", scatter_dimension=0, tiled=True).astype(jnp.float32)
     grad_two_low = grad_two.astype(jnp.bfloat16)
     grad_cross_out = inner_t(grad_two_low, crossed)
     grad_crossed = matmul(grad_two_low, w_cross_out).astype(jnp.bfloat16).reshape(row_shape)
@@ -944,13 +1166,12 @@
     grad_cv = grad_cv.reshape(streams * text_rows, width)
     text_part = (matmul_t(grad_ck, w_text_key) + matmul_t(grad_cv, w_text_value)).astype(jnp.bfloat16)
     text_part = text_part.reshape(text_states.shape)
-    grad_normed_two = head_total(matmul_t(grad_cq, w_cross), 7)
-    _, pull_two = jax.vjp(norm_rows, hidden_one, gains[1])
-    back_one, gain_grad_two = pull_two(grad_normed_two)
-    grad_one = grad_two + back_one
-    grad_one_low = grad_one.astype(jnp.bfloat16)
+    grad_one, grad_one_low, grad_attended, gain_grad_two = row_step(
+        grad_cq, weights, 3, grad_two, gains[1:2], 7, hidden=hidden_one, follow=6
+    )
+    gain_grad_two = gain_grad_two[0]
     grad_self_out = inner_t(grad_one_low, attended)
-    grad_attended = matmul(grad_one_low, w_self_out).astype(jnp.bfloat16).reshape(row_shape)
+    grad_attended = grad_attended.reshape(row_shape)
     grad_queries, grad_keys, grad_values = attention_back(
         queries, keys, values, offsets, self_totals, grad_attended, True
     )
@@ -972,7 +1193,7 @@
 
     flat = lambda part: part.reshape(-1, width)
     grads = [
-        part.astype(jnp.bfloat16)
+        part.astype(jnp.bfloat16)[None]
         for part in (
             inner_t(normed_one, grad_queries),
             inner_t(normed_all, flat(grad_keys)),
@@ -984,6 +1205,8 @@
             grad_cross_out,
         )
     ]
+    grads.append(grad_up)
+    returned, down_sum = lax.optimization_barrier((returned, down_sum))
     summed, came_back = reduce_grads(bands, grads, returned, 2)
     came_low = came_back.astype(jnp.bfloat16)
     (came_there,) = swapped(9, came_low)
@@ -995,7 +1218,7 @@
     back_zero, gain_grad_one = pull_one(grad_normed_one)
     grad_tokens = (grad_one + back_zero).reshape(tokens.shape)
 
-    squares = jnp.sum(summed * summed) + jnp.sum(mlp_grad * mlp_grad)
+    squares = jnp.sum(summed * summed) + jnp.sum(down_sum * down_sum)
     gain_rows = jnp.stack([gain_grad_one, gain_grad_two, gain_grad_three]).reshape(-1, LANES)
     tile = jnp.concatenate([gain_rows, jnp.full((8, LANES), squares)])
     tile = mesh_total(bands, tile, 10)
@@ -1003,6 +1226,8 @@
     grad_norm = jnp.sqrt(tile[-1, 0] + jnp.sum(gain_total * gain_total))
     gain_grad = lax.dynamic_slice_in_dim(gain_total, lax.axis_index("band") * shard_rows, shard_rows, 1)
     proj_grad, out_grad = summed[:6], summed[6:8]
+    up_sum = summed[8:].transpose(1, 0, 2).reshape(down_sum.shape)
+    mlp_grad = jnp.stack([up_sum, down_sum])
     factor = jnp.minimum(1.0, CLIP / grad_norm)
     matrix_rate = 2.0 * D ** (-0.5)
     new_proj = adamw_update(

time: 668 us -> 618 us (0.925)
  matrix products: 104 us -> 41.5 us
  waiting for transfers between devices: 0.1 us -> 19.8 us
  other arithmetic: 57.9 us -> 42.5 us
  Pallas kernels: 446 us -> 456 us
    pallas_call x1 -> x5, Pallas kernels: 190 us -> 223 us  [the longest x1 172 us: reduce_grads(): pl.pallas_call(partial(reduce_kernel, dims, len(grads), has_context), out...]
    dot_general x10 -> x5, matrix products: 36.5 us -> 8.18 us  [matmul_t(): lax.dot_general(former, latter, (((1,), (1,)), ((), ())), preferred_eleme...]
    dot_general x10 -> x6, matrix products: 41.7 us -> 14.3 us  [matmul(): return jnp.dot(former, latter, preferred_element_type=jnp.float32)]
    pallas_call x7 -> x2, Pallas kernels: 39.9 us -> 15.3 us  [swapped(): pl.pallas_call(partial(swap_kernel, len(arrays)), out_shape=[jax.ShapeDty...]
    reduce_scatter x2 -> x1, waiting for transfers between devices: 0.01 us -> 10.5 us  [local(): lax.psum_scatter(grad_down, 'band', scatter_dimension=0, tiled=True)]
    all_gather x1, waiting for transfers between devices: 0.01 us -> 9.26 us  [local(): w_down = lax.all_gather(down_low, 'band', axis=0, tiled=True)]
    unnamed x180 -> x152, local copies, waits for them, and re-layouts: 18.6 us -> 10.7 us
    reduce_sum x3 -> x1, other arithmetic: 8.53 us -> 1.1 us  [norm_rows(): return centre * lax.rsqrt(spread + EPS) * gain_row]
  transfers between devices with their start and end apart: 4 -> 2, of which waited for: 0 -> 2; matrix products, arithmetic and copies ran while one was open for 22% -> 11% of each run, Pallas kernels for 65% -> 12%
where the time goes in v4:
time: 618 us; the launch traced here: 612 us
  Pallas kernels  456 us (74%)
  other arithmetic  42.5 us (7%)
  matrix products  41.5 us (7%)
  local copies, waits for them, and re-layouts  33.3 us (5%)
  waiting for transfers between devices  19.8 us (3%)
  between operations  19 us (3%)
    pallas_call x1, Pallas kernels, reduce_grads(): pl.pallas_call(partial(reduce_kernel, dims, len(grads), has_context), out...  172 us
    pallas_call x1, Pallas kernels, gather_weights(): pl.pallas_call(partial(gather_kernel, dims, has_context), out_shape=out_s...  168 us
    pallas_call x1, Pallas kernels, mlp_both_ways(): pl.pallas_call(mlp_kernel, grid=(units // cut,), in_specs=[whole, whole,...  27.2 us
    pallas_call x3, Pallas kernels, row_step(): pl.pallas_call(partial(row_kernel, backward, follows), grid=(1,), in_spec...  23.7 us
    pallas_call x2, Pallas kernels, attention_back(): pl.pallas_call(partial(by_offset, attend_back_body, causal), grid=(stream...  19.1 us
    dot_general x8, matrix products, inner_t(): lax.dot_general(former, latter, (((0,), (0,)), ((), ())), preferred_eleme...  19 us
    pallas_call x2, Pallas kernels, attention(): pl.pallas_call(partial(by_offset, attend_body, causal), grid=(streams, wi...  17.6 us
    pallas_call x2, Pallas kernels, swapped(): pl.pallas_call(partial(swap_kernel, len(arrays)), out_shape=[jax.ShapeDty...  15.3 us
  transfers between devices with their start and end apart: 2, of which 2 were waited for; matrix products, arithmetic and copies ran while one was open for 11% of the time, Pallas kernels for 12%

profile of v4, /device:TPU:0, one launch (start us, length us, event | category | flops | bytes accessed | tf_op | source)
XLA Modules:
  0.0 612.5 jit_solution(7266469831489256271)
XLA Ops:
  7.3 1.4 convert.21
  11.3 1.0 pad_maximum_fusion.2.refs_0_
  12.3 168.2 %gather_weights.1 = (bf16[12,4,2,2,64,512]{5,4,3,2,1,0:T(8,128)(2,1)}, f32[4,2,2,8,128]{4,3,2,1,0:T(8,128)}, bf16[2,3,384,1024]{3,2,1,0:T(8,128)(2,1)}) custom-call(bf16[12,64,512]{2,1,0:T(8,128)(2,1)} %pad_maximum_fusion.2.refs_0_, f32[8,128]{1,0:T(8,128)} %pad_convert_fusion.refs_1_, bf16[384,1024]{1,0:T(8,128)(2,1)} %fusion.22.refs_2_), custom_call_target="tpu_custom_call" | custom-call | flops 199999995904 | tf_op jit(solution)/shard_map/gather_weights/pallas_call | solution.py:311
  180.5 4.2 slice.101
  184.8 2.7 convert_reduce_fusion
  187.8 1.6 fusion.2
  189.4 1.7 fusion.5
  191.1 2.0 copy-done.18
  194.6 4.8 fusion.36
  199.5 1.8 convolution_convert_fusion.9
  201.3 3.7 convolution_convert_fusion
  205.0 3.7 convolution_convert_fusion.1
  208.7 9.5 %attend.2 = (bf16[2,256,512]{2,1,0:T(8,128)(2,1)}, f32[2,4,8,256]{3,2,1,0:T(8,128)}) custom-call(s32[2]{0:T(128)} %bitcast.244, bf16[2,256,512]{2,1,0:T(8,128)(2,1)} %bitcast.207, bf16[2,4,256,512]{3,2,1,0:T(8,128)(2,1)} %bitcast.187, bf16[2,4,256,512]{3,2,1,0:T(8,128)(2,1)} %bitcast.185), custom_call_target="tpu_custom_call" | custom-call | flops 1000000000 | tf_op jit(solution)/shard_map/attend/pallas_call | solution.py:938
  218.3 7.6 %row_step.3 = (f32[512,1024]{1,0:T(8,128)}, bf16[512,1024]{1,0:T(8,128)(2,1)}, bf16[512,512]{1,0:T(8,128)(2,1)}) custom-call(bf16[512,512]{1,0:T(8,128)(2,1)} %bitcast.227, bf16[12,1024,512]{2,1,0:T(8,128)(2,1)} %bitcast.165, bf16[512,1024]{1,0:T(8,128)(2,1)} %bitcast.171, f32[1,1024]{1,0:T(1,128)} %slice.110.refs_3_, bf16[12,1024,512]{2,1,0:T(8,128)(2,1)} %bitcast.166), custom_call_target="tpu_custom_call" | custom-call | flops 1000000000 | tf_op jit(solution)/shard_map/row_step/pallas_call | solution.py:821
  226.0 2.5 fusion.24
  228.5 1.1 convolution_convert_fusion.10
  229.6 1.1 convolution_convert_fusion.11
  230.8 8.0 %attend.3 = (bf16[2,256,512]{2,1,0:T(8,128)(2,1)}, f32[2,4,8,256]{3,2,1,0:T(8,128)}) custom-call(s32[2]{0:T(128)} %bitcast.245, bf16[2,256,512]{2,1,0:T(8,128)(2,1)} %bitcast.251, bf16[2,1,128,512]{3,2,1,0:T(8,128)(2,1)} %bitcast.234, bf16[2,1,128,512]{3,2,1,0:T(8,128)(2,1)} %bitcast.232), custom_call_target="tpu_custom_call" | custom-call | flops 1000000000 | tf_op jit(solution)/shard_map/attend/pallas_call | solution.py:938
  238.8 6.6 %row_step.4.hidden_ref = f32[512,1024]{1,0:T(8,128)} custom-call(bf16[512,512]{1,0:T(8,128)(2,1)} %bitcast.204, bf16[12,1024,512]{2,1,0:T(8,128)(2,1)} %bitcast.167, f32[512,1024]{1,0:T(8,128)} %get-tuple-element.56.refs_2_.refs_4_, f32[1,1024]{1,0:T(1,128)} %slice.117.refs_3_.gain_ref), custom_call_target="tpu_custom_call" | custom-call | flops 1000000000 | tf_op jit(solution)/shard_map/row_step/pallas_call | solution.py:821
  245.4 9.3 %all-gather.2.cloned.1.call-done.down_ref = bf16[1024,2048]{1,0:T(8,128)(2,1)} async-done(((bf16[64,2048]{1,0:T(8,128)(2,1)}), bf16[1024,2048]{1,0:T(8,128)(2,1)}) %all-gather.2.cloned.1.call-update) | async-done | bytes 4194320 | tf_op jit(solution)/shard_map/all_gather | solution.py:1115
  254.7 27.2 %mlp_both_ways.1 = (bf16[512,1024]{1,0:T(8,128)(2,1)}, f32[512,1024]{1,0:T(8,128)}, f32[1,1024]{1,0:T(1,128)}, bf16[4,1024,512]{2,1,0:T(8,128)(2,1)}, bf16[1024,2048]{1,0:T(8,128)(2,1)}) custom-call(f32[512,1024]{1,0:T(8,128)} %row_step.4.hidden_ref, bf16[512,1024]{1,0:T(8,128)(2,1)} %bitcast.224, f32[1,1024]{1,0:T(1,128)} %slice.117.refs_3_.gain_ref, ...), custom_call_target="tpu_custom_call" | custom-call | flops 1000000000 | tf_op jit(solution)/shard_map/mlp_both_ways/pallas_call | solution.py:715
  282.1 1.1 copy-done.2
  284.6 2.7 convolution_convert_fusion.8
  287.3 8.1 %attend_back.2 = (bf16[2,256,512]{2,1,0:T(8,128)(2,1)}, bf16[2,1,128,512]{3,2,1,0:T(8,128)(2,1)}, bf16[2,1,128,512]{3,2,1,0:T(8,128)(2,1)}) custom-call(s32[2]{0:T(128)} %bitcast.246, bf16[2,256,512]{2,1,0:T(8,128)(2,1)} %bitcast.252, bf16[2,1,128,512]{3,2,1,0:T(8,128)(2,1)} %bitcast.235, bf16[2,1,128,512]{3,2,1,0:T(8,128)(2,1)} %bitcast.233, ...), custom_call_target="tpu_custom_call" | custom-call | flops 1000000000 | tf_op jit(solution)/shard_map/attend_back/pallas_call | solution.py:955
  295.4 9.5 %row_step.5 = (f32[512,1024]{1,0:T(8,128)}, bf16[512,1024]{1,0:T(8,128)(2,1)}, bf16[512,512]{1,0:T(8,128)(2,1)}, f32[1,1024]{1,0:T(1,128)}) custom-call(bf16[512,512]{1,0:T(8,128)(2,1)} %bitcast.225, bf16[12,1024,512]{2,1,0:T(8,128)(2,1)} %bitcast.169, f32[512,1024]{1,0:T(8,128)} %get-tuple-element.60.refs_2_, f32[1,1024]{1,0:T(1,128)} %slice.110.refs_3_, ...), custom_call_target="tpu_custom_call" | custom-call | flops 1000000000 | tf_op jit(solution)/shard_map/row_step/pallas_call | solution.py:821
  304.9 11.0 %attend_back.3 = (bf16[2,256,512]{2,1,0:T(8,128)(2,1)}, bf16[2,4,256,512]{3,2,1,0:T(8,128)(2,1)}, bf16[2,4,256,512]{3,2,1,0:T(8,128)(2,1)}) custom-call(s32[2]{0:T(128)} %bitcast.247, bf16[2,256,512]{2,1,0:T(8,128)(2,1)} %bitcast.208, bf16[2,4,256,512]{3,2,1,0:T(8,128)(2,1)} %bitcast.188, bf16[2,4,256,512]{3,2,1,0:T(8,128)(2,1)} %bitcast.186, ...), custom_call_target="tpu_custom_call" | custom-call | flops 1000000000 | tf_op jit(solution)/shard_map/attend_back/pallas_call | solution.py:955
  315.9 4.1 fusion.41
  320.0 2.4 convolution_add_fusion
  327.3 1.3 pad_maximum_fusion.1.refs_0_
  328.8 1.2 copy-done.8
  329.9 1.6 fusion.10.refs_1_
  331.6 11.0 %swap_heads.2 = (bf16[2,384,1024]{2,1,0:T(8,128)(2,1)}, bf16[3,384,1024]{2,1,0:T(8,128)(2,1)}) custom-call(bf16[2,384,1024]{2,1,0:T(8,128)(2,1)} %pad_maximum_fusion.1.refs_0_, bf16[3,384,1024]{2,1,0:T(8,128)(2,1)} %fusion.10.refs_1_), custom_call_target="tpu_custom_call" | custom-call | flops 1000000000 | tf_op jit(solution)/shard_map/swap_heads/pallas_call | solution.py:992
  342.6 2.6 convolution_convert_fusion.3
  345.2 2.5 convolution_convert_fusion.2
  347.8 1.8 convolution_convert_fusion.5
  349.5 1.7 convolution_convert_fusion.6
  351.3 1.7 convolution_convert_fusion.7
  353.0 1.7 convolution_convert_fusion.4
  354.8 2.6 fusion.6.refs_9_
  357.4 1.1 copy-done.70
  358.5 3.6 bitcast_convert_fusion.1
  362.1 3.4 bitcast_convert_fusion
  365.4 10.5 %reduce-scatter.2.cloned.1.call-done = bf16[64,2048]{1,0:T(8,128)(2,1)} async-done(((bf16[1024,2048]{1,0:T(8,128)(2,1)}), bf16[64,2048]{1,0:T(8,128)(2,1)}) %reduce-scatter.2.cloned.1.call-update) | async-done | bytes 262160 | tf_op jit(solution)/shard_map/reduce_scatter | solution.py:1157
  376.0 1.8 convert_element_type.157
  377.8 171.9 %reduce_grads.1 = (f32[12,64,512]{2,1,0:T(8,128)}, f32[384,1024]{1,0:T(8,128)}) custom-call(bf16[1,4,2,2,64,512]{5,4,3,2,1,0:T(8,128)(2,1)} %bitcast.211, bf16[1,4,2,2,64,512]{5,4,3,2,1,0:T(8,128)(2,1)} %bitcast.212, bf16[1,4,2,2,64,512]{5,4,3,2,1,0:T(8,128)(2,1)} %bitcast.213, bf16[1,4,2,2,64,512]{5,4,3,2,1,0:T(8,128)(2,1)} %bitcast.210, ...), custom_call_target="tpu_custom_call" | custom-call | flops 1000000000 | tf_op jit(solution)/shard_map/reduce_grads/pallas_call | solution.py:571
  549.7 2.5 multiply_reduce_fusion.3
  552.2 1.8 multiply_reduce_fusion.4
  554.0 1.0 convert_element_type.158.refs_0_
  555.0 4.3 swap_heads.3
  559.4 1.4 select_bitcast_fusion.1
  561.5 1.0 convert_add_fusion.1
  563.4 1.1 multiply_reduce_fusion
  566.5 13.4 %mesh_total.1 = f32[32,128]{1,0:T(8,128)} custom-call(f32[32,128]{1,0:T(8,128)} %concatenate.24.in_ref), custom_call_target="tpu_custom_call" | custom-call | flops 1000000000 | tf_op jit(solution)/shard_map/mesh_total/pallas_call | solution.py:1055
  579.9 1.3 fusion.39
  581.2 1.2 slice.124
  582.4 1.9 slice_bitcast_fusion.3
  584.3 2.3 slice.141
  588.0 2.2 copy.45
  590.2 2.2 stack_reshape.3
  592.4 2.2 multiply_subtract_fusion.2
  594.7 3.6 multiply_subtract_fusion.1
  599.1 2.2 multiply_subtract_fusion
  601.3 2.0 fusion.12
  603.3 1.0 copy.63
  (189 shorter events, 14.2 us)
Async XLA Ops:
  7.2 2.5 copy-start.33
  7.2 247.5 %all-gather.2.cloned.1.call-start = ((), (), s32[]{:S(2)}) async-start(), calls=%async_computation.1 | async-start | bytes 4456448 | tf_op jit(solution)/shard_map/all_gather | solution.py:1115
  7.2 2.5 copy-start.47
  8.6 1.7 copy-start
  8.6 1.7 copy-start.36
  180.5 195.5 %reduce-scatter.2.cloned.1.call-start = ((), (), s32[]{:S(2)}) async-start(), calls=%async_computation.2 | async-start | bytes 4456448 | tf_op jit(solution)/shard_map/reduce_scatter | solution.py:1157
  180.5 4.2 copy-start.59
  180.5 4.3 copy-start.1
  184.8 4.6 copy-start.56
  184.8 2.7 copy-start.63
  184.8 3.0 copy-start.4
  191.1 2.0 copy-start.18
  193.2 6.3 %copy-start.45 = (bf16[2,1,256,1024]{3,2,1,0:T(8,128)(2,1)}, bf16[2,1,256,1024]{3,2,1,0:T(8,128)(2,1)S(1)}, u32[]{:S(2)}) copy-start(bf16[2,1,256,1024]{3,2,1,0:T(8,128)(2,1)S(1)} %slice.133) | copy-start | bytes 3145732
  194.6 6.7 %copy-start.19 = (bf16[2,4,256,1024]{3,2,1,0:T(8,128)(2,1)S(1)}, bf16[2,4,256,1024]{3,2,1,0:T(8,128)(2,1)}, u32[]{:S(2)}) copy-start(bf16[2,4,256,1024]{3,2,1,0:T(8,128)(2,1)} %copy-done.18) | copy-start | bytes 12582916
  199.5 5.5 copy-start.28
  199.5 5.5 copy-start.30
  199.5 5.5 copy-start.41
  218.3 7.6 %copy-start.64 = (s32[2,1]{0,1:T(1,128)S(1)}, s32[2,1]{0,1:T(1,128)}, u32[]{:S(2)}) copy-start(s32[2,1]{0,1:T(1,128)} %param.19) | copy-start | bytes 28
  218.3 7.7 %copy-start.37 = (bf16[2,128,1024]{2,1,0:T(8,128)(2,1)S(1)}, bf16[2,128,1024]{2,1,0:T(8,128)(2,1)}, u32[]{:S(2)}) copy-start(bf16[2,128,1024]{2,1,0:T(8,128)(2,1)} %param.17) | copy-start | bytes 1572868
  225.9 2.6 copy-start.12
  226.0 3.7 copy-start.14
  281.9 2.6 copy-start.65
  281.9 2.7 copy-start.6
  304.9 11.0 %copy-start.42 = (bf16[1,4,2,2,64,512]{5,4,3,2,1,0:T(8,128)(2,1)S(1)}, bf16[1,4,2,2,64,512]{5,4,3,2,1,0:T(8,128)(2,1)}, u32[]{:S(2)}) copy-start(bf16[1,4,2,2,64,512]{5,4,3,2,1,0:T(8,128)(2,1)} %copy-done.41) | copy-start | bytes 3145732
  315.9 4.1 copy-start.21
  315.9 4.1 copy-start.29
  322.4 1.3 copy-start.43
  323.0 1.3 copy-start.13
  323.0 1.4 copy-start.49
  324.2 1.3 copy-start.31
  324.2 1.4 copy-start.54
  324.9 1.4 copy-start.26
  342.6 2.7 copy-start.11
  342.6 5.2 copy-start.53
  342.6 5.2 copy-start.72
  345.2 4.3 copy-start.52
  345.2 4.3 copy-start.71
  349.5 1.7 copy-start.46
  349.5 1.7 copy-start.55
  351.3 1.8 copy-start.7
  351.3 1.8 copy-start.35
  351.3 3.5 copy-start.34
  353.0 1.7 copy-start.9
  354.8 2.6 copy-start.20
  354.8 3.7 copy-start.70
  358.5 3.6 copy-start.22
  549.7 4.3 copy-start.23
  559.3 1.5 copy-start.17
  559.4 1.6 copy-start.27
  559.4 2.1 copy-start.40
  562.5 2.0 copy-start.5
  584.3 8.1 %copy-start.48 = (f32[2,64,512]{2,1,0:T(8,128)S(1)}, f32[2,64,512]{2,1,0:T(8,128)}, u32[]{:S(2)}) copy-start(f32[2,64,512]{2,1,0:T(8,128)} %param.21) | copy-start | bytes 786436
  592.4 2.3 copy-start.24
  594.7 3.7 copy-start.61
  594.7 3.7 copy-start.68
  594.7 3.7 copy-start.69
  594.7 4.4 copy-start.25
  594.7 4.3 copy-start.32
  594.7 4.3 copy-start.39
  594.7 4.3 copy-start.50
  594.7 4.3 copy-start.51
  599.1 2.2 copy-start.38
  599.1 2.2 copy-start.62
  601.3 2.0 copy-start.44
  (11 other events, 12.8 us)
Sparse Core Ops, SparseCore 0:
  180.6 74.0 all-gather.1
  282.1 93.8 reduce-scatter.1

commit v5 on v4

--- a/solution.py
+++ b/solution.py
@@ -28,6 +28,7 @@
 MESH = pl.DeviceIdType.MESH
 ORDERS = ((2, 0, 1), (1, 0, 2))
 GROUP = 4
+PIECES = 6
 GAP = 2
 
 
@@ -115,9 +116,11 @@
             ctx_ref, prev_ref, up_sem.at[0], up_sem.at[1], device_id=(band + GROUP, head), device_id_type=MESH
         )
 
-    def peer_copy(back, source):
+    def peer_copy(back, piece_at, source):
+        cut = ctx_ref.shape[0] // PIECES
+        rows = pl.ds(piece_at * cut, cut)
         return pltpu.make_async_remote_copy(
-            source, ctx_out.at[head, back - 1], csend.at[back - 1], crecv.at[back - 1],
+            source.at[rows], ctx_out.at[head, back - 1, rows], csend.at[back - 1, piece_at], crecv.at[back - 1, piece_at],
             device_id=(base + (mine + back) % GROUP, head), device_id_type=MESH,
         )
 
@@ -178,24 +181,33 @@
     depth = len(stages[0])
 
     def context_step(t):
-        for back in range(1, GROUP):
-            @pl.when((t == back - 1) & (mine + back < GROUP))
+        for one in range(PIECES):
+            @pl.when(t == one)
             def _():
-                peer_copy(back, ctx_ref).start()
-        @pl.when((t == 2) & (band >= GROUP))
+                for back in range(1, GROUP):
+                    @pl.when(mine + back < GROUP)
+                    def _():
+                        peer_copy(back, one, ctx_ref).start()
+        @pl.when((t == 4) & (band >= GROUP))
         def _():
             pltpu.make_async_remote_copy(
                 ctx_ref, prev_ref, up_sem.at[0], up_sem.at[1], device_id=(band - GROUP, head), device_id_type=MESH
             ).wait_recv()
-        for back in range(1, GROUP):
-            @pl.when((t == GROUP - back + 1) & (mine + back >= GROUP) & (band >= GROUP))
+        for one in range(PIECES):
+            @pl.when((t == 4 + one) & (band >= GROUP))
             def _():
-                peer_copy(back, prev_ref).start()
-        for back in range(1, GROUP):
-            @pl.when((t == 7) & ((mine >= back) | (band >= GROUP)))
-            def _():
-                peer_copy(back, ctx_ref).wait_recv()
-                pair_copy(back).start()
+                for back in range(1, GROUP):
+                    @pl.when(mine + back >= GROUP)
+                    def _():
+                        peer_copy(back, one, prev_ref).start()
+        @pl.when(t == 13)
+        def _():
+            for back in range(1, GROUP):
+                @pl.when((mine >= back) | (band >= GROUP))
+                def _():
+                    for one in range(PIECES):
+                        peer_copy(back, one, ctx_ref).wait_recv()
+                    pair_copy(back).start()
 
     def gains_step(t):
         for stage in range(depth + 1):
@@ -253,7 +265,8 @@
                 pair_copy(back).wait_send()
             @pl.when((mine + back < GROUP) | (band >= GROUP))
             def _():
-                peer_copy(back, ctx_ref).wait_send()
+                for one in range(PIECES):
+                    peer_copy(back, one, ctx_ref).wait_send()
         @pl.when(band + GROUP < bands)
         def _():
             up_copy().wait_send()
@@ -303,8 +316,8 @@
         scratch += [
             pltpu.VMEM(context.shape, context.dtype),
             pltpu.SemaphoreType.DMA((2,)),
-            pltpu.SemaphoreType.DMA((GROUP - 1,)),
-            pltpu.SemaphoreType.DMA((GROUP - 1,)),
+            pltpu.SemaphoreType.DMA((GROUP - 1, PIECES)),
+            pltpu.SemaphoreType.DMA((GROUP - 1, PIECES)),
             pltpu.SemaphoreType.DMA((GROUP - 1,)),
             pltpu.SemaphoreType.DMA((GROUP - 1,)),
         ]
@@ -325,7 +338,7 @@
     count, refs = len(sources), refs[arrays:]
     if has_context:
         (back_ref, out_ref, back_out, gv, load_sem, last_ref, mid_ref, first_ref, send_sem, recv_sem,
-         landed, relay, from_up, csend, crecv, up_sem) = refs
+         landed, relay, from_up, csend, crecv, up_sem, pair_sem) = refs
     else:
         (out_ref, gv, load_sem, last_ref, mid_ref, first_ref, send_sem, recv_sem) = refs
     band, place = place_of(dims)
@@ -351,17 +364,27 @@
             extra.append((true, base + (mine + shift) % GROUP, head))
         extra.append((band + GROUP < bands, band + GROUP, head))
         extra.append((band >= GROUP, band - GROUP, head))
+        extra.append((true, band, 1 - head))
     greet(dims, place, band, head, extra)
 
-    def peer_copy(back):
+    def peer_copy(back, piece_at):
+        cut = relay.shape[0] // PIECES
+        rows = pl.ds(piece_at * cut, cut)
         return pltpu.make_async_remote_copy(
-            back_ref.at[back - 1], landed.at[back - 1], csend.at[back - 1], crecv.at[back - 1],
+            back_ref.at[back - 1, rows], landed.at[back - 1, rows],
+            csend.at[back - 1, piece_at], crecv.at[back - 1, piece_at],
             device_id=(base + (mine + GROUP - back) % GROUP, head), device_id_type=MESH,
         )
 
     def down_copy(target):
         return pltpu.make_async_remote_copy(
             relay, from_up, up_sem.at[0], up_sem.at[1], device_id=(target, head), device_id_type=MESH
+        )
+
+    def pair_copy(stream):
+        return pltpu.make_async_remote_copy(
+            back_out.at[stream], back_out.at[stream], pair_sem.at[0], pair_sem.at[1],
+            device_id=(band, 1 - head), device_id_type=MESH,
         )
 
     def slot(size, step, way):
@@ -473,36 +496,48 @@
                     if stage < depth:
                         send(m, color, *stages[color][stage])
         if has_context:
-            for back in range(1, GROUP):
-                @pl.when((t == back - 1) & ((mine >= back) | (band >= GROUP)))
+            for one in range(PIECES):
+                @pl.when(t == one)
                 def _():
-                    peer_copy(back).start()
-            @pl.when(t == 4)
+                    for back in range(1, GROUP):
+                        @pl.when((mine >= back) | (band >= GROUP))
+                        def _():
+                            peer_copy(back, one).start()
+            @pl.when(t == 8)
             def _():
                 for back in range(1, GROUP):
                     @pl.when((mine + back < GROUP) | (band >= GROUP))
                     def _():
-                        peer_copy(back).wait_recv()
+                        for one in range(PIECES):
+                            peer_copy(back, one).wait_recv()
                 @pl.when((mine > 0) & (band >= GROUP))
                 def _():
-                    for cut in range(0, relay.shape[0], 64):
-                        rows = pl.ds(cut, 64)
+                    def relayed(at, inner):
+                        rows = pl.ds(pl.multiple_of(at * 64, 64), 64)
                         total = landed[GROUP - 2, rows, :].astype(jnp.float32)
                         for back in range(1, GROUP - 1):
                             total = total + jnp.where(mine + back >= GROUP, landed[back - 1, rows, :].astype(jnp.float32), 0.0)
                         relay[rows, :] = total.astype(relay.dtype)
+                        return inner
+
+                    lax.fori_loop(0, relay.shape[0] // 64, relayed, 0)
                     down_copy(band - GROUP).start()
-            @pl.when(t == 8)
+            @pl.when(t == 13)
             def _():
                 @pl.when((mine > 0) & (band + GROUP < bands))
                 def _():
                     down_copy(band + GROUP).wait_recv()
-                for cut in range(0, relay.shape[0], 64):
-                    rows = pl.ds(cut, 64)
+
+                def settled(at, inner):
+                    rows = pl.ds(pl.multiple_of(at * 64, 64), 64)
                     total = jnp.where((mine > 0) & (band + GROUP < bands), from_up[rows, :].astype(jnp.float32), 0.0)
                     for back in range(1, GROUP):
                         total = total + jnp.where(mine + back < GROUP, landed[back - 1, rows, :].astype(jnp.float32), 0.0)
-                    back_out[rows, :] = total
+                    back_out[head, rows, :] = total.astype(back_out.dtype)
+                    return inner
+
+                lax.fori_loop(0, relay.shape[0] // 64, settled, 0)
+                pair_copy(head).start()
         return carry
 
     lax.fori_loop(0, count + depth, body, 0)
@@ -511,10 +546,13 @@
         for back in range(1, GROUP):
             @pl.when((mine >= back) | (band >= GROUP))
             def _():
-                peer_copy(back).wait_send()
+                for one in range(PIECES):
+                    peer_copy(back, one).wait_send()
         @pl.when((mine > 0) & (band >= GROUP))
         def _():
             down_copy(band - GROUP).wait_send()
+        pair_copy(head).wait_send()
+        pair_copy(1 - head).wait_recv()
 
     def drain(m, carry):
         for stage in range(depth):
@@ -559,13 +597,14 @@
         args.append(returned)
         in_specs.append(vmem)
         ctx_shape = returned.shape[1:]
-        out_shape.append(jax.ShapeDtypeStruct(ctx_shape, jnp.float32))
+        out_shape.append(jax.ShapeDtypeStruct((2, *ctx_shape), returned.dtype))
         scratch += [
             pltpu.VMEM(returned.shape, returned.dtype),
             pltpu.VMEM(ctx_shape, returned.dtype),
             pltpu.VMEM(ctx_shape, returned.dtype),
-            pltpu.SemaphoreType.DMA((GROUP - 1,)),
-            pltpu.SemaphoreType.DMA((GROUP - 1,)),
+            pltpu.SemaphoreType.DMA((GROUP - 1, PIECES)),
+            pltpu.SemaphoreType.DMA((GROUP - 1, PIECES)),
+            pltpu.SemaphoreType.DMA((2,)),
             pltpu.SemaphoreType.DMA((2,)),
         ]
     return pl.pallas_call(
@@ -1001,67 +1040,63 @@
     )(*arrays)
 
 
-def total_kernel(dims, in_ref, out_ref, *scratch):
-    slots, (send_sem, recv_sem) = scratch[:4], scratch[4:]
+def total_kernel(dims, in_ref, out_ref, near, far, send_sem, recv_sem):
+    head = lax.axis_index("head")
     band, place = place_of(dims)
-    head = lax.axis_index("head")
-    strides = strides_of(dims)
+    layer = dims[1] * dims[2]
+    inside = (band % layer) * 2 + head
     lines = [
-        (dims[axis], place[axis], lambda at, axis=axis: (band + (at - place[axis]) * strides[axis], head))
-        for axis in (2, 1, 0)
+        (near, layer * 2, inside, lambda at: (place[0] * layer + at // 2, at % 2)),
+        (far, dims[0], place[0], lambda at: (at * layer + band % layer, head)),
     ]
-    lines.append((2, head, lambda at: (band, at)))
     barrier = pltpu.get_barrier_semaphore()
-    for size, mine, device in lines:
+    for _, size, mine, device in lines:
         for shift in range(1, size):
             pl.semaphore_signal(barrier, inc=1, device_id=device((mine + shift) % size), device_id_type=MESH)
-    pl.semaphore_wait(barrier, sum(size - 1 for size, _, _ in lines))
-    out_ref[...] = in_ref[...]
-    rows = in_ref.shape[0]
-    for line, (size, mine, device) in enumerate(lines):
-        part = pl.ds(0, rows) if line < 3 else pl.ds(rows - 8, 8)
-        slots[line][mine] = out_ref[part, :]
-
-        def copy(shift):
+    pl.semaphore_wait(barrier, sum(size - 1 for _, size, _, _ in lines))
+    total = in_ref[...]
+    for line, (slots, size, mine, device) in enumerate(lines):
+        slots[mine] = total
+
+        def copy(there, shift):
             return pltpu.make_async_remote_copy(
-                slots[line].at[mine], slots[line].at[mine], send_sem.at[line, shift - 1], recv_sem.at[line, shift - 1],
-                device_id=device((mine + shift) % size), device_id_type=MESH,
-            )
-
-        def incoming(shift):
-            there = (mine + size - shift) % size
-            return pltpu.make_async_remote_copy(
-                slots[line].at[there], slots[line].at[there], send_sem.at[line, shift - 1], recv_sem.at[line, shift - 1],
+                slots.at[mine], slots.at[mine], send_sem.at[line, shift - 1], recv_sem.at[line, shift - 1],
                 device_id=device(there), device_id_type=MESH,
             )
 
+        def incoming(there, shift):
+            return pltpu.make_async_remote_copy(
+                slots.at[there], slots.at[there], send_sem.at[line, shift - 1], recv_sem.at[line, shift - 1],
+                device_id=device(there), device_id_type=MESH,
+            )
+
         for shift in range(1, size):
-            copy(shift).start()
+            copy((mine + shift) % size, shift).start()
         for shift in range(1, size):
-            incoming(shift).wait_recv()
-        total = slots[line][0]
+            incoming((mine + size - shift) % size, shift).wait_recv()
+        total = slots[0]
         for at in range(1, size):
-            total = total + slots[line][at]
-        out_ref[part, :] = total
+            total = total + slots[at]
         for shift in range(1, size):
-            copy(shift).wait_send()
+            copy((mine + shift) % size, shift).wait_send()
+    out_ref[...] = total
 
 
 def mesh_total(bands, tile, collective_id):
     dims = band_dims(bands)
-    longest = max(*dims, 2)
+    near = dims[1] * dims[2] * 2
+    longest = max(dims[0], near)
     vmem = pl.BlockSpec(memory_space=pltpu.VMEM)
-    rows = tile.shape[0]
     return pl.pallas_call(
         partial(total_kernel, dims),
         out_shape=jax.ShapeDtypeStruct(tile.shape, tile.dtype),
         in_specs=[vmem],
         out_specs=vmem,
         scratch_shapes=[
-            *(pltpu.VMEM((dims[axis], rows, LANES), tile.dtype) for axis in (2, 1, 0)),
-            pltpu.VMEM((2, 8, LANES), tile.dtype),
-            pltpu.SemaphoreType.DMA((4, longest - 1)),
-            pltpu.SemaphoreType.DMA((4, longest - 1)),
+            pltpu.VMEM((near, *tile.shape), tile.dtype),
+            pltpu.VMEM((dims[0], *tile.shape), tile.dtype),
+            pltpu.SemaphoreType.DMA((2, longest - 1)),
+            pltpu.SemaphoreType.DMA((2, longest - 1)),
         ],
         compiler_params=pltpu.CompilerParams(collective_id=collective_id, has_side_effects=True),
         cost_estimate=worth(1),
@@ -1208,10 +1243,7 @@
     grads.append(grad_up)
     returned, down_sum = lax.optimization_barrier((returned, down_sum))
     summed, came_back = reduce_grads(bands, grads, returned, 2)
-    came_low = came_back.astype(jnp.bfloat16)
-    (came_there,) = swapped(9, came_low)
-    came_both = jnp.stack([jnp.where(head == 0, came_low, came_there), jnp.where(head == 0, came_there, came_low)])
-    back_all = own_back + came_both.astype(jnp.float32)
+    back_all = own_back + came_back.astype(jnp.float32)
     grad_normed_one = back_all[:, :band_rows].reshape(row_count, model_width)
     grad_text = back_all[:, band_rows:]
     _, pull_one = jax.vjp(norm_rows, inputs, gains[0])
@@ -1222,7 +1254,7 @@
     gain_rows = jnp.stack([gain_grad_one, gain_grad_two, gain_grad_three]).reshape(-1, LANES)
     tile = jnp.concatenate([gain_rows, jnp.full((8, LANES), squares)])
     tile = mesh_total(bands, tile, 10)
-    gain_total = tile[:-8].reshape(3, model_width)
+    gain_total = 0.5 * tile[:-8].reshape(3, model_width)
     grad_norm = jnp.sqrt(tile[-1, 0] + jnp.sum(gain_total * gain_total))
     gain_grad = lax.dynamic_slice_in_dim(gain_total, lax.axis_index("band") * shard_rows, shard_rows, 1)
     proj_grad, out_grad = summed[:6], summed[6:8]

time: 618 us -> 585 us (0.947)
  Pallas kernels: 456 us -> 421 us
    pallas_call x1, Pallas kernels: 168 us -> 148 us  [gather_weights(): pl.pallas_call(partial(gather_kernel, dims, has_context), out_shape=out_s...]
    pallas_call x1, Pallas kernels: 172 us -> 162 us  [reduce_grads(): pl.pallas_call(partial(reduce_kernel, dims, len(grads), has_context), out...]
    pallas_call x2 -> x1, Pallas kernels: 15.3 us -> 11 us  [swapped(): pl.pallas_call(partial(swap_kernel, len(arrays)), out_shape=[jax.ShapeDty...]
  transfers between devices with their start and end apart: 2 -> 2, of which waited for: 2 -> 2; matrix products, arithmetic and copies ran while one was open for 11% -> 12% of each run, Pallas kernels for 12% -> 12%
where the time goes in v5:
time: 585 us; the launch traced here: 579 us
  Pallas kernels  421 us (72%)
  other arithmetic  41.6 us (7%)
  matrix products  40.4 us (7%)
  local copies, waits for them, and re-layouts  32.4 us (6%)
  waiting for transfers between devices  25 us (4%)
  between operations  19 us (3%)
    pallas_call x1, Pallas kernels, reduce_grads(): pl.pallas_call(partial(reduce_kernel, dims, len(grads), has_context), out...  162 us
    pallas_call x1, Pallas kernels, gather_weights(): pl.pallas_call(partial(gather_kernel, dims, has_context), out_shape=out_s...  148 us
    pallas_call x1, Pallas kernels, mlp_both_ways(): pl.pallas_call(mlp_kernel, grid=(units // cut,), in_specs=[whole, whole,...  27.4 us
    pallas_call x3, Pallas kernels, row_step(): pl.pallas_call(partial(row_kernel, backward, follows), grid=(1,), in_spec...  23.6 us
    pallas_call x2, Pallas kernels, attention_back(): pl.pallas_call(partial(by_offset, attend_back_body, causal), grid=(stream...  19.1 us
    dot_general x8, matrix products, inner_t(): lax.dot_general(former, latter, (((0,), (0,)), ((), ())), preferred_eleme...  18 us
    pallas_call x2, Pallas kernels, attention(): pl.pallas_call(partial(by_offset, attend_body, causal), grid=(streams, wi...  17.7 us
    dot_general x6, matrix products, matmul(): return jnp.dot(former, latter, preferred_element_type=jnp.float32)  14.3 us
  transfers between devices with their start and end apart: 2, of which 2 were waited for; matrix products, arithmetic and copies ran while one was open for 12% of the time, Pallas kernels for 12%

profile of v5, /device:TPU:0, one launch (start us, length us, event | category | flops | bytes accessed | tf_op | source)
XLA Modules:
  0.0 579.5 jit_solution(8571696134886733904)
XLA Ops:
  7.3 1.4 convert.21
  10.4 0.9 fusion.22.refs_2_
  11.3 1.0 pad_maximum_fusion.2.refs_0_
  12.3 147.8 %gather_weights.1 = (bf16[12,4,2,2,64,512]{5,4,3,2,1,0:T(8,128)(2,1)}, f32[4,2,2,8,128]{4,3,2,1,0:T(8,128)}, bf16[2,3,384,1024]{3,2,1,0:T(8,128)(2,1)}) custom-call(bf16[12,64,512]{2,1,0:T(8,128)(2,1)} %pad_maximum_fusion.2.refs_0_, f32[8,128]{1,0:T(8,128)} %pad_convert_fusion.refs_1_, bf16[384,1024]{1,0:T(8,128)(2,1)} %fusion.22.refs_2_), custom_call_target="tpu_custom_call" | custom-call | flops 199999995904 | tf_op jit(solution)/shard_map/gather_weights/pallas_call | solution.py:324
  160.2 4.2 slice.101
  164.5 2.7 convert_reduce_fusion
  167.3 1.6 fusion.2
  168.9 1.7 fusion.5
  170.6 2.0 copy-done.18
  172.7 0.8 slice.110.refs_3_
  174.2 4.8 fusion.36
  179.0 1.8 convolution_convert_fusion.9
  180.8 3.7 convolution_convert_fusion
  184.5 3.7 convolution_convert_fusion.1
  188.2 9.7 %attend.2 = (bf16[2,256,512]{2,1,0:T(8,128)(2,1)}, f32[2,4,8,256]{3,2,1,0:T(8,128)}) custom-call(s32[2]{0:T(128)} %bitcast.238, bf16[2,256,512]{2,1,0:T(8,128)(2,1)} %bitcast.201, bf16[2,4,256,512]{3,2,1,0:T(8,128)(2,1)} %bitcast.181, bf16[2,4,256,512]{3,2,1,0:T(8,128)(2,1)} %bitcast.179), custom_call_target="tpu_custom_call" | custom-call | flops 1000000000 | tf_op jit(solution)/shard_map/attend/pallas_call | solution.py:977
  197.9 7.6 %row_step.3 = (f32[512,1024]{1,0:T(8,128)}, bf16[512,1024]{1,0:T(8,128)(2,1)}, bf16[512,512]{1,0:T(8,128)(2,1)}) custom-call(bf16[512,512]{1,0:T(8,128)(2,1)} %bitcast.221, bf16[12,1024,512]{2,1,0:T(8,128)(2,1)} %bitcast.159, bf16[512,1024]{1,0:T(8,128)(2,1)} %bitcast.165, f32[1,1024]{1,0:T(1,128)} %slice.110.refs_3_, bf16[12,1024,512]{2,1,0:T(8,128)(2,1)} %bitcast.160), custom_call_target="tpu_custom_call" | custom-call | flops 1000000000 | tf_op jit(solution)/shard_map/row_step/pallas_call | solution.py:860
  205.6 2.1 fusion.24
  207.7 1.1 convolution_convert_fusion.10
  208.8 1.1 convolution_convert_fusion.11
  210.0 8.1 %attend.3 = (bf16[2,256,512]{2,1,0:T(8,128)(2,1)}, f32[2,4,8,256]{3,2,1,0:T(8,128)}) custom-call(s32[2]{0:T(128)} %bitcast.239, bf16[2,256,512]{2,1,0:T(8,128)(2,1)} %bitcast.245, bf16[2,1,128,512]{3,2,1,0:T(8,128)(2,1)} %bitcast.228, bf16[2,1,128,512]{3,2,1,0:T(8,128)(2,1)} %bitcast.226), custom_call_target="tpu_custom_call" | custom-call | flops 1000000000 | tf_op jit(solution)/shard_map/attend/pallas_call | solution.py:977
  218.0 6.6 %row_step.4.hidden_ref = f32[512,1024]{1,0:T(8,128)} custom-call(bf16[512,512]{1,0:T(8,128)(2,1)} %bitcast.198, bf16[12,1024,512]{2,1,0:T(8,128)(2,1)} %bitcast.161, f32[512,1024]{1,0:T(8,128)} %get-tuple-element.56.refs_2_.refs_4_, f32[1,1024]{1,0:T(1,128)} %slice.117.refs_3_.gain_ref), custom_call_target="tpu_custom_call" | custom-call | flops 1000000000 | tf_op jit(solution)/shard_map/row_step/pallas_call | solution.py:860
  224.6 13.5 %all-gather.2.cloned.1.call-done.down_ref = bf16[1024,2048]{1,0:T(8,128)(2,1)} async-done(((bf16[64,2048]{1,0:T(8,128)(2,1)}), bf16[1024,2048]{1,0:T(8,128)(2,1)}) %all-gather.2.cloned.1.call-update) | async-done | bytes 4194320 | tf_op jit(solution)/shard_map/all_gather | solution.py:1150
  238.1 27.4 %mlp_both_ways.1 = (bf16[512,1024]{1,0:T(8,128)(2,1)}, f32[512,1024]{1,0:T(8,128)}, f32[1,1024]{1,0:T(1,128)}, bf16[4,1024,512]{2,1,0:T(8,128)(2,1)}, bf16[1024,2048]{1,0:T(8,128)(2,1)}) custom-call(f32[512,1024]{1,0:T(8,128)} %row_step.4.hidden_ref, bf16[512,1024]{1,0:T(8,128)(2,1)} %bitcast.218, f32[1,1024]{1,0:T(1,128)} %slice.117.refs_3_.gain_ref, ...), custom_call_target="tpu_custom_call" | custom-call | flops 1000000000 | tf_op jit(solution)/shard_map/mlp_both_ways/pallas_call | solution.py:754
  265.7 1.1 copy-done.2
  268.2 2.7 convolution_convert_fusion.8
  271.0 8.1 %attend_back.2 = (bf16[2,256,512]{2,1,0:T(8,128)(2,1)}, bf16[2,1,128,512]{3,2,1,0:T(8,128)(2,1)}, bf16[2,1,128,512]{3,2,1,0:T(8,128)(2,1)}) custom-call(s32[2]{0:T(128)} %bitcast.240, bf16[2,256,512]{2,1,0:T(8,128)(2,1)} %bitcast.246, bf16[2,1,128,512]{3,2,1,0:T(8,128)(2,1)} %bitcast.229, bf16[2,1,128,512]{3,2,1,0:T(8,128)(2,1)} %bitcast.227, ...), custom_call_target="tpu_custom_call" | custom-call | flops 1000000000 | tf_op jit(solution)/shard_map/attend_back/pallas_call | solution.py:994
  279.0 9.5 %row_step.5 = (f32[512,1024]{1,0:T(8,128)}, bf16[512,1024]{1,0:T(8,128)(2,1)}, bf16[512,512]{1,0:T(8,128)(2,1)}, f32[1,1024]{1,0:T(1,128)}) custom-call(bf16[512,512]{1,0:T(8,128)(2,1)} %bitcast.219, bf16[12,1024,512]{2,1,0:T(8,128)(2,1)} %bitcast.163, f32[512,1024]{1,0:T(8,128)} %get-tuple-element.60.refs_2_, f32[1,1024]{1,0:T(1,128)} %slice.110.refs_3_, ...), custom_call_target="tpu_custom_call" | custom-call | flops 1000000000 | tf_op jit(solution)/shard_map/row_step/pallas_call | solution.py:860
  288.5 11.0 %attend_back.3 = (bf16[2,256,512]{2,1,0:T(8,128)(2,1)}, bf16[2,4,256,512]{3,2,1,0:T(8,128)(2,1)}, bf16[2,4,256,512]{3,2,1,0:T(8,128)(2,1)}) custom-call(s32[2]{0:T(128)} %bitcast.241, bf16[2,256,512]{2,1,0:T(8,128)(2,1)} %bitcast.202, bf16[2,4,256,512]{3,2,1,0:T(8,128)(2,1)} %bitcast.182, bf16[2,4,256,512]{3,2,1,0:T(8,128)(2,1)} %bitcast.180, ...), custom_call_target="tpu_custom_call" | custom-call | flops 1000000000 | tf_op jit(solution)/shard_map/attend_back/pallas_call | solution.py:994
  299.5 4.1 fusion.40
  303.7 2.4 convolution_add_fusion
  310.0 1.0 copy-done.16
  311.0 1.3 pad_maximum_fusion.1.refs_0_
  312.4 1.2 copy-done.8
  313.6 1.7 fusion.10.refs_1_
  315.3 11.0 %swap_heads.1 = (bf16[2,384,1024]{2,1,0:T(8,128)(2,1)}, bf16[3,384,1024]{2,1,0:T(8,128)(2,1)}) custom-call(bf16[2,384,1024]{2,1,0:T(8,128)(2,1)} %pad_maximum_fusion.1.refs_0_, bf16[3,384,1024]{2,1,0:T(8,128)(2,1)} %fusion.10.refs_1_), custom_call_target="tpu_custom_call" | custom-call | flops 1000000000 | tf_op jit(solution)/shard_map/swap_heads/pallas_call | solution.py:1031
  326.3 2.7 convolution_convert_fusion.2
  329.0 1.4 convolution_convert_fusion.3
  330.4 1.8 convolution_convert_fusion.5
  332.2 1.7 convolution_convert_fusion.6
  334.0 1.7 convolution_convert_fusion.7
  335.7 1.7 convolution_convert_fusion.4
  337.4 2.6 fusion.6.refs_9_
  340.1 1.1 copy-done.22
  341.2 3.6 bitcast_convert_fusion
  344.7 3.4 bitcast_convert_fusion.1
  348.1 11.5 %reduce-scatter.2.cloned.1.call-done = bf16[64,2048]{1,0:T(8,128)(2,1)} async-done(((bf16[1024,2048]{1,0:T(8,128)(2,1)}), bf16[64,2048]{1,0:T(8,128)(2,1)}) %reduce-scatter.2.cloned.1.call-update) | async-done | bytes 262160 | tf_op jit(solution)/shard_map/reduce_scatter | solution.py:1192
  359.6 1.8 convert_element_type.154
  361.4 161.6 %reduce_grads.1 = (f32[12,64,512]{2,1,0:T(8,128)}, bf16[2,384,1024]{2,1,0:T(8,128)(2,1)}) custom-call(bf16[1,4,2,2,64,512]{5,4,3,2,1,0:T(8,128)(2,1)} %bitcast.205, bf16[1,4,2,2,64,512]{5,4,3,2,1,0:T(8,128)(2,1)} %bitcast.207, bf16[1,4,2,2,64,512]{5,4,3,2,1,0:T(8,128)(2,1)} %bitcast.206, bf16[1,4,2,2,64,512]{5,4,3,2,1,0:T(8,128)(2,1)} %bitcast.204, ...), custom_call_target="tpu_custom_call" | custom-call | flops 1000000000 | tf_op jit(solution)/shard_map/reduce_grads/pallas_call | solution.py:610
  523.0 2.5 multiply_reduce_fusion.3
  525.5 1.8 multiply_reduce_fusion.4
  527.3 3.0 convert_add_fusion.1
  531.1 1.1 multiply_reduce_fusion
  534.1 12.7 %mesh_total.1 = f32[32,128]{1,0:T(8,128)} custom-call(f32[32,128]{1,0:T(8,128)} %concatenate.24.in_ref), custom_call_target="tpu_custom_call" | custom-call | flops 1000000000 | tf_op jit(solution)/shard_map/mesh_total/pallas_call | solution.py:1090
  546.9 1.3 slice_multiply_fusion.2
  548.2 1.2 slice.124
  549.4 1.9 slice_bitcast_fusion.3
  551.2 2.3 slice.141
  555.0 2.2 copy.44
  557.2 2.2 stack_reshape.3
  559.4 2.2 multiply_subtract_fusion.2
  561.7 3.6 multiply_subtract_fusion.1
  566.1 2.2 multiply_subtract_fusion
  568.3 2.0 fusion.12
  570.3 1.0 copy.61
  (182 shorter events, 10.6 us)
Async XLA Ops:
  7.2 2.5 copy-start.32
  7.2 230.9 %all-gather.2.cloned.1.call-start = ((), (), s32[]{:S(2)}) async-start(), calls=%async_computation.1 | async-start | bytes 4456448 | tf_op jit(solution)/shard_map/all_gather | solution.py:1150
  7.2 2.5 copy-start.45
  8.6 1.7 copy-start
  8.6 1.7 copy-start.35
  160.1 199.5 %reduce-scatter.2.cloned.1.call-start = ((), (), s32[]{:S(2)}) async-start(), calls=%async_computation.2 | async-start | bytes 4456448 | tf_op jit(solution)/shard_map/reduce_scatter | solution.py:1192
  160.1 4.2 copy-start.57
  160.2 4.3 copy-start.1
  164.5 4.4 copy-start.54
  164.5 2.7 copy-start.61
  164.5 2.9 copy-start.4
  170.6 2.0 copy-start.18
  172.7 6.3 %copy-start.43 = (bf16[2,1,256,1024]{3,2,1,0:T(8,128)(2,1)}, bf16[2,1,256,1024]{3,2,1,0:T(8,128)(2,1)S(1)}, u32[]{:S(2)}) copy-start(bf16[2,1,256,1024]{3,2,1,0:T(8,128)(2,1)S(1)} %slice.133) | copy-start | bytes 3145732
  174.2 6.7 %copy-start.19 = (bf16[2,4,256,1024]{3,2,1,0:T(8,128)(2,1)S(1)}, bf16[2,4,256,1024]{3,2,1,0:T(8,128)(2,1)}, u32[]{:S(2)}) copy-start(bf16[2,4,256,1024]{3,2,1,0:T(8,128)(2,1)} %copy-done.18) | copy-start | bytes 12582916
  179.0 5.5 copy-start.27
  179.0 5.5 copy-start.29
  179.0 5.5 copy-start.39
  197.9 7.6 %copy-start.62 = (s32[2,1]{0,1:T(1,128)S(1)}, s32[2,1]{0,1:T(1,128)}, u32[]{:S(2)}) copy-start(s32[2,1]{0,1:T(1,128)} %param.19) | copy-start | bytes 28
  197.9 7.6 %copy-start.36 = (bf16[2,128,1024]{2,1,0:T(8,128)(2,1)S(1)}, bf16[2,128,1024]{2,1,0:T(8,128)(2,1)}, u32[]{:S(2)}) copy-start(bf16[2,128,1024]{2,1,0:T(8,128)(2,1)} %param.17) | copy-start | bytes 1572868
  205.5 2.1 copy-start.12
  205.6 3.3 copy-start.14
  265.5 2.6 copy-start.63
  265.5 2.7 copy-start.6
  288.5 11.0 %copy-start.40 = (bf16[1,4,2,2,64,512]{5,4,3,2,1,0:T(8,128)(2,1)S(1)}, bf16[1,4,2,2,64,512]{5,4,3,2,1,0:T(8,128)(2,1)}, u32[]{:S(2)}) copy-start(bf16[1,4,2,2,64,512]{5,4,3,2,1,0:T(8,128)(2,1)} %copy-done.39) | copy-start | bytes 3145732
  299.5 4.1 copy-start.21
  299.5 4.1 copy-start.28
  306.6 1.3 copy-start.13
  306.6 1.4 copy-start.47
  307.8 1.3 copy-start.30
  307.8 1.4 copy-start.52
  308.6 1.4 copy-start.25
  326.3 2.7 copy-start.11
  326.3 4.2 copy-start.51
  326.3 4.2 copy-start.70
  329.0 3.2 copy-start.50
  329.0 3.2 copy-start.69
  332.2 1.7 copy-start.44
  332.2 1.7 copy-start.53
  333.9 1.8 copy-start.7
  333.9 1.8 copy-start.34
  333.9 3.5 copy-start.33
  335.7 1.7 copy-start.9
  337.4 2.6 copy-start.20
  337.4 3.8 copy-start.22
  341.2 3.6 copy-start.68
  523.0 4.3 copy-start.17
  523.0 4.3 copy-start.26
  527.3 3.0 copy-start.3
  527.3 3.0 copy-start.55
  527.3 3.0 copy-start.56
  530.3 1.8 copy-start.5
  551.2 8.1 %copy-start.46 = (f32[2,64,512]{2,1,0:T(8,128)S(1)}, f32[2,64,512]{2,1,0:T(8,128)}, u32[]{:S(2)}) copy-start(f32[2,64,512]{2,1,0:T(8,128)} %param.21) | copy-start | bytes 786436
  559.4 2.3 copy-start.23
  561.6 3.7 copy-start.59
  561.6 3.7 copy-start.66
  561.6 3.7 copy-start.67
  561.6 4.4 copy-start.24
  561.7 4.3 copy-start.31
  561.7 4.3 copy-start.38
  561.7 4.3 copy-start.48
  561.7 4.3 copy-start.49
  566.0 2.2 copy-start.37
  566.0 2.2 copy-start.60
  568.3 2.0 copy-start.42
  (9 other events, 10.4 us)
Sparse Core Ops, SparseCore 0:
  160.2 77.8 all-gather.1
  265.7 93.8 reduce-scatter.1

commit v6 on v5

--- a/solution.py
+++ b/solution.py
@@ -30,6 +30,7 @@
 GROUP = 4
 PIECES = 6
 GAP = 2
+REDUCE_GAP = 1
 
 
 def band_dims(bands):
@@ -337,7 +338,7 @@
     sources = [ref.at[one] for ref in refs[:arrays] for one in range(ref.shape[0])]
     count, refs = len(sources), refs[arrays:]
     if has_context:
-        (back_ref, out_ref, back_out, gv, load_sem, last_ref, mid_ref, first_ref, send_sem, recv_sem,
+        (back_ref, out_ref, back_out, squares_ref, gv, load_sem, last_ref, mid_ref, first_ref, send_sem, recv_sem,
          landed, relay, from_up, csend, crecv, up_sem, pair_sem) = refs
     else:
         (out_ref, gv, load_sem, last_ref, mid_ref, first_ref, send_sem, recv_sem) = refs
@@ -485,7 +486,7 @@
 
     def body(t, carry):
         for stage in range(depth, -1, -1):
-            m = t - stage
+            m = t - REDUCE_GAP * stage
             @pl.when((m >= 0) & (m < count))
             def _():
                 if stage == 0:
@@ -540,7 +541,18 @@
                 pair_copy(head).start()
         return carry
 
-    lax.fori_loop(0, count + depth, body, 0)
+    lax.fori_loop(0, count + REDUCE_GAP * depth, body, 0)
+
+    if has_context:
+        def add_squares(m, total):
+            block = out_ref[m]
+            for top in range(0, block.shape[0], 8):
+                for left in range(0, block.shape[1], LANES):
+                    part = block[top : top + 8, left : left + LANES]
+                    total = total + part * part
+            return total
+
+        squares_ref[...] = lax.fori_loop(0, count, add_squares, jnp.zeros(squares_ref.shape, jnp.float32))
 
     if has_context:
         for back in range(1, GROUP):
@@ -597,7 +609,9 @@
         args.append(returned)
         in_specs.append(vmem)
         ctx_shape = returned.shape[1:]
-        out_shape.append(jax.ShapeDtypeStruct((2, *ctx_shape), returned.dtype))
+        out_shape += [
+            jax.ShapeDtypeStruct((2, *ctx_shape), returned.dtype), jax.ShapeDtypeStruct((8, LANES), jnp.float32)
+        ]
         scratch += [
             pltpu.VMEM(returned.shape, returned.dtype),
             pltpu.VMEM(ctx_shape, returned.dtype),
@@ -877,6 +891,101 @@
     )(*args)
 
 
+def adamw_kernel(rate, factor_ref, *refs):
+    ins, outs = refs[:12], refs[12:]
+    first_grads, up_grad, down_grad = ins[:3]
+    factor = factor_ref[0]
+
+    def update(state, results, at, gradient):
+        weight, one, two = (ref[at] for ref in state)
+        for result, value in zip(results, adamw_update(weight, one, two, gradient * factor, rate, DECAY)):
+            result[at] = value
+
+    proj, out, mlp = ins[3:6], ins[6:9], ins[9:12]
+    new_proj, new_out, new_mlp = outs[:3], outs[3:6], outs[6:9]
+    for at in range(proj[0].shape[0]):
+        update(proj, new_proj, at, first_grads[at])
+    for at in range(out[0].shape[0]):
+        update(out, new_out, at, first_grads[proj[0].shape[0] + at])
+    update(mlp, new_mlp, 0, up_grad[...])
+    update(mlp, new_mlp, 1, down_grad[...])
+
+
+def adamw_all(factor, summed, down_sum, proj, out, mlp, rate):
+    rows, width = summed.shape[1:]
+    steps = mlp[0].shape[2] // width
+    cut = width // steps
+    narrow = lambda count: pl.BlockSpec((count, rows, cut), lambda step: (0, 0, step))
+    first = proj[0].shape[0] + out[0].shape[0]
+    proj_spec, out_spec = narrow(proj[0].shape[0]), narrow(out[0].shape[0])
+    mlp_spec = pl.BlockSpec((2, rows, width), lambda step: (0, 0, step))
+    state_specs = [proj_spec] * 3 + [out_spec] * 3 + [mlp_spec] * 3
+    state = [*proj, *out, *mlp]
+    results = pl.pallas_call(
+        partial(adamw_kernel, rate),
+        grid=(steps,),
+        in_specs=[
+            pl.BlockSpec(memory_space=pltpu.SMEM),
+            narrow(first),
+            pl.BlockSpec((None, rows, width), lambda step: (first + step, 0, 0)),
+            pl.BlockSpec((rows, width), lambda step: (0, step)),
+            *state_specs,
+        ],
+        out_specs=state_specs,
+        out_shape=[jax.ShapeDtypeStruct(part.shape, part.dtype) for part in state],
+        name="adamw_all",
+    )(factor.reshape(1), summed, summed, down_sum, *state)
+    return results[:3], results[3:6], results[6:]
+
+
+def finish_kernel(tokens_ref, gain_ref, own_ref, there_ref, came_ref, grad_ref, tokens_out, text_out, gain_grad_ref):
+    band_rows, text_rows = tokens_ref.shape[0], text_out.shape[0]
+    tile = 64
+
+    @pl.when(pl.program_id(0) == 0)
+    def _():
+        gain_grad_ref[...] = jnp.zeros_like(gain_grad_ref)
+
+    def total_of(part):
+        own = own_ref[part, :].astype(jnp.float32) + there_ref[part, :].astype(jnp.float32)
+        return own + came_ref[part, :].astype(jnp.float32)
+
+    def one(at, carry):
+        part = pl.ds(pl.multiple_of(at * tile, tile), tile)
+        pulled, gain_part = norm_pull(tokens_ref[part, :].astype(jnp.float32), gain_ref[...], total_of(part))
+        tokens_out[part, :] = grad_ref[part, :] + pulled
+        gain_grad_ref[...] += gain_part
+        return carry
+
+    def text(at, carry):
+        start = pl.multiple_of(at * tile, tile)
+        text_out[pl.ds(start, tile), :] = total_of(pl.ds(pl.multiple_of(start + band_rows, tile), tile))
+        return carry
+
+    lax.fori_loop(0, band_rows // tile, one, 0)
+    lax.fori_loop(0, text_rows // tile, text, 0)
+
+
+def finish_rows(tokens, gain_row, own, there, came, grad_one):
+    streams, band_rows, width = tokens.shape
+    text_rows = own.shape[1] - band_rows
+    block = lambda rows: pl.BlockSpec((None, rows, width), lambda stream: (stream, 0, 0))
+    line = pl.BlockSpec((1, width), lambda stream: (0, 0))
+    both = band_rows + text_rows
+    return pl.pallas_call(
+        finish_kernel,
+        grid=(streams,),
+        in_specs=[block(band_rows), line, block(both), block(both), block(both), block(band_rows)],
+        out_specs=[block(band_rows), block(text_rows), line],
+        out_shape=[
+            jax.ShapeDtypeStruct((streams, band_rows, width), jnp.float32),
+            jax.ShapeDtypeStruct((streams, text_rows, width), jnp.float32),
+            jax.ShapeDtypeStruct((1, width), jnp.float32),
+        ],
+        name="finish_rows",
+    )(tokens, gain_row, own, there, came, grad_one)
+
+
 def heads_of(block):
     lane = lax.broadcasted_iota(jnp.int32, block.shape, 1) // HEAD_DIM
     return [
@@ -1155,7 +1264,6 @@
     offsets = earlier[:, 0]
     reach_ids = jnp.arange(SEQ_BANDS)
     within = reach_ids[None, :] <= offsets[:, None]
-    inputs = tokens.astype(jnp.float32).reshape(row_count, model_width)
     reached = jnp.concatenate([tokens[:, None], passed[:, :, :band_rows]], axis=1)
     normed_all = jnp.where(
         within[:, :, None, None], norm_rows(reached.astype(jnp.float32), gains[0]), 0.0
@@ -1223,7 +1331,6 @@
     mine = lax.dynamic_index_in_dim(sent_back, head, 0, keepdims=False)
     other = lax.dynamic_index_in_dim(sent_back, 1 - head, 0, keepdims=False)
     own_there, mine_there = swapped(8, own_back, other)
-    own_back = own_back.astype(jnp.float32) + own_there.astype(jnp.float32)
     returned = (mine.astype(jnp.float32) + mine_there.astype(jnp.float32)).astype(jnp.bfloat16)
 
     flat = lambda part: part.reshape(-1, width)
@@ -1242,31 +1349,28 @@
     ]
     grads.append(grad_up)
     returned, down_sum = lax.optimization_barrier((returned, down_sum))
-    summed, came_back = reduce_grads(bands, grads, returned, 2)
-    back_all = own_back + came_back.astype(jnp.float32)
-    grad_normed_one = back_all[:, :band_rows].reshape(row_count, model_width)
-    grad_text = back_all[:, band_rows:]
-    _, pull_one = jax.vjp(norm_rows, inputs, gains[0])
-    back_zero, gain_grad_one = pull_one(grad_normed_one)
-    grad_tokens = (grad_one + back_zero).reshape(tokens.shape)
-
-    squares = jnp.sum(summed * summed) + jnp.sum(down_sum * down_sum)
+    summed, came_back, squares = reduce_grads(bands, grads, returned, 2)
+    grad_tokens, grad_text, gain_grad_one = finish_rows(
+        tokens, gains[0:1], own_back, own_there, came_back, grad_one.reshape(tokens.shape)
+    )
+    gain_grad_one = gain_grad_one[0]
     gain_rows = jnp.stack([gain_grad_one, gain_grad_two, gain_grad_three]).reshape(-1, LANES)
-    tile = jnp.concatenate([gain_rows, jnp.full((8, LANES), squares)])
+    down_square = jnp.sum(down_sum * down_sum) / (8 * LANES)
+    tile = jnp.concatenate([gain_rows, squares + down_square])
     tile = mesh_total(bands, tile, 10)
     gain_total = 0.5 * tile[:-8].reshape(3, model_width)
-    grad_norm = jnp.sqrt(tile[-1, 0] + jnp.sum(gain_total * gain_total))
+    grad_norm = jnp.sqrt(jnp.sum(tile[-8:]) + jnp.sum(gain_total * gain_total))
     gain_grad = lax.dynamic_slice_in_dim(gain_total, lax.axis_index("band") * shard_rows, shard_rows, 1)
-    proj_grad, out_grad = summed[:6], summed[6:8]
-    up_sum = summed[8:].transpose(1, 0, 2).reshape(down_sum.shape)
-    mlp_grad = jnp.stack([up_sum, down_sum])
     factor = jnp.minimum(1.0, CLIP / grad_norm)
-    matrix_rate = 2.0 * D ** (-0.5)
-    new_proj = adamw_update(
-        proj_master, proj_first, proj_second, proj_grad * factor, matrix_rate, DECAY
-    )
-    new_out = adamw_update(out_master, out_first, out_second, out_grad * factor, matrix_rate, DECAY)
-    new_mlp = adamw_update(mlp_master, mlp_first, mlp_second, mlp_grad * factor, matrix_rate, DECAY)
+    new_proj, new_out, new_mlp = adamw_all(
+        factor,
+        summed,
+        down_sum,
+        (proj_master, proj_first, proj_second),
+        (out_master, out_first, out_second),
+        (mlp_master, mlp_first, mlp_second),
+        2.0 * D ** (-0.5),
+    )
     new_gain = adamw_update(
         gain_master, gain_first, gain_second, gain_grad * factor, GAIN_RATE, 0.0
     )

time: 585 us -> 575 us (0.983)
  other arithmetic: 41.6 us -> 25.1 us
  local copies, waits for them, and re-layouts: 32.4 us -> 16.2 us
  Pallas kernels: 421 us -> 435 us
  waiting for transfers between devices: 25 us -> 33.4 us
    pallas_call x0 -> x2, Pallas kernels: none -> 13.4 us  [the longest x1 7.02 us: adamw_all(): pl.pallas_call(partial(adamw_kernel, rate), grid=(steps,), in_specs=[pl.B...]
    sub x4 -> x1, other arithmetic: 8.71 us -> 0.68 us  [adamw_update(): weight - step_rate * (unbiased_one / (jnp.sqrt(unbiased_two) + ADAM_EPS)...]
    all_gather x1, waiting for transfers between devices: 13.5 us -> 19.4 us  [local(): w_down = lax.all_gather(down_low, 'band', axis=0, tiled=True)]
  transfers between devices with their start and end apart: 2 -> 2, of which waited for: 2 -> 2; matrix products, arithmetic and copies ran while one was open for 12% -> 11% of each run, Pallas kernels for 12% -> 13%
where the time goes in v6:
time: 575 us; the launch traced here: 569 us
  Pallas kernels  435 us (76%)
  matrix products  41.8 us (7%)
  waiting for transfers between devices  33.4 us (6%)
  other arithmetic  25.1 us (4%)
  between operations  18.1 us (3%)
  local copies, waits for them, and re-layouts  16.2 us (3%)
    pallas_call x1, Pallas kernels, reduce_grads(): pl.pallas_call(partial(reduce_kernel, dims, len(grads), has_context), out...  162 us
    pallas_call x1, Pallas kernels, gather_weights(): pl.pallas_call(partial(gather_kernel, dims, has_context), out_shape=out_s...  148 us
    pallas_call x1, Pallas kernels, mlp_both_ways(): pl.pallas_call(mlp_kernel, grid=(units // cut,), in_specs=[whole, whole,...  27.2 us
    pallas_call x3, Pallas kernels, row_step(): pl.pallas_call(partial(row_kernel, backward, follows), grid=(1,), in_spec...  23.7 us
    all_gather x1, waiting for transfers between devices, local(): w_down = lax.all_gather(down_low, 'band', axis=0, tiled=True)  19.4 us
    dot_general x8, matrix products, inner_t(): lax.dot_general(former, latter, (((0,), (0,)), ((), ())), preferred_eleme...  19.1 us
    pallas_call x2, Pallas kernels, attention_back(): pl.pallas_call(partial(by_offset, attend_back_body, causal), grid=(stream...  19 us
    pallas_call x2, Pallas kernels, attention(): pl.pallas_call(partial(by_offset, attend_body, causal), grid=(streams, wi...  17.8 us
  transfers between devices with their start and end apart: 2, of which 2 were waited for; matrix products, arithmetic and copies ran while one was open for 11% of the time, Pallas kernels for 13%

profile of v6, /device:TPU:0, one launch (start us, length us, event | category | flops | bytes accessed | tf_op | source)
XLA Modules:
  0.0 569.4 jit_solution(13542774846476470449)
XLA Ops:
  7.2 0.7 convert_element_type.114
  8.5 1.0 convert.20
  9.5 1.3 convert.19
  10.8 1.3 convert.21
  12.1 0.7 fusion.23
  13.1 1.0 pad_maximum_fusion.2.refs_0_
  14.1 0.9 fusion.15.refs_2_
  15.0 147.8 %gather_weights.1 = (bf16[12,4,2,2,64,512]{5,4,3,2,1,0:T(8,128)(2,1)}, f32[4,2,2,8,128]{4,3,2,1,0:T(8,128)}, bf16[2,3,384,1024]{3,2,1,0:T(8,128)(2,1)}) custom-call(bf16[12,64,512]{2,1,0:T(8,128)(2,1)} %pad_maximum_fusion.2.refs_0_, f32[8,128]{1,0:T(8,128)} %pad_convert_fusion.refs_1_, bf16[384,1024]{1,0:T(8,128)(2,1)} %fusion.15.refs_2_), custom_call_target="tpu_custom_call" | custom-call | flops 199999995904 | tf_op jit(solution)/shard_map/gather_weights/pallas_call | solution.py:325
  162.9 0.8 slice.114
  163.7 0.7 slice.104.refs_3_.gain_ref
  164.4 0.7 slice.97.refs_3_
  165.1 2.4 slice.88
  168.4 1.6 fusion.2
  170.0 1.7 fusion.5
  172.2 2.4 fusion.22
  174.6 1.8 convolution_convert_fusion.9
  176.5 3.7 convolution_convert_fusion
  180.2 3.7 convolution_convert_fusion.1
  183.9 9.7 %attend.2 = (bf16[2,256,512]{2,1,0:T(8,128)(2,1)}, f32[2,4,8,256]{3,2,1,0:T(8,128)}) custom-call(s32[2]{0:T(128)} %bitcast.208, bf16[2,256,512]{2,1,0:T(8,128)(2,1)} %bitcast.177, bf16[2,4,256,512]{3,2,1,0:T(8,128)(2,1)} %bitcast.158, bf16[2,4,256,512]{3,2,1,0:T(8,128)(2,1)} %bitcast.156), custom_call_target="tpu_custom_call" | custom-call | flops 1000000000 | tf_op jit(solution)/shard_map/attend/pallas_call | solution.py:1086
  193.6 7.7 %row_step.3 = (f32[512,1024]{1,0:T(8,128)}, bf16[512,1024]{1,0:T(8,128)(2,1)}, bf16[512,512]{1,0:T(8,128)(2,1)}) custom-call(bf16[512,512]{1,0:T(8,128)(2,1)} %bitcast.197, bf16[12,1024,512]{2,1,0:T(8,128)(2,1)} %bitcast.134, bf16[512,1024]{1,0:T(8,128)(2,1)} %bitcast.144, f32[1,1024]{1,0:T(1,128)} %slice.97.refs_3_, bf16[12,1024,512]{2,1,0:T(8,128)(2,1)} %bitcast.135), custom_call_target="tpu_custom_call" | custom-call | flops 1000000000 | tf_op jit(solution)/shard_map/row_step/pallas_call | solution.py:874
  201.4 2.0 fusion.17
  203.4 2.6 convolution_convert_fusion.10
  206.0 1.1 convolution_convert_fusion.11
  207.1 8.1 %attend.3 = (bf16[2,256,512]{2,1,0:T(8,128)(2,1)}, f32[2,4,8,256]{3,2,1,0:T(8,128)}) custom-call(s32[2]{0:T(128)} %bitcast.209, bf16[2,256,512]{2,1,0:T(8,128)(2,1)} %bitcast.215, bf16[2,1,128,512]{3,2,1,0:T(8,128)(2,1)} %bitcast.204, bf16[2,1,128,512]{3,2,1,0:T(8,128)(2,1)} %bitcast.202), custom_call_target="tpu_custom_call" | custom-call | flops 1000000000 | tf_op jit(solution)/shard_map/attend/pallas_call | solution.py:1086
  215.2 6.6 %row_step.4.hidden_ref = f32[512,1024]{1,0:T(8,128)} custom-call(bf16[512,512]{1,0:T(8,128)(2,1)} %bitcast.175, bf16[12,1024,512]{2,1,0:T(8,128)(2,1)} %bitcast.136, f32[512,1024]{1,0:T(8,128)} %get-tuple-element.69.refs_2_.refs_4_, f32[1,1024]{1,0:T(1,128)} %slice.104.refs_3_.gain_ref), custom_call_target="tpu_custom_call" | custom-call | flops 1000000000 | tf_op jit(solution)/shard_map/row_step/pallas_call | solution.py:874
  221.8 19.4 %all-gather.2.cloned.1.call-done.down_ref = bf16[1024,2048]{1,0:T(8,128)(2,1)} async-done(((bf16[64,2048]{1,0:T(8,128)(2,1)}), bf16[1024,2048]{1,0:T(8,128)(2,1)}) %all-gather.2.cloned.1.call-update) | async-done | bytes 4194320 | tf_op jit(solution)/shard_map/all_gather | solution.py:1259
  241.2 27.2 %mlp_both_ways.1 = (bf16[512,1024]{1,0:T(8,128)(2,1)}, f32[512,1024]{1,0:T(8,128)}, f32[1,1024]{1,0:T(1,128)}, bf16[4,1024,512]{2,1,0:T(8,128)(2,1)}, bf16[1024,2048]{1,0:T(8,128)(2,1)}) custom-call(f32[512,1024]{1,0:T(8,128)} %row_step.4.hidden_ref, bf16[512,1024]{1,0:T(8,128)(2,1)} %bitcast.194, f32[1,1024]{1,0:T(1,128)} %slice.104.refs_3_.gain_ref, ...), custom_call_target="tpu_custom_call" | custom-call | flops 1000000000 | tf_op jit(solution)/shard_map/mlp_both_ways/pallas_call | solution.py:768
  268.5 0.7 slice.105.gain_ref
  269.4 0.7 copy-done.2
  270.3 1.5 convolution_convert_fusion.8
  271.8 8.1 %attend_back.2 = (bf16[2,256,512]{2,1,0:T(8,128)(2,1)}, bf16[2,1,128,512]{3,2,1,0:T(8,128)(2,1)}, bf16[2,1,128,512]{3,2,1,0:T(8,128)(2,1)}) custom-call(s32[2]{0:T(128)} %bitcast.210, bf16[2,256,512]{2,1,0:T(8,128)(2,1)} %bitcast.216, bf16[2,1,128,512]{3,2,1,0:T(8,128)(2,1)} %bitcast.205, bf16[2,1,128,512]{3,2,1,0:T(8,128)(2,1)} %bitcast.203, ...), custom_call_target="tpu_custom_call" | custom-call | flops 1000000000 | tf_op jit(solution)/shard_map/attend_back/pallas_call | solution.py:1103
  279.9 9.5 %row_step.5 = (f32[512,1024]{1,0:T(8,128)}, bf16[512,1024]{1,0:T(8,128)(2,1)}, bf16[512,512]{1,0:T(8,128)(2,1)}, f32[1,1024]{1,0:T(1,128)}) custom-call(bf16[512,512]{1,0:T(8,128)(2,1)} %bitcast.195, bf16[12,1024,512]{2,1,0:T(8,128)(2,1)} %bitcast.138, f32[512,1024]{1,0:T(8,128)} %get-tuple-element.74.refs_2_, f32[1,1024]{1,0:T(1,128)} %slice.97.refs_3_, ...), custom_call_target="tpu_custom_call" | custom-call | flops 1000000000 | tf_op jit(solution)/shard_map/row_step/pallas_call | solution.py:874
  289.4 11.0 %attend_back.3 = (bf16[2,256,512]{2,1,0:T(8,128)(2,1)}, bf16[2,4,256,512]{3,2,1,0:T(8,128)(2,1)}, bf16[2,4,256,512]{3,2,1,0:T(8,128)(2,1)}) custom-call(s32[2]{0:T(128)} %bitcast.211, bf16[2,256,512]{2,1,0:T(8,128)(2,1)} %bitcast.178, bf16[2,4,256,512]{3,2,1,0:T(8,128)(2,1)} %bitcast.159, bf16[2,4,256,512]{3,2,1,0:T(8,128)(2,1)} %bitcast.157, ...), custom_call_target="tpu_custom_call" | custom-call | flops 1000000000 | tf_op jit(solution)/shard_map/attend_back/pallas_call | solution.py:1103
  300.4 4.1 fusion.25
  304.6 2.4 convolution_add_fusion
  307.5 0.7 copy-done.9
  309.7 0.8 fusion.12
  310.4 1.3 pad_maximum_fusion.1.refs_0_.own_ref
  312.0 1.1 copy-done.4
  313.1 1.7 fusion.10.refs_1_
  314.8 10.9 %swap_heads.1 = (bf16[2,384,1024]{2,1,0:T(8,128)(2,1)}, bf16[3,384,1024]{2,1,0:T(8,128)(2,1)}) custom-call(bf16[2,384,1024]{2,1,0:T(8,128)(2,1)} %pad_maximum_fusion.1.refs_0_.own_ref, bf16[3,384,1024]{2,1,0:T(8,128)(2,1)} %fusion.10.refs_1_), custom_call_target="tpu_custom_call" | custom-call | flops 1000000000 | tf_op jit(solution)/shard_map/swap_heads/pallas_call | solution.py:1140
  325.7 2.8 convolution_convert_fusion.2
  328.5 2.5 convolution_convert_fusion.3
  331.0 1.7 convolution_convert_fusion.6
  332.7 1.7 convolution_convert_fusion.7
  334.5 1.8 convolution_convert_fusion.5
  336.3 1.7 convolution_convert_fusion.4
  338.0 2.6 fusion.6.refs_9_
  340.6 1.1 copy-done.44
  341.7 3.6 bitcast_convert_fusion.1
  345.3 3.4 bitcast_convert_fusion
  348.7 13.9 %reduce-scatter.2.cloned.1.call-done = bf16[64,2048]{1,0:T(8,128)(2,1)} async-done(((bf16[1024,2048]{1,0:T(8,128)(2,1)}), bf16[64,2048]{1,0:T(8,128)(2,1)}) %reduce-scatter.2.cloned.1.call-update) | async-done | bytes 262160 | tf_op jit(solution)/shard_map/reduce_scatter | solution.py:1300
  362.6 1.0 convert_element_type.140.refs_2_
  363.6 0.8 copy-done.14
  364.4 0.7 multiply_reduce_fusion
  365.1 162.0 %reduce_grads.1 = (f32[12,64,512]{2,1,0:T(8,128)}, bf16[2,384,1024]{2,1,0:T(8,128)(2,1)}, f32[8,128]{1,0:T(8,128)}) custom-call(bf16[1,4,2,2,64,512]{5,4,3,2,1,0:T(8,128)(2,1)} %bitcast.180, bf16[1,4,2,2,64,512]{5,4,3,2,1,0:T(8,128)(2,1)} %bitcast.182, bf16[1,4,2,2,64,512]{5,4,3,2,1,0:T(8,128)(2,1)} %bitcast.183, bf16[1,4,2,2,64,512]{5,4,3,2,1,0:T(8,128)(2,1)} %bitcast.179, ...), custom_call_target="tpu_custom_call" | custom-call | flops 1000000000 | tf_op jit(solution)/shard_map/reduce_grads/pallas_call | solution.py:624
  527.2 6.4 %finish_rows.1 = (f32[2,256,1024]{2,1,0:T(8,128)}, f32[2,128,1024]{2,1,0:T(8,128)}, f32[1,1024]{1,0:T(1,128)}) custom-call(bf16[2,256,1024]{2,1,0:T(8,128)(2,1)} %tokens_ref.1, f32[1,1024]{1,0:T(1,128)} %slice.105.gain_ref, bf16[2,384,1024]{2,1,0:T(8,128)(2,1)} %pad_maximum_fusion.1.refs_0_.own_ref, bf16[2,384,1024]{2,1,0:T(8,128)(2,1)} %get-tuple-element.82.there_ref, ...), custom_call_target="tpu_custom_call" | custom-call | tf_op jit(solution)/shard_map/finish_rows/pallas_call | solution.py:975
  533.6 0.7 pad_maximum_fusion.3
  535.6 12.8 %mesh_total.1 = f32[32,128]{1,0:T(8,128)} custom-call(f32[32,128]{1,0:T(8,128)} %pad_maximum_fusion.4.in_ref), custom_call_target="tpu_custom_call" | custom-call | flops 1000000000 | tf_op jit(solution)/shard_map/mesh_total/pallas_call | solution.py:1199
  548.4 1.3 slice_reduce_fusion
  549.7 1.3 slice_multiply_fusion
  552.5 0.7 multiply_subtract_fusion
  553.1 7.0 %adamw_all.1 = (f32[6,64,512]{2,1,0:T(8,128)}, f32[6,64,512]{2,1,0:T(8,128)}, f32[6,64,512]{2,1,0:T(8,128)}, f32[2,64,512]{2,1,0:T(8,128)}, f32[2,64,512]{2,1,0:...) custom-call(f32[1]{0:T(128)} %bitcast.59.factor_ref, ...), custom_call_target="tpu_custom_call" | custom-call | tf_op jit(solution)/shard_map/adamw_all/pallas_call | solution.py:924
  560.2 1.0 copy.58
  (124 shorter events, 5.7 us)
Async XLA Ops:
  7.2 234.0 %all-gather.2.cloned.1.call-start = ((), (), s32[]{:S(2)}) async-start(), calls=%async_computation.1 | async-start | bytes 4456448 | tf_op jit(solution)/shard_map/all_gather | solution.py:1259
  9.5 4.6 copy-start
  9.5 4.6 copy-start.22
  162.8 199.8 %reduce-scatter.2.cloned.1.call-start = ((), (), s32[]{:S(2)}) async-start(), calls=%async_computation.2 | async-start | bytes 4456448 | tf_op jit(solution)/shard_map/reduce_scatter | solution.py:1300
  165.1 2.4 copy-start.1
  165.1 6.6 %slice-start = ((s8[12582912]{0:T(1024)(128)(4,1)}), s8[4194304]{0:T(1024)(128)(4,1)S(1)}, s32[]{:S(2)}) async-start(s8[12582912]{0:T(1024)(128)(4,1)} %bitcast.140), calls=%async_computation.3 | async-start | bytes 8388608
  167.6 0.7 copy-start.36
  167.6 4.2 slice-start.1
  170.0 2.2 slice-start.2
  171.7 8.5 %copy-start.10 = (bf16[2,4,256,1024]{3,2,1,0:T(8,128)(2,1)}, bf16[2,4,256,1024]{3,2,1,0:T(8,128)(2,1)S(1)}, u32[]{:S(2)}) copy-start(bf16[2,4,256,1024]{3,2,1,0:T(8,128)(2,1)S(1)} %fusion.5) | copy-start | bytes 12582916
  171.8 2.9 copy-start.28
  174.6 5.5 copy-start.15
  174.6 5.5 copy-start.18
  174.6 5.5 copy-start.24
  193.6 7.7 %copy-start.37 = (s32[2,1]{0,1:T(1,128)S(1)}, s32[2,1]{0,1:T(1,128)}, u32[]{:S(2)}) copy-start(s32[2,1]{0,1:T(1,128)} %param.19) | copy-start | bytes 28
  193.6 7.7 %copy-start.23 = (bf16[2,128,1024]{2,1,0:T(8,128)(2,1)S(1)}, bf16[2,128,1024]{2,1,0:T(8,128)(2,1)}, u32[]{:S(2)}) copy-start(bf16[2,128,1024]{2,1,0:T(8,128)(2,1)} %param.17) | copy-start | bytes 1572868
  201.3 4.7 copy-start.8
  203.4 2.6 copy-start.6
  268.5 0.8 copy-start.38
  268.5 1.6 copy-start.2
  268.5 1.9 copy-start.17
  289.4 11.0 %copy-start.25 = (bf16[1,4,2,2,64,512]{5,4,3,2,1,0:T(8,128)(2,1)S(1)}, bf16[1,4,2,2,64,512]{5,4,3,2,1,0:T(8,128)(2,1)}, u32[]{:S(2)}) copy-start(bf16[1,4,2,2,64,512]{5,4,3,2,1,0:T(8,128)(2,1)} %copy-done.24) | copy-start | bytes 3145732
  300.4 4.2 copy-start.12
  300.4 4.2 copy-start.16
  306.9 1.2 copy-start.9
  307.0 1.3 copy-start.26
  307.0 1.7 copy-start.7
  307.0 1.7 copy-start.30
  308.2 1.3 copy-start.19
  308.2 1.5 copy-start.33
  312.0 1.1 copy-start.4
  325.7 5.3 copy-start.31
  325.7 5.3 copy-start.45
  325.7 7.0 %copy-start.29 = (bf16[2,1,256,1024]{3,2,1,0:T(8,128)(2,1)S(1)}, bf16[2,1,256,1024]{3,2,1,0:T(8,128)(2,1)}, u32[]{:S(2)}) copy-start(bf16[2,1,256,1024]{3,2,1,0:T(8,128)(2,1)} %copy-done.28) | copy-start | bytes 3145732
  325.7 7.0 %copy-start.34 = (bf16[2,256,512]{2,1,0:T(8,128)(2,1)S(1)}, bf16[2,256,512]{2,1,0:T(8,128)(2,1)}, u32[]{:S(2)}) copy-start(bf16[2,256,512]{2,1,0:T(8,128)(2,1)} %get-tuple-element.77) | copy-start | bytes 1572868
  331.0 3.5 copy-start.32
  331.0 3.5 copy-start.46
  332.7 3.5 copy-start.3
  332.7 3.5 copy-start.21
  334.5 3.5 copy-start.5
  334.5 3.5 copy-start.20
  338.0 2.6 copy-start.11
  338.0 3.8 copy-start.44
  341.7 3.6 copy-start.13
  363.6 0.8 copy-start.14
  527.2 6.4 %copy-start.39 = (f32[1,1024]{1,0:T(1,128)S(1)}, f32[1,1024]{1,0:T(1,128)}, u32[]{:S(2)}) copy-start(f32[1,1024]{1,0:T(1,128)} %get-tuple-element.95) | copy-start | bytes 12292
  527.2 6.4 %copy-start.40 = (f32[1,1024]{1,0:T(1,128)S(1)}, f32[1,1024]{1,0:T(1,128)}, u32[]{:S(2)}) copy-start(f32[1,1024]{1,0:T(1,128)} %get-tuple-element.94) | copy-start | bytes 12292
  527.2 7.8 %copy-start.41 = (f32[8,128]{1,0:T(8,128)S(1)}, f32[8,128]{1,0:T(8,128)}, u32[]{:S(2)}) copy-start(f32[8,128]{1,0:T(8,128)} %get-tuple-element.96) | copy-start | bytes 12292
  533.6 18.9 %copy-start.35 = (f32[3,64]{1,0:T(4,128)S(1)}, f32[3,64]{1,0:T(4,128)}, u32[]{:S(2)}) copy-start(f32[3,64]{1,0:T(4,128)} %param.23) | copy-start | bytes 2308
  533.6 18.9 %copy-start.42 = (f32[3,64]{1,0:T(4,128)S(1)}, f32[3,64]{1,0:T(4,128)}, u32[]{:S(2)}) copy-start(f32[3,64]{1,0:T(4,128)} %param.30) | copy-start | bytes 2308
  533.6 18.9 %copy-start.43 = (f32[3,64]{1,0:T(4,128)S(1)}, f32[3,64]{1,0:T(4,128)}, u32[]{:S(2)}) copy-start(f32[3,64]{1,0:T(4,128)} %param.31) | copy-start | bytes 2308
  553.1 7.0 %copy-start.27 = (bf16[512,1024]{1,0:T(8,128)(2,1)S(1)}, bf16[512,1024]{1,0:T(8,128)(2,1)}, u32[]{:S(2)}) copy-start(bf16[512,1024]{1,0:T(8,128)(2,1)} %get-tuple-element.71) | copy-start | bytes 3145732
Sparse Core Ops, SparseCore 0:
  162.9 78.2 all-gather.1
  268.6 93.9 reduce-scatter.1

commit v7 on v6

--- a/solution.py
+++ b/solution.py
@@ -1063,7 +1063,10 @@
 def by_offset(body, causal, offset_ref, *refs):
     reaches = refs[1].shape[0]
     if reaches == 1:
-        body(1, causal, *refs)
+        for pair in range(refs[0].shape[1] // LANES):
+            lanes = pl.ds(pair * LANES, LANES)
+            views = [ref.at[pair] if ref.dtype == jnp.float32 else ref.at[..., lanes] for ref in refs]
+            body(1, causal, *views)
         return
     offset = offset_ref[pl.program_id(0)]
     for earlier_bands in range(reaches):
@@ -1074,18 +1077,26 @@
 
 def attention_specs(queries, keys):
     rows, reaches, key_rows = queries.shape[1], keys.shape[1], keys.shape[2]
+    width = queries.shape[2]
+    if reaches == 1:
+        return (
+            1,
+            pl.BlockSpec((None, rows, width), lambda stream, pair: (stream, 0, 0)),
+            pl.BlockSpec((None, reaches, key_rows, width), lambda stream, pair: (stream, 0, 0, 0)),
+            pl.BlockSpec((None, width // LANES, 8, rows), lambda stream, pair: (stream, 0, 0, 0)),
+        )
     row_spec = pl.BlockSpec((None, rows, LANES), lambda stream, pair: (stream, 0, pair))
     key_spec = pl.BlockSpec((None, reaches, key_rows, LANES), lambda stream, pair: (stream, 0, 0, pair))
     total_spec = pl.BlockSpec((None, None, 8, rows), lambda stream, pair: (stream, pair, 0, 0))
-    return row_spec, key_spec, total_spec
+    return width // LANES, row_spec, key_spec, total_spec
 
 
 def attention(queries, keys, values, offsets, causal):
     streams, rows, width = queries.shape
-    row_spec, key_spec, total_spec = attention_specs(queries, keys)
+    steps, row_spec, key_spec, total_spec = attention_specs(queries, keys)
     return pl.pallas_call(
         partial(by_offset, attend_body, causal),
-        grid=(streams, width // LANES),
+        grid=(streams, steps),
         in_specs=[pl.BlockSpec(memory_space=pltpu.SMEM), row_spec, key_spec, key_spec],
         out_specs=[row_spec, total_spec],
         out_shape=[
@@ -1099,10 +1110,10 @@
 
 def attention_back(queries, keys, values, offsets, totals, grad_out, causal):
     streams, rows, width = queries.shape
-    row_spec, key_spec, total_spec = attention_specs(queries, keys)
+    steps, row_spec, key_spec, total_spec = attention_specs(queries, keys)
     return pl.pallas_call(
         partial(by_offset, attend_back_body, causal),
-        grid=(streams, width // LANES),
+        grid=(streams, steps),
         in_specs=[pl.BlockSpec(memory_space=pltpu.SMEM), row_spec, key_spec, key_spec, total_spec, row_spec],
         out_specs=[row_spec, key_spec, key_spec],
         out_shape=[
@@ -1348,7 +1359,6 @@
         )
     ]
     grads.append(grad_up)
-    returned, down_sum = lax.optimization_barrier((returned, down_sum))
     summed, came_back, squares = reduce_grads(bands, grads, returned, 2)
     grad_tokens, grad_text, gain_grad_one = finish_rows(
         tokens, gains[0:1], own_back, own_there, came_back, grad_one.reshape(tokens.shape)

time: 575 us -> 568 us (0.988)
  waiting for transfers between devices: 33.4 us -> 23.4 us
    reduce_scatter x1, waiting for transfers between devices: 13.9 us -> 0.02 us  [local(): lax.psum_scatter(grad_down, 'band', scatter_dimension=0, tiled=True)]
    pallas_call x1, Pallas kernels: 162 us -> 171 us  [reduce_grads(): pl.pallas_call(partial(reduce_kernel, dims, len(grads), has_context), out...]
  transfers between devices with their start and end apart: 2 -> 2, of which waited for: 2 -> 1; matrix products, arithmetic and copies ran while one was open for 11% -> 11% of each run, Pallas kernels for 13% -> 43%
where the time goes in v7:
time: 568 us; the launch traced here: 563 us
  Pallas kernels  439 us (77%)
  matrix products  41.8 us (7%)
  other arithmetic  25.9 us (5%)
  waiting for transfers between devices  23.4 us (4%)
  between operations  18.1 us (3%)
  local copies, waits for them, and re-layouts  15.4 us (3%)
    pallas_call x1, Pallas kernels, reduce_grads(): pl.pallas_call(partial(reduce_kernel, dims, len(grads), has_context), out...  171 us
    pallas_call x1, Pallas kernels, gather_weights(): pl.pallas_call(partial(gather_kernel, dims, has_context), out_shape=out_s...  148 us
    pallas_call x1, Pallas kernels, mlp_both_ways(): pl.pallas_call(mlp_kernel, grid=(units // cut,), in_specs=[whole, whole,...  27.2 us
    pallas_call x3, Pallas kernels, row_step(): pl.pallas_call(partial(row_kernel, backward, follows), grid=(1,), in_spec...  23.7 us
    all_gather x1, waiting for transfers between devices, local(): w_down = lax.all_gather(down_low, 'band', axis=0, tiled=True)  23.3 us
    dot_general x8, matrix products, inner_t(): lax.dot_general(former, latter, (((0,), (0,)), ((), ())), preferred_eleme...  19.1 us
    pallas_call x2, Pallas kernels, attention_back(): pl.pallas_call(partial(by_offset, attend_back_body, causal), grid=(stream...  17.4 us
    dot_general x6, matrix products, matmul(): return jnp.dot(former, latter, preferred_element_type=jnp.float32)  14.4 us
  transfers between devices with their start and end apart: 2, of which 1 were waited for; matrix products, arithmetic and copies ran while one was open for 11% of the time, Pallas kernels for 43%

profile of v7, /device:TPU:0, one launch (start us, length us, event | category | flops | bytes accessed | tf_op | source)
XLA Modules:
  0.0 563.4 jit_solution(6173689270501276925)
XLA Ops:
  7.2 0.7 convert_element_type.114
  8.5 1.0 convert.20
  9.5 1.3 convert.19
  10.8 1.3 convert.21
  12.1 0.7 fusion.23
  13.1 1.0 pad_maximum_fusion.2.refs_0_
  14.1 0.9 fusion.15.refs_2_
  15.0 147.8 %gather_weights.1 = (bf16[12,4,2,2,64,512]{5,4,3,2,1,0:T(8,128)(2,1)}, f32[4,2,2,8,128]{4,3,2,1,0:T(8,128)}, bf16[2,3,384,1024]{3,2,1,0:T(8,128)(2,1)}) custom-call(bf16[12,64,512]{2,1,0:T(8,128)(2,1)} %pad_maximum_fusion.2.refs_0_, f32[8,128]{1,0:T(8,128)} %pad_convert_fusion.refs_1_, bf16[384,1024]{1,0:T(8,128)(2,1)} %fusion.15.refs_2_), custom_call_target="tpu_custom_call" | custom-call | flops 199999995904 | tf_op jit(solution)/shard_map/gather_weights/pallas_call | solution.py:325
  162.9 0.8 slice.114
  163.7 0.7 slice.104.refs_3_.gain_ref
  164.4 0.7 slice.97.refs_3_
  165.1 2.4 slice.88
  167.6 0.6 convert_reduce_fusion
  168.4 1.6 fusion.2
  170.0 1.7 fusion.5
  172.2 2.4 fusion.22
  174.6 1.8 convolution_convert_fusion.9
  176.5 3.7 convolution_convert_fusion
  180.2 3.7 convolution_convert_fusion.1
  183.9 9.7 %attend.2 = (bf16[2,256,512]{2,1,0:T(8,128)(2,1)}, f32[2,4,8,256]{3,2,1,0:T(8,128)}) custom-call(s32[2]{0:T(128)} %bitcast.208, bf16[2,256,512]{2,1,0:T(8,128)(2,1)} %bitcast.177, bf16[2,4,256,512]{3,2,1,0:T(8,128)(2,1)} %bitcast.158, bf16[2,4,256,512]{3,2,1,0:T(8,128)(2,1)} %bitcast.156), custom_call_target="tpu_custom_call" | custom-call | flops 1000000000 | tf_op jit(solution)/shard_map/attend/pallas_call | solution.py:1097
  193.6 7.7 %row_step.3 = (f32[512,1024]{1,0:T(8,128)}, bf16[512,1024]{1,0:T(8,128)(2,1)}, bf16[512,512]{1,0:T(8,128)(2,1)}) custom-call(bf16[512,512]{1,0:T(8,128)(2,1)} %bitcast.197, bf16[12,1024,512]{2,1,0:T(8,128)(2,1)} %bitcast.134, bf16[512,1024]{1,0:T(8,128)(2,1)} %bitcast.144, f32[1,1024]{1,0:T(1,128)} %slice.97.refs_3_, bf16[12,1024,512]{2,1,0:T(8,128)(2,1)} %bitcast.135), custom_call_target="tpu_custom_call" | custom-call | flops 1000000000 | tf_op jit(solution)/shard_map/row_step/pallas_call | solution.py:874
  201.4 2.0 fusion.17
  203.4 2.6 convolution_convert_fusion.10
  206.0 1.1 convolution_convert_fusion.11
  207.1 3.8 attend.3
  210.9 6.6 %row_step.4.hidden_ref = f32[512,1024]{1,0:T(8,128)} custom-call(bf16[512,512]{1,0:T(8,128)(2,1)} %bitcast.175, bf16[12,1024,512]{2,1,0:T(8,128)(2,1)} %bitcast.136, f32[512,1024]{1,0:T(8,128)} %get-tuple-element.67.refs_2_.refs_4_, f32[1,1024]{1,0:T(1,128)} %slice.104.refs_3_.gain_ref), custom_call_target="tpu_custom_call" | custom-call | flops 1000000000 | tf_op jit(solution)/shard_map/row_step/pallas_call | solution.py:874
  217.6 23.3 %all-gather.2.cloned.1.call-done.down_ref = bf16[1024,2048]{1,0:T(8,128)(2,1)} async-done(((bf16[64,2048]{1,0:T(8,128)(2,1)}), bf16[1024,2048]{1,0:T(8,128)(2,1)}) %all-gather.2.cloned.1.call-update) | async-done | bytes 4194320 | tf_op jit(solution)/shard_map/all_gather | solution.py:1270
  240.8 27.2 %mlp_both_ways.1 = (bf16[512,1024]{1,0:T(8,128)(2,1)}, f32[512,1024]{1,0:T(8,128)}, f32[1,1024]{1,0:T(1,128)}, bf16[4,1024,512]{2,1,0:T(8,128)(2,1)}, bf16[1024,2048]{1,0:T(8,128)(2,1)}) custom-call(f32[512,1024]{1,0:T(8,128)} %row_step.4.hidden_ref, bf16[512,1024]{1,0:T(8,128)(2,1)} %bitcast.194, f32[1,1024]{1,0:T(1,128)} %slice.104.refs_3_.gain_ref, ...), custom_call_target="tpu_custom_call" | custom-call | flops 1000000000 | tf_op jit(solution)/shard_map/mlp_both_ways/pallas_call | solution.py:768
  268.1 0.7 slice.105.gain_ref
  269.0 0.7 copy-done.2
  270.0 1.5 convolution_convert_fusion.8
  271.5 6.4 %attend_back.2 = (bf16[2,256,512]{2,1,0:T(8,128)(2,1)}, bf16[2,1,128,512]{3,2,1,0:T(8,128)(2,1)}, bf16[2,1,128,512]{3,2,1,0:T(8,128)(2,1)}) custom-call(s32[2]{0:T(128)} %bitcast.210, bf16[2,256,512]{2,1,0:T(8,128)(2,1)} %bitcast.216, bf16[2,1,128,512]{3,2,1,0:T(8,128)(2,1)} %bitcast.205, bf16[2,1,128,512]{3,2,1,0:T(8,128)(2,1)} %bitcast.203, ...), custom_call_target="tpu_custom_call" | custom-call | flops 1000000000 | tf_op jit(solution)/shard_map/attend_back/pallas_call | solution.py:1114
  277.9 9.4 %row_step.5 = (f32[512,1024]{1,0:T(8,128)}, bf16[512,1024]{1,0:T(8,128)(2,1)}, bf16[512,512]{1,0:T(8,128)(2,1)}, f32[1,1024]{1,0:T(1,128)}) custom-call(bf16[512,512]{1,0:T(8,128)(2,1)} %bitcast.195, bf16[12,1024,512]{2,1,0:T(8,128)(2,1)} %bitcast.138, f32[512,1024]{1,0:T(8,128)} %get-tuple-element.72.refs_2_, f32[1,1024]{1,0:T(1,128)} %slice.97.refs_3_, ...), custom_call_target="tpu_custom_call" | custom-call | flops 1000000000 | tf_op jit(solution)/shard_map/row_step/pallas_call | solution.py:874
  287.3 11.0 %attend_back.3 = (bf16[2,256,512]{2,1,0:T(8,128)(2,1)}, bf16[2,4,256,512]{3,2,1,0:T(8,128)(2,1)}, bf16[2,4,256,512]{3,2,1,0:T(8,128)(2,1)}) custom-call(s32[2]{0:T(128)} %bitcast.211, bf16[2,256,512]{2,1,0:T(8,128)(2,1)} %bitcast.178, bf16[2,4,256,512]{3,2,1,0:T(8,128)(2,1)} %bitcast.159, bf16[2,4,256,512]{3,2,1,0:T(8,128)(2,1)} %bitcast.157, ...), custom_call_target="tpu_custom_call" | custom-call | flops 1000000000 | tf_op jit(solution)/shard_map/attend_back/pallas_call | solution.py:1114
  298.3 4.1 fusion.25
  302.5 2.4 convolution_add_fusion
  305.4 0.7 copy-done.9
  307.6 0.8 fusion.12
  308.4 1.3 pad_maximum_fusion.1.refs_0_.own_ref
  309.9 1.1 copy-done.4
  311.0 1.7 fusion.10.refs_1_
  312.7 10.9 %swap_heads.1 = (bf16[2,384,1024]{2,1,0:T(8,128)(2,1)}, bf16[3,384,1024]{2,1,0:T(8,128)(2,1)}) custom-call(bf16[2,384,1024]{2,1,0:T(8,128)(2,1)} %pad_maximum_fusion.1.refs_0_.own_ref, bf16[3,384,1024]{2,1,0:T(8,128)(2,1)} %fusion.10.refs_1_), custom_call_target="tpu_custom_call" | custom-call | flops 1000000000 | tf_op jit(solution)/shard_map/swap_heads/pallas_call | solution.py:1151
  323.6 2.8 convolution_convert_fusion.2
  326.4 2.5 convolution_convert_fusion.3
  328.9 1.7 convolution_convert_fusion.6
  330.6 1.7 convolution_convert_fusion.7
  332.4 1.8 convolution_convert_fusion.5
  334.1 1.7 convolution_convert_fusion.4
  335.9 2.6 fusion.6.refs_9_
  338.5 1.1 copy-done.44
  339.6 3.6 bitcast_convert_fusion.1
  343.2 3.4 bitcast_convert_fusion
  346.6 171.4 %reduce_grads.1 = (f32[12,64,512]{2,1,0:T(8,128)}, bf16[2,384,1024]{2,1,0:T(8,128)(2,1)}, f32[8,128]{1,0:T(8,128)}) custom-call(bf16[1,4,2,2,64,512]{5,4,3,2,1,0:T(8,128)(2,1)} %bitcast.180, bf16[1,4,2,2,64,512]{5,4,3,2,1,0:T(8,128)(2,1)} %bitcast.182, bf16[1,4,2,2,64,512]{5,4,3,2,1,0:T(8,128)(2,1)} %bitcast.183, bf16[1,4,2,2,64,512]{5,4,3,2,1,0:T(8,128)(2,1)} %bitcast.179, ...), custom_call_target="tpu_custom_call" | custom-call | flops 1000000000 | tf_op jit(solution)/shard_map/reduce_grads/pallas_call | solution.py:624
  518.0 6.4 %finish_rows.1 = (f32[2,256,1024]{2,1,0:T(8,128)}, f32[2,128,1024]{2,1,0:T(8,128)}, f32[1,1024]{1,0:T(1,128)}) custom-call(bf16[2,256,1024]{2,1,0:T(8,128)(2,1)} %tokens_ref.1, f32[1,1024]{1,0:T(1,128)} %slice.105.gain_ref, bf16[2,384,1024]{2,1,0:T(8,128)(2,1)} %pad_maximum_fusion.1.refs_0_.own_ref, bf16[2,384,1024]{2,1,0:T(8,128)(2,1)} %get-tuple-element.80.there_ref, ...), custom_call_target="tpu_custom_call" | custom-call | tf_op jit(solution)/shard_map/finish_rows/pallas_call | solution.py:975
  524.4 0.7 pad_maximum_fusion.3
  525.2 1.8 multiply_reduce_fusion
  527.6 0.6 pad_maximum_fusion.4.in_ref
  528.2 13.4 %mesh_total.1 = f32[32,128]{1,0:T(8,128)} custom-call(f32[32,128]{1,0:T(8,128)} %pad_maximum_fusion.4.in_ref), custom_call_target="tpu_custom_call" | custom-call | flops 1000000000 | tf_op jit(solution)/shard_map/mesh_total/pallas_call | solution.py:1210
  541.6 1.3 slice_reduce_fusion
  542.9 1.3 slice_multiply_fusion
  545.7 0.7 multiply_subtract_fusion
  546.3 0.8 convert_element_type.140.refs_2_
  547.2 7.0 %adamw_all.1 = (f32[6,64,512]{2,1,0:T(8,128)}, f32[6,64,512]{2,1,0:T(8,128)}, f32[6,64,512]{2,1,0:T(8,128)}, f32[2,64,512]{2,1,0:T(8,128)}, f32[2,64,512]{2,1,0:...) custom-call(f32[1]{0:T(128)} %bitcast.59.factor_ref, ...), custom_call_target="tpu_custom_call" | custom-call | tf_op jit(solution)/shard_map/adamw_all/pallas_call | solution.py:924
  554.2 1.0 copy.58
  (124 shorter events, 4.5 us)
Async XLA Ops:
  7.2 233.7 %all-gather.2.cloned.1.call-start = ((), (), s32[]{:S(2)}) async-start(), calls=%async_computation.1 | async-start | bytes 4456448 | tf_op jit(solution)/shard_map/all_gather | solution.py:1270
  9.5 4.6 copy-start
  9.5 4.6 copy-start.21
  162.8 362.4 %reduce-scatter.2.cloned.1.call-start = ((), (), s32[]{:S(2)}) async-start(), calls=%async_computation.2 | async-start | bytes 4456448 | tf_op jit(solution)/shard_map/reduce_scatter | solution.py:1311
  165.1 2.4 copy-start.1
  165.1 6.6 %slice-start = ((s8[12582912]{0:T(1024)(128)(4,1)}), s8[4194304]{0:T(1024)(128)(4,1)S(1)}, s32[]{:S(2)}) async-start(s8[12582912]{0:T(1024)(128)(4,1)} %bitcast.140), calls=%async_computation.3 | async-start | bytes 8388608
  167.6 0.7 copy-start.36
  167.6 4.2 slice-start.1
  170.0 2.2 slice-start.2
  171.7 8.5 %copy-start.10 = (bf16[2,4,256,1024]{3,2,1,0:T(8,128)(2,1)}, bf16[2,4,256,1024]{3,2,1,0:T(8,128)(2,1)S(1)}, u32[]{:S(2)}) copy-start(bf16[2,4,256,1024]{3,2,1,0:T(8,128)(2,1)S(1)} %fusion.5) | copy-start | bytes 12582916
  171.8 2.9 copy-start.28
  174.6 5.5 copy-start.14
  174.6 5.5 copy-start.17
  174.6 5.5 copy-start.23
  193.6 7.7 %copy-start.37 = (s32[2,1]{0,1:T(1,128)S(1)}, s32[2,1]{0,1:T(1,128)}, u32[]{:S(2)}) copy-start(s32[2,1]{0,1:T(1,128)} %param.19) | copy-start | bytes 28
  193.6 7.7 %copy-start.22 = (bf16[2,128,1024]{2,1,0:T(8,128)(2,1)S(1)}, bf16[2,128,1024]{2,1,0:T(8,128)(2,1)}, u32[]{:S(2)}) copy-start(bf16[2,128,1024]{2,1,0:T(8,128)(2,1)} %param.17) | copy-start | bytes 1572868
  201.3 4.7 copy-start.8
  203.4 2.6 copy-start.6
  268.1 0.8 copy-start.38
  268.1 1.6 copy-start.2
  268.1 1.9 copy-start.16
  287.3 11.0 %copy-start.24 = (bf16[1,4,2,2,64,512]{5,4,3,2,1,0:T(8,128)(2,1)S(1)}, bf16[1,4,2,2,64,512]{5,4,3,2,1,0:T(8,128)(2,1)}, u32[]{:S(2)}) copy-start(bf16[1,4,2,2,64,512]{5,4,3,2,1,0:T(8,128)(2,1)} %copy-done.23) | copy-start | bytes 3145732
  298.3 4.2 copy-start.12
  298.3 4.2 copy-start.15
  304.8 1.2 copy-start.9
  304.9 1.3 copy-start.25
  304.9 1.7 copy-start.7
  304.9 1.7 copy-start.30
  306.1 1.3 copy-start.18
  306.1 1.5 copy-start.33
  309.9 1.1 copy-start.4
  323.6 5.3 copy-start.31
  323.6 5.3 copy-start.45
  323.6 7.0 %copy-start.29 = (bf16[2,1,256,1024]{3,2,1,0:T(8,128)(2,1)S(1)}, bf16[2,1,256,1024]{3,2,1,0:T(8,128)(2,1)}, u32[]{:S(2)}) copy-start(bf16[2,1,256,1024]{3,2,1,0:T(8,128)(2,1)} %copy-done.28) | copy-start | bytes 3145732
  323.6 7.0 %copy-start.34 = (bf16[2,256,512]{2,1,0:T(8,128)(2,1)S(1)}, bf16[2,256,512]{2,1,0:T(8,128)(2,1)}, u32[]{:S(2)}) copy-start(bf16[2,256,512]{2,1,0:T(8,128)(2,1)} %get-tuple-element.75) | copy-start | bytes 1572868
  328.9 3.5 copy-start.32
  328.9 3.5 copy-start.46
  330.6 3.5 copy-start.3
  330.6 3.5 copy-start.20
  332.4 3.5 copy-start.5
  332.4 3.5 copy-start.19
  335.9 2.6 copy-start.11
  335.9 3.8 copy-start.44
  339.6 3.6 copy-start.13
  518.0 6.4 %copy-start.39 = (f32[1,1024]{1,0:T(1,128)S(1)}, f32[1,1024]{1,0:T(1,128)}, u32[]{:S(2)}) copy-start(f32[1,1024]{1,0:T(1,128)} %get-tuple-element.91) | copy-start | bytes 12292
  518.0 6.4 %copy-start.40 = (f32[1,1024]{1,0:T(1,128)S(1)}, f32[1,1024]{1,0:T(1,128)}, u32[]{:S(2)}) copy-start(f32[1,1024]{1,0:T(1,128)} %get-tuple-element.90) | copy-start | bytes 12292
  518.0 9.6 %copy-start.41 = (f32[8,128]{1,0:T(8,128)S(1)}, f32[8,128]{1,0:T(8,128)}, u32[]{:S(2)}) copy-start(f32[8,128]{1,0:T(8,128)} %get-tuple-element.92) | copy-start | bytes 12292
  524.4 21.3 %copy-start.35 = (f32[3,64]{1,0:T(4,128)S(1)}, f32[3,64]{1,0:T(4,128)}, u32[]{:S(2)}) copy-start(f32[3,64]{1,0:T(4,128)} %param.23) | copy-start | bytes 2308
  524.4 21.3 %copy-start.42 = (f32[3,64]{1,0:T(4,128)S(1)}, f32[3,64]{1,0:T(4,128)}, u32[]{:S(2)}) copy-start(f32[3,64]{1,0:T(4,128)} %param.30) | copy-start | bytes 2308
  524.4 21.3 %copy-start.43 = (f32[3,64]{1,0:T(4,128)S(1)}, f32[3,64]{1,0:T(4,128)}, u32[]{:S(2)}) copy-start(f32[3,64]{1,0:T(4,128)} %param.31) | copy-start | bytes 2308
  525.2 21.2 %copy-start.26 = (bf16[64,2048]{1,0:T(8,128)(2,1)S(1)}, bf16[64,2048]{1,0:T(8,128)(2,1)}, u32[]{:S(2)}) copy-start(bf16[64,2048]{1,0:T(8,128)(2,1)} %reduce-scatter.2.cloned.1.call-done) | copy-start | bytes 786436
  547.2 7.0 %copy-start.27 = (bf16[512,1024]{1,0:T(8,128)(2,1)S(1)}, bf16[512,1024]{1,0:T(8,128)(2,1)}, u32[]{:S(2)}) copy-start(bf16[512,1024]{1,0:T(8,128)(2,1)} %get-tuple-element.69) | copy-start | bytes 3145732
Sparse Core Ops, SparseCore 0:
  162.9 77.8 all-gather.1
  268.3 93.9 reduce-scatter.1
